TPU v7x, 256 devices: a whole 4x4x8 slice. The times are simulated.
256 devices in a mesh: level: 32 (over y_lo, z, core), band: 8 (over x, y_hi).
Axes of the slice: x: 4, y: 4 (y_hi: 2, y_lo: 2; y = y_hi * 2 + y_lo), z: 8, core: 2. Of those that a mesh axis runs over, the one named last changes fastest.
Arguments:
- latents: float32 [32, 4, 40, 64], P('level', None, 'band'), may hold values from -18 to 18
- timesteps: int32 [32], P('level'), may hold values from 16 to 999
- fresh: float32 [1, 4, 40, 64], P(None, None, 'band'), may hold values from -6 to 6
- w_in: float32 [4, 320], replicated, may hold values from -3 to 3
- conv_first: float32 [3, 3, 320, 320], replicated, may hold values from -0.109375 to 0.109375
- conv_second: float32 [3, 3, 320, 320], replicated, may hold values from -0.109375 to 0.109375
- w_time: float32 [320, 320], replicated, may hold values from -0.3125 to 0.3125
- temporal: float32 [3, 320, 320], replicated, may hold values from -0.1875 to 0.1875
- w_out: float32 [320, 4], replicated, may hold values from -0.3125 to 0.3125
Outputs:
- queue: float32 [32, 4, 40, 64], P('level', None, 'band')
All inputs are finite; a program needn't handle non-finite values.
Results may differ from a plain program's by a relative error of at most 0.0001.
Values sent between devices are 32-bit elements; how exact they have to be, the bound alone decides.
No kernel may reach another device: no remote copies, remote signals or barrier semaphores. Data moves between devices by JAX's collectives and lax.ppermute only.
A program may use at most 128 MiB of HBM per device.

v0:
```python
import math

import jax
import jax.numpy as jnp
from jax import lax
from jax.sharding import PartitionSpec as P

GROUPS = 32
ITERS = 2
NSTEPS = 1000
STRIDE = 16


EPSILON = 1e-05
HIGHEST = lax.Precision.HIGHEST


def copy_for_each(shard, axis):
    size = lax.axis_size(axis)
    return lax.all_to_all(
        jnp.broadcast_to(shard[None], (size, *shard.shape)), axis, 0, 0, tiled=True
    )


def of_everyone(shard, axis):
    everything = copy_for_each(shard, axis)
    return jnp.sum(everything, axis=0)


def together(arrays, axis):
    vector, at, outs = (jnp.concatenate([a.reshape(-1) for a in arrays]), 0, [])
    so_far = of_everyone(vector, axis)
    for a in arrays:
        outs.append(so_far[at : at + a.size].reshape(a.shape))
        at += a.size
    return tuple(outs)


def padded_2(shard, sides, width):
    for axis, dim in sides:
        size, length = (lax.axis_size(axis), shard.shape[dim])
        up = [(i, (i + 1) % size) for i in range(size - 1)]
        down = [(j, i) for i, j in up]
        last = lax.slice_in_dim(shard, length - width, length, axis=dim)
        initial = lax.slice_in_dim(shard, 0, width, axis=dim)
        before = lax.ppermute(last, axis, up)
        after = lax.ppermute(initial, axis, down)
        shard = jnp.concatenate([before, shard, after], axis=dim)
    return shard


def shifted_2(block, axis, distance):
    devices = range(lax.axis_size(axis))
    route = [(i - distance, i) for i in devices if i - distance in devices]
    return lax.ppermute(block, axis, route)


def noise_table():
    position = jnp.arange(NSTEPS, dtype=jnp.float32)
    root_beta = math.sqrt(0.00085) + position / (NSTEPS - 1) * (
        math.sqrt(0.012) - math.sqrt(0.00085)
    )
    return jnp.cumprod(1.0 - root_beta * root_beta)


def look_up(plan, step_ids):
    position = jnp.arange(NSTEPS, dtype=jnp.int32)
    return jnp.sum(jnp.where(position[None, :] == step_ids[:, None], plan[None, :], 0.0), axis=1)


def time_embed(step_ids, w_time):
    half_width = w_time.shape[0] // 2
    frequency = jnp.exp(-math.log(10000.0) * jnp.arange(half_width, dtype=jnp.float32) / half_width)
    angles = step_ids.astype(jnp.float32)[:, None] * frequency[None, :]
    harmonic = jnp.concatenate([jnp.cos(angles), jnp.sin(angles)], axis=1)
    return jax.nn.silu(
        jnp.dot(harmonic, w_time, precision=HIGHEST, preferred_element_type=jnp.float32)
    )


def group_norm(values, first_row, last_row, members):
    frame_total = values.shape[0]
    per_group = values.shape[3] // GROUPS
    inside = values[:, first_row:last_row]
    summed = jnp.sum(inside, axis=(1, 2)).reshape(frame_total, GROUPS, per_group).sum(axis=2)
    square = (
        jnp.sum(inside * inside, axis=(1, 2)).reshape(frame_total, GROUPS, per_group).sum(axis=2)
    )
    summed, square = together((summed, square), "band")
    center = summed / members
    spread = square / members - center * center
    factor = lax.rsqrt(spread + EPSILON)
    center = jnp.repeat(center, per_group, axis=1)
    factor = jnp.repeat(factor, per_group, axis=1)
    return (values - center[:, None, None, :]) * factor[:, None, None, :]


def convolve(padded, kernel, out_rows):
    columns = padded.shape[2]
    widened = jnp.pad(padded, ((0, 0), (0, 0), (1, 1), (0, 0)))
    result = jnp.zeros((padded.shape[0], out_rows, columns, kernel.shape[3]), jnp.float32)
    for row_tap in range(3):
        for col_tap in range(3):
            result = result + jnp.einsum(
                "fhwc,cd->fhwd",
                widened[:, row_tap : row_tap + out_rows, col_tap : col_tap + columns],
                kernel[row_tap, col_tap],
                precision=HIGHEST,
            )
    return result


def block(frames, embedded, w_in, conv_first, conv_second, members):
    band_rows = frames.shape[1]
    lifted = jnp.einsum("fhwk,kc->fhwc", frames, w_in, precision=HIGHEST)
    first_act = jax.nn.silu(group_norm(lifted, 0, band_rows, members))
    padded = padded_2(first_act, (("band", 1),), 2)
    middle = convolve(padded, conv_first, band_rows + 2) + embedded[:, None, None, :]
    second_act = jax.nn.silu(group_norm(middle, 1, band_rows + 1, members))
    row_pos = jnp.arange(band_rows + 2, dtype=jnp.int32)
    band_pos = lax.axis_index("band")
    keep_rows = ((row_pos > 0) | (band_pos > 0)) & (
        (row_pos < band_rows + 1) | (band_pos < lax.axis_size("band") - 1)
    )
    second_act = jnp.where(keep_rows[None, :, None, None], second_act, 0.0)
    hidden = lifted + convolve(second_act, conv_second, band_rows)
    return (hidden, jax.nn.silu(group_norm(hidden, 0, band_rows, members)))


def on_device(latents, timesteps, fresh, w_in, conv_first, conv_second, w_time, temporal, w_out):
    band_rows = latents.shape[2]
    members = float(
        band_rows * lax.axis_size("band") * latents.shape[3] * (w_in.shape[1] // GROUPS)
    )
    plan = noise_table()
    alpha_now = look_up(plan, timesteps)[0]
    alpha_prev = look_up(plan, timesteps - STRIDE)[0]
    embedded = time_embed(timesteps, w_time)
    latent_now = latents[0].transpose(1, 2, 0)
    for iteration in range(ITERS):
        hidden, activated = block(
            latent_now[None], embedded, w_in, conv_first, conv_second, members
        )
        folded = jnp.einsum("kcd,dj->kcj", temporal, w_out, precision=HIGHEST)
        outgoing = jnp.einsum(
            "fhwc,kcj->fkhwj", activated, folded[jnp.array([0, 2])], precision=HIGHEST
        )
        arrived = padded_2(outgoing, (("level", 0),), 1)
        local_part = jnp.einsum("hwc,cj->hwj", hidden[0], w_out, precision=HIGHEST)
        local_part = local_part + jnp.einsum(
            "hwc,cj->hwj", activated[0], folded[1], precision=HIGHEST
        )
        noise_pred = local_part + arrived[0, 0] + arrived[2, 1]
        denoised = (latent_now - jnp.sqrt(1.0 - alpha_now) * noise_pred) / jnp.sqrt(alpha_now)
        latent_now = jnp.sqrt(alpha_prev) * denoised + jnp.sqrt(1.0 - alpha_prev) * noise_pred
        if iteration + 1 < ITERS:
            shifted = shifted_2(latent_now, "level", 1)
            latent_now = jnp.where(
                lax.axis_index("level") == 0, fresh[iteration].transpose(1, 2, 0), shifted
            )
    return latent_now.transpose(2, 0, 1)[None]


def solution(mesh):
    placed = (
        P("level", None, "band", None),
        P("level"),
        P(None, None, "band", None),
        P(),
        P(),
        P(),
        P(),
        P(),
        P(),
    )
    return jax.shard_map(
        on_device,
        mesh=mesh,
        in_specs=placed,
        out_specs=P("level", None, "band", None),
        check_vma=False,
    )
```

profile of v0, /device:TPU:97, one launch (start us, length us, event | category | flops | bytes accessed | tf_op | source)
XLA Modules:
  0.0 201.6 jit_solution(8741669056295483340)
XLA Ops:
  2.7 6.7 %all-to-all-start = ((f32[8,1,64]{2,1,0:T(1,128)}), f32[8,1,64]{2,1,0:T(1,128)S(1)}, u32[]{:S(2)}, u32[]{:S(2)}) async-start(f32[8,1,64]{2,1,0:T(1,128)} %broadcast_in_dim.142), calls=%async_computation | async-start | bytes 8192 | tf_op jit(solution)/shard_map/all_to_all | solution.py:20
  10.7 2.2 %fusion.153 = f32[3,320,4]{1,2,0:T(4,128)S(1)} fusion(f32[3,320,320]{2,1,0:T(8,128)S(1)} %copy-done, f32[320,4]{0,1:T(4,128)} %param.19), kind=kOutput, calls=%fused_computation.226 | convolution fusion | flops 14745600 | bytes 1249280 | tf_op jit(solution)/shard_map/kcd,dj->kcj/dot_general | solution.py:144
  16.5 4.1 %collective-permute-start = (f32[1,2,64,320]{3,2,1,0:T(8,128)S(1)}, f32[1,2,64,320]{3,2,1,0:T(8,128)}, u32[]{:S(2)}, u32[]{:S(2)}) collective-permute-start(f32[1,2,64,320]{3,2,1,0:T(8,128)S(1)} %get-tuple-element.21), channel_id=1, source_target_pairs={{0,1},{1,2},{2,3},{3,4},{4,5},{5,6},{6,7},{8,9},{9,10},{10,11},{11... | collective-permute-start | bytes 491528 | tf_op jit(solution)/shard_map/ppermute | solution.py:46
  22.9 6.0 %collective-permute-done.1 = f32[1,2,64,320]{3,2,1,0:T(8,128)S(1)} collective-permute-done((f32[1,2,64,320]{3,2,1,0:T(8,128)S(1)}, f32[1,2,64,320]{3,2,1,0:T(8,128)S(1)}, u32[]{:S(2)}, u32[]{:S(2)}) %collective-permute-start.1) | collective-permute-done | bytes 163872 | tf_op jit(solution)/shard_map/ppermute | solution.py:47
  30.0 2.5 %fusion.7 = f32[7,64,320]{2,1,0:T(8,128)S(1)} fusion(f32[1,9,64,320]{3,2,1,0:T(8,128)S(1)} %pad_maximum_fusion, f32[3,3,320,320]{3,2,1,0:T(8,128)} %param.15), kind=kOutput, calls=%fused_computation.69 | convolution fusion | flops 550502400 | bytes 1802240 | tf_op jit(solution)/shard_map/fhwc,cd->fhwd/dot_general | solution.py:104
  32.5 2.5 %fusion.18 = f32[7,64,320]{2,1,0:T(8,128)S(1)} fusion(f32[1,9,64,320]{3,2,1,0:T(8,128)S(1)} %pad_maximum_fusion, f32[3,3,320,320]{3,2,1,0:T(8,128)} %param.15), kind=kOutput, calls=%fused_computation.75 | convolution fusion | flops 550502400 | bytes 1802240 | tf_op jit(solution)/shard_map/fhwc,cd->fhwd/dot_general | solution.py:104
  35.0 2.4 %convolution_add_fusion.13 = f32[7,64,320]{2,1,0:T(8,128)S(1)} fusion(f32[7,64,320]{2,1,0:T(8,128)S(1)} %fusion.7, f32[1,5,64,320]{3,2,1,0:T(8,128)S(1)} %multiply_bitcast_fusion.1, f32[1,2,64,320]{3,2,1,0:T(8,128)} %collective-permute-done, f32[3,3,320,320]{3,2,1,0:T(8,128)S(1)} %copy-done.1), kind=kOutput, calls=%fused_computation.18 | convolution fusion | flops 550789120 | bytes 2408448 | tf_op jit(solution)/shard_map/fhwc,cd->fhwd/dot_general | solution.py:104
  47.9 4.5 %all-to-all-start.1 = ((f32[8,1,64]{2,1,0:T(1,128)}), f32[8,1,64]{2,1,0:T(1,128)S(1)}, u32[]{:S(2)}, u32[]{:S(2)}) async-start(f32[8,1,64]{2,1,0:T(1,128)} %broadcast_in_dim.147), calls=%async_computation.1 | async-start | bytes 8192 | tf_op jit(solution)/shard_map/all_to_all | solution.py:20
  52.4 6.4 %all-to-all-done.1 = f32[8,1,64]{2,1,0:T(1,128)S(1)} async-done(((f32[8,1,64]{2,1,0:T(1,128)}), f32[8,1,64]{2,1,0:T(1,128)S(1)}, u32[]{:S(2)}, u32[]{:S(2)}) %all-to-all-start.1) | async-done | bytes 2080 | tf_op jit(solution)/shard_map/all_to_all | solution.py:20
  59.6 2.3 %fusion.43 = f32[5,64,320]{2,1,0:T(8,128)S(1)} fusion(f32[1,7,64,320]{3,2,1,0:T(8,128)S(1)} %select_bitcast_fusion.1, f32[3,3,320,320]{3,2,1,0:T(8,128)} %param.16), kind=kOutput, calls=%fused_computation.101 | convolution fusion | flops 393216000 | bytes 1474560 | tf_op jit(solution)/shard_map/fhwc,cd->fhwd/dot_general | solution.py:104
  61.8 2.1 %convolution_add_fusion.29 = f32[5,64,320]{2,1,0:T(8,128)S(1)} fusion(f32[5,64,320]{2,1,0:T(8,128)S(1)} %fusion.43, f32[1,7,64,320]{3,2,1,0:T(8,128)S(1)} %select_bitcast_fusion.1, f32[3,3,320,320]{3,2,1,0:T(8,128)} %param.16), kind=kOutput, calls=%fused_computation.36 | convolution fusion | flops 393318400 | bytes 1884160 | tf_op jit(solution)/shard_map/fhwc,cd->fhwd/dot_general | solution.py:104
  64.0 2.1 %convolution_add_fusion.28 = f32[5,64,320]{2,1,0:T(8,128)S(1)} fusion(f32[5,64,320]{2,1,0:T(8,128)S(1)} %convolution_add_fusion.29, f32[1,7,64,320]{3,2,1,0:T(8,128)S(1)} %select_bitcast_fusion.1, f32[3,3,320,320]{3,2,1,0:T(8,128)} %param.16), kind=kOutput, calls=%fused_computation.35 | convolution fusion | flops 393318400 | bytes 1884160 | tf_op jit(solution)/shard_map/fhwc,cd->fhwd/dot_general | solution.py:104
  66.1 2.1 %convolution_add_fusion.27 = f32[5,64,320]{2,1,0:T(8,128)S(1)} fusion(f32[5,64,320]{2,1,0:T(8,128)S(1)} %convolution_add_fusion.28, f32[1,7,64,320]{3,2,1,0:T(8,128)S(1)} %select_bitcast_fusion.1, f32[3,3,320,320]{3,2,1,0:T(8,128)} %param.16), kind=kOutput, calls=%fused_computation.34 | convolution fusion | flops 393318400 | bytes 1884160 | tf_op jit(solution)/shard_map/fhwc,cd->fhwd/dot_general | solution.py:104
  75.0 3.3 %all-to-all-start.2 = ((f32[8,1,64]{2,1,0:T(1,128)}), f32[8,1,64]{2,1,0:T(1,128)S(1)}, u32[]{:S(2)}, u32[]{:S(2)}) async-start(f32[8,1,64]{2,1,0:T(1,128)} %broadcast_in_dim.153), calls=%async_computation.2 | async-start | bytes 8192 | tf_op jit(solution)/shard_map/all_to_all | solution.py:20
  81.6 3.1 %all-to-all-done.2 = f32[8,1,64]{2,1,0:T(1,128)S(1)} async-done(((f32[8,1,64]{2,1,0:T(1,128)}), f32[8,1,64]{2,1,0:T(1,128)S(1)}, u32[]{:S(2)}, u32[]{:S(2)}) %all-to-all-start.2) | async-done | bytes 2080 | tf_op jit(solution)/shard_map/all_to_all | solution.py:20
  86.1 10.5 %collective-permute-start.2 = (f32[1,2,5,64,4]{3,4,2,1,0:T(4,128)S(1)}, f32[1,2,5,64,4]{3,4,2,1,0:T(4,128)S(1)}, u32[]{:S(2)}, u32[]{:S(2)}) collective-permute-start(f32[1,2,5,64,4]{3,4,2,1,0:T(4,128)S(1)} %convolution_bitcast_fusion.1), channel_id=1, source_target_pairs={{0,8},{8,16},{16,24},{24,32},{32,40},{40,48},{48,56},{56,64},{64,7... | collective-permute-start | bytes 30728 | tf_op jit(solution)/shard_map/ppermute | solution.py:46
  96.6 2.1 %collective-permute-start.3 = (f32[1,2,5,64,4]{3,4,2,1,0:T(4,128)S(1)}, f32[1,2,5,64,4]{3,4,2,1,0:T(4,128)S(1)}, u32[]{:S(2)}, u32[]{:S(2)}) collective-permute-start(f32[1,2,5,64,4]{3,4,2,1,0:T(4,128)S(1)} %convolution_bitcast_fusion.1), channel_id=1, source_target_pairs={{8,0},{16,8},{24,16},{32,24},{40,32},{48,40},{56,48},{64,56},{72,6... | collective-permute-start | bytes 30728 | tf_op jit(solution)/shard_map/ppermute | solution.py:47
  99.6 3.4 %collective-permute-done.3 = f32[1,2,5,64,4]{3,4,2,1,0:T(4,128)S(1)} collective-permute-done((f32[1,2,5,64,4]{3,4,2,1,0:T(4,128)S(1)}, f32[1,2,5,64,4]{3,4,2,1,0:T(4,128)S(1)}, u32[]{:S(2)}, u32[]{:S(2)}) %collective-permute-start.3) | collective-permute-done | bytes 10272 | tf_op jit(solution)/shard_map/ppermute | solution.py:47
  103.9 1.9 collective-permute-start.4
  108.3 8.9 %all_to_all.36 = f32[8,1,64]{2,1,0:T(1,128)S(1)} all-to-all(f32[8,1,64]{2,1,0:T(1,128)S(1)} %broadcast_in_dim.159), channel_id=1, replica_groups=mesh['level'=32,'band'=8] {'band'}, dimensions={0} | all-to-all | bytes 4096 | tf_op jit(solution)/shard_map/all_to_all | solution.py:20
  117.9 2.5 %collective-permute-start.5 = (f32[1,2,64,320]{3,2,1,0:T(8,128)S(1)}, f32[1,2,64,320]{3,2,1,0:T(8,128)S(1)}, u32[]{:S(2)}, u32[]{:S(2)}) collective-permute-start(f32[1,2,64,320]{3,2,1,0:T(8,128)S(1)} %get-tuple-element.19), channel_id=1, source_target_pairs={{0,1},{1,2},{2,3},{3,4},{4,5},{5,6},{6,7},{8,9},{9,10},{10,11},{11... | collective-permute-start | bytes 491528 | tf_op jit(solution)/shard_map/ppermute | solution.py:46
  122.9 5.3 %collective-permute-done.6 = f32[1,2,64,320]{3,2,1,0:T(8,128)S(1)} collective-permute-done((f32[1,2,64,320]{3,2,1,0:T(8,128)S(1)}, f32[1,2,64,320]{3,2,1,0:T(8,128)S(1)}, u32[]{:S(2)}, u32[]{:S(2)}) %collective-permute-start.6) | collective-permute-done | bytes 163872 | tf_op jit(solution)/shard_map/ppermute | solution.py:47
  128.3 2.5 %fusion.21 = f32[7,64,320]{2,1,0:T(8,128)S(1)} fusion(f32[1,9,64,320]{3,2,1,0:T(8,128)S(1)} %pad_maximum_fusion.1, f32[3,3,320,320]{3,2,1,0:T(8,128)} %param.15), kind=kOutput, calls=%fused_computation.77 | convolution fusion | flops 550502400 | bytes 1802240 | tf_op jit(solution)/shard_map/fhwc,cd->fhwd/dot_general | solution.py:104
  130.9 2.5 %fusion.32 = f32[7,64,320]{2,1,0:T(8,128)S(1)} fusion(f32[1,9,64,320]{3,2,1,0:T(8,128)S(1)} %pad_maximum_fusion.1, f32[3,3,320,320]{3,2,1,0:T(8,128)} %param.15), kind=kOutput, calls=%fused_computation.83 | convolution fusion | flops 550502400 | bytes 1802240 | tf_op jit(solution)/shard_map/fhwc,cd->fhwd/dot_general | solution.py:104
  144.5 13.7 %all_to_all.37 = f32[8,1,64]{2,1,0:T(1,128)S(1)} all-to-all(f32[8,1,64]{2,1,0:T(1,128)S(1)} %broadcast_in_dim.164), channel_id=1, replica_groups=mesh['level'=32,'band'=8] {'band'}, dimensions={0} | all-to-all | bytes 4096 | tf_op jit(solution)/shard_map/all_to_all | solution.py:20
  158.9 2.3 %fusion.56 = f32[5,64,320]{2,1,0:T(8,128)S(1)} fusion(f32[1,7,64,320]{3,2,1,0:T(8,128)S(1)} %select_bitcast_fusion, f32[3,3,320,320]{3,2,1,0:T(8,128)} %param.16), kind=kOutput, calls=%fused_computation.108 | convolution fusion | flops 393216000 | bytes 1474560 | tf_op jit(solution)/shard_map/fhwc,cd->fhwd/dot_general | solution.py:104
  161.2 2.1 %convolution_add_fusion.21 = f32[5,64,320]{2,1,0:T(8,128)S(1)} fusion(f32[5,64,320]{2,1,0:T(8,128)S(1)} %fusion.56, f32[1,7,64,320]{3,2,1,0:T(8,128)S(1)} %select_bitcast_fusion, f32[3,3,320,320]{3,2,1,0:T(8,128)} %param.16), kind=kOutput, calls=%fused_computation.27 | convolution fusion | flops 393318400 | bytes 1884160 | tf_op jit(solution)/shard_map/fhwc,cd->fhwd/dot_general | solution.py:104
  163.3 2.1 %convolution_add_fusion.20 = f32[5,64,320]{2,1,0:T(8,128)S(1)} fusion(f32[5,64,320]{2,1,0:T(8,128)S(1)} %convolution_add_fusion.21, f32[1,7,64,320]{3,2,1,0:T(8,128)S(1)} %select_bitcast_fusion, f32[3,3,320,320]{3,2,1,0:T(8,128)} %param.16), kind=kOutput, calls=%fused_computation.26 | convolution fusion | flops 393318400 | bytes 1884160 | tf_op jit(solution)/shard_map/fhwc,cd->fhwd/dot_general | solution.py:104
  165.5 2.1 %convolution_add_fusion.19 = f32[5,64,320]{2,1,0:T(8,128)S(1)} fusion(f32[5,64,320]{2,1,0:T(8,128)S(1)} %convolution_add_fusion.20, f32[1,7,64,320]{3,2,1,0:T(8,128)S(1)} %select_bitcast_fusion, f32[3,3,320,320]{3,2,1,0:T(8,128)} %param.16), kind=kOutput, calls=%fused_computation.25 | convolution fusion | flops 393318400 | bytes 1884160 | tf_op jit(solution)/shard_map/fhwc,cd->fhwd/dot_general | solution.py:104
  173.8 8.9 %all_to_all.38 = f32[8,1,64]{2,1,0:T(1,128)S(1)} all-to-all(f32[8,1,64]{2,1,0:T(1,128)S(1)} %broadcast_in_dim.169), channel_id=1, replica_groups=mesh['level'=32,'band'=8] {'band'}, dimensions={0} | all-to-all | bytes 4096 | tf_op jit(solution)/shard_map/all_to_all | solution.py:20
  184.0 9.5 %collective-permute-start.7 = (f32[1,2,5,64,4]{3,4,2,1,0:T(4,128)S(1)}, f32[1,2,5,64,4]{3,4,2,1,0:T(4,128)S(1)}, u32[]{:S(2)}, u32[]{:S(2)}) collective-permute-start(f32[1,2,5,64,4]{3,4,2,1,0:T(4,128)S(1)} %convolution_bitcast_fusion), channel_id=1, source_target_pairs={{0,8},{8,16},{16,24},{24,32},{32,40},{40,48},{48,56},{56,64},{64,7... | collective-permute-start | bytes 30728 | tf_op jit(solution)/shard_map/ppermute | solution.py:46
  196.2 3.6 %collective-permute-done.8 = f32[1,2,5,64,4]{3,4,2,1,0:T(4,128)S(1)} collective-permute-done((f32[1,2,5,64,4]{3,4,2,1,0:T(4,128)S(1)}, f32[1,2,5,64,4]{3,4,2,1,0:T(4,128)S(1)}, u32[]{:S(2)}, u32[]{:S(2)}) %collective-permute-start.8) | collective-permute-done | bytes 10272 | tf_op jit(solution)/shard_map/ppermute | solution.py:47
  (168 shorter events, 61.0 us)
Async XLA Ops:
  0.0 10.7 %copy-start = (f32[3,320,320]{2,1,0:T(8,128)S(1)}, f32[3,320,320]{2,1,0:T(8,128)}, u32[]{:S(2)}) copy-start(f32[3,320,320]{2,1,0:T(8,128)} %param.18) | copy-start | bytes 3686404
  2.7 13.1 %all-to-all-start = ((f32[8,1,64]{2,1,0:T(1,128)}), f32[8,1,64]{2,1,0:T(1,128)S(1)}, u32[]{:S(2)}, u32[]{:S(2)}) async-start(f32[8,1,64]{2,1,0:T(1,128)} %broadcast_in_dim.142), calls=%async_computation | async-start | bytes 8192 | tf_op jit(solution)/shard_map/all_to_all | solution.py:20
  16.5 6.4 %collective-permute-start = (f32[1,2,64,320]{3,2,1,0:T(8,128)S(1)}, f32[1,2,64,320]{3,2,1,0:T(8,128)}, u32[]{:S(2)}, u32[]{:S(2)}) collective-permute-start(f32[1,2,64,320]{3,2,1,0:T(8,128)S(1)} %get-tuple-element.21), channel_id=1, source_target_pairs={{0,1},{1,2},{2,3},{3,4},{4,5},{5,6},{6,7},{8,9},{9,10},{10,11},{11... | collective-permute-start | bytes 491528 | tf_op jit(solution)/shard_map/ppermute | solution.py:46
  20.6 8.3 %collective-permute-start.1 = (f32[1,2,64,320]{3,2,1,0:T(8,128)S(1)}, f32[1,2,64,320]{3,2,1,0:T(8,128)S(1)}, u32[]{:S(2)}, u32[]{:S(2)}) collective-permute-start(f32[1,2,64,320]{3,2,1,0:T(8,128)S(1)} %get-tuple-element.22), channel_id=1, source_target_pairs={{1,0},{2,1},{3,2},{4,3},{5,4},{6,5},{7,6},{9,8},{10,9},{11,10},{12... | collective-permute-start | bytes 491528 | tf_op jit(solution)/shard_map/ppermute | solution.py:47
  22.1 12.9 %copy-start.1 = (f32[3,3,320,320]{3,2,1,0:T(8,128)S(1)}, f32[3,3,320,320]{3,2,1,0:T(8,128)}, u32[]{:S(2)}) copy-start(f32[3,3,320,320]{3,2,1,0:T(8,128)} %param.15) | copy-start | bytes 11059204
  28.9 10.0 %copy-start.2 = (f32[1,2,64,320]{3,2,1,0:T(8,128)}, f32[1,2,64,320]{3,2,1,0:T(8,128)S(1)}, u32[]{:S(2)}) copy-start(f32[1,2,64,320]{3,2,1,0:T(8,128)S(1)} %collective-permute-done.1) | copy-start | bytes 491524
  40.4 4.4 %copy-start.3 = (f32[1,2,64,320]{3,2,1,0:T(8,128)S(1)}, f32[1,2,64,320]{3,2,1,0:T(8,128)}, u32[]{:S(2)}) copy-start(f32[1,2,64,320]{3,2,1,0:T(8,128)} %copy-done.2) | copy-start | bytes 491524
  44.8 23.5 %slice-start.2 = ((s8[4423680]{0:T(1024)(128)(4,1)}), s8[229376]{0:T(1024)(128)(4,1)S(1)}, s32[]{:S(2)}) async-start(s8[4423680]{0:T(1024)(128)(4,1)} %bitcast.374), calls=%async_computation.8 | async-start | bytes 458752
  47.9 10.9 %all-to-all-start.1 = ((f32[8,1,64]{2,1,0:T(1,128)}), f32[8,1,64]{2,1,0:T(1,128)S(1)}, u32[]{:S(2)}, u32[]{:S(2)}) async-start(f32[8,1,64]{2,1,0:T(1,128)} %broadcast_in_dim.147), calls=%async_computation.1 | async-start | bytes 8192 | tf_op jit(solution)/shard_map/all_to_all | solution.py:20
  59.5 8.7 %slice-start.3 = ((s8[4423680]{0:T(1024)(128)(4,1)}), s8[4194304]{0:T(1024)(128)(4,1)S(1)}, s32[]{:S(2)}) async-start(s8[4423680]{0:T(1024)(128)(4,1)} %bitcast.374), calls=%async_computation.9 | async-start | bytes 8388608
  71.6 27.1 %copy-start.4 = (f32[320,4]{0,1:T(4,128)S(1)}, f32[320,4]{0,1:T(4,128)}, u32[]{:S(2)}) copy-start(f32[320,4]{0,1:T(4,128)} %param.19) | copy-start | bytes 15364
  71.6 31.3 %copy-start.6 = (f32[1,4,5,64]{3,1,2,0:T(4,128)S(1)}, f32[1,4,5,64]{3,1,2,0:T(4,128)}, u32[]{:S(2)}) copy-start(f32[1,4,5,64]{3,1,2,0:T(4,128)} %param.11) | copy-start | bytes 15364
  72.7 34.2 %copy-start.5 = (f32[4,320]{1,0:T(4,128)S(1)}, f32[4,320]{1,0:T(4,128)}, u32[]{:S(2)}) copy-start(f32[4,320]{1,0:T(4,128)} %param.14) | copy-start | bytes 15364
  72.7 34.2 %copy-start.7 = (f32[1,4,5,64]{3,1,2,0:T(4,128)S(1)}, f32[1,4,5,64]{3,1,2,0:T(4,128)}, u32[]{:S(2)}) copy-start(f32[1,4,5,64]{3,1,2,0:T(4,128)} %param.13) | copy-start | bytes 15364
  75.0 9.7 %all-to-all-start.2 = ((f32[8,1,64]{2,1,0:T(1,128)}), f32[8,1,64]{2,1,0:T(1,128)S(1)}, u32[]{:S(2)}, u32[]{:S(2)}) async-start(f32[8,1,64]{2,1,0:T(1,128)} %broadcast_in_dim.153), calls=%async_computation.2 | async-start | bytes 8192 | tf_op jit(solution)/shard_map/all_to_all | solution.py:20
  85.2 48.2 %slice-start = ((s8[4423680]{0:T(1024)(128)(4,1)}), s8[229376]{0:T(1024)(128)(4,1)S(1)}, s32[]{:S(2)}) async-start(s8[4423680]{0:T(1024)(128)(4,1)} %bitcast.372), calls=%async_computation.6 | async-start | bytes 458752
  86.1 13.5 %collective-permute-start.2 = (f32[1,2,5,64,4]{3,4,2,1,0:T(4,128)S(1)}, f32[1,2,5,64,4]{3,4,2,1,0:T(4,128)S(1)}, u32[]{:S(2)}, u32[]{:S(2)}) collective-permute-start(f32[1,2,5,64,4]{3,4,2,1,0:T(4,128)S(1)} %convolution_bitcast_fusion.1), channel_id=1, source_target_pairs={{0,8},{8,16},{16,24},{24,32},{32,40},{40,48},{48,56},{56,64},{64,7... | collective-permute-start | bytes 30728 | tf_op jit(solution)/shard_map/ppermute | solution.py:46
  96.6 6.3 %collective-permute-start.3 = (f32[1,2,5,64,4]{3,4,2,1,0:T(4,128)S(1)}, f32[1,2,5,64,4]{3,4,2,1,0:T(4,128)S(1)}, u32[]{:S(2)}, u32[]{:S(2)}) collective-permute-start(f32[1,2,5,64,4]{3,4,2,1,0:T(4,128)S(1)} %convolution_bitcast_fusion.1), channel_id=1, source_target_pairs={{8,0},{16,8},{24,16},{32,24},{40,32},{48,40},{56,48},{64,56},{72,6... | collective-permute-start | bytes 30728 | tf_op jit(solution)/shard_map/ppermute | solution.py:47
  103.9 3.1 %collective-permute-start.4 = (f32[5,64,4]{1,2,0:T(4,128)S(1)}, f32[5,64,4]{1,2,0:T(4,128)S(1)}, u32[]{:S(2)}, u32[]{:S(2)}) collective-permute-start(f32[5,64,4]{1,2,0:T(4,128)S(1)} %multiply_add_fusion), channel_id=1, source_target_pairs={{0,8},{8,16},{16,24},{24,32},{32,40},{40,48},{48,56},{56,64},{64,7... | collective-permute-start | bytes 15368 | tf_op jit(solution)/shard_map/ppermute | solution.py:55
  117.7 15.7 %slice-start.1 = ((s8[4423680]{0:T(1024)(128)(4,1)}), s8[4194304]{0:T(1024)(128)(4,1)S(1)}, s32[]{:S(2)}) async-start(s8[4423680]{0:T(1024)(128)(4,1)} %bitcast.372), calls=%async_computation.7 | async-start | bytes 8388608
  117.9 5.1 %collective-permute-start.5 = (f32[1,2,64,320]{3,2,1,0:T(8,128)S(1)}, f32[1,2,64,320]{3,2,1,0:T(8,128)S(1)}, u32[]{:S(2)}, u32[]{:S(2)}) collective-permute-start(f32[1,2,64,320]{3,2,1,0:T(8,128)S(1)} %get-tuple-element.19), channel_id=1, source_target_pairs={{0,1},{1,2},{2,3},{3,4},{4,5},{5,6},{6,7},{8,9},{9,10},{10,11},{11... | collective-permute-start | bytes 491528 | tf_op jit(solution)/shard_map/ppermute | solution.py:46
  120.3 7.9 %collective-permute-start.6 = (f32[1,2,64,320]{3,2,1,0:T(8,128)S(1)}, f32[1,2,64,320]{3,2,1,0:T(8,128)S(1)}, u32[]{:S(2)}, u32[]{:S(2)}) collective-permute-start(f32[1,2,64,320]{3,2,1,0:T(8,128)S(1)} %get-tuple-element.20), channel_id=1, source_target_pairs={{1,0},{2,1},{3,2},{4,3},{5,4},{6,5},{7,6},{9,8},{10,9},{11,10},{12... | collective-permute-start | bytes 491528 | tf_op jit(solution)/shard_map/ppermute | solution.py:47
  142.2 25.4 %slice-start.4 = ((s8[4423680]{0:T(1024)(128)(4,1)}), s8[229376]{0:T(1024)(128)(4,1)S(1)}, s32[]{:S(2)}) async-start(s8[4423680]{0:T(1024)(128)(4,1)} %bitcast.376), calls=%async_computation.10 | async-start | bytes 458752
  158.9 8.7 %slice-start.5 = ((s8[4423680]{0:T(1024)(128)(4,1)}), s8[4194304]{0:T(1024)(128)(4,1)S(1)}, s32[]{:S(2)}) async-start(s8[4423680]{0:T(1024)(128)(4,1)} %bitcast.376), calls=%async_computation.11 | async-start | bytes 8388608
  184.0 12.2 %collective-permute-start.7 = (f32[1,2,5,64,4]{3,4,2,1,0:T(4,128)S(1)}, f32[1,2,5,64,4]{3,4,2,1,0:T(4,128)S(1)}, u32[]{:S(2)}, u32[]{:S(2)}) collective-permute-start(f32[1,2,5,64,4]{3,4,2,1,0:T(4,128)S(1)} %convolution_bitcast_fusion), channel_id=1, source_target_pairs={{0,8},{8,16},{16,24},{24,32},{32,40},{40,48},{48,56},{56,64},{64,7... | collective-permute-start | bytes 30728 | tf_op jit(solution)/shard_map/ppermute | solution.py:46
  193.5 6.3 %collective-permute-start.8 = (f32[1,2,5,64,4]{3,4,2,1,0:T(4,128)S(1)}, f32[1,2,5,64,4]{3,4,2,1,0:T(4,128)S(1)}, u32[]{:S(2)}, u32[]{:S(2)}) collective-permute-start(f32[1,2,5,64,4]{3,4,2,1,0:T(4,128)S(1)} %convolution_bitcast_fusion), channel_id=1, source_target_pairs={{8,0},{16,8},{24,16},{32,24},{40,32},{48,40},{56,48},{64,56},{72,6... | collective-permute-start | bytes 30728 | tf_op jit(solution)/shard_map/ppermute | solution.py:47
where the time goes:
time: 206 us; the launch traced here: 202 us
  matrix products  72.5 us (35%)
  starting transfers between devices  49.7 us (24%)
  waiting for transfers between devices  31.9 us (15%)
  blocking collectives  31.5 us (15%)
  local copies, waits for them, and re-layouts  6.16 us (3%)
  other arithmetic  5.55 us (3%)
  between operations  4.25 us (2%)
    dot_general x36, matrix products, convolve(): jnp.einsum('fhwc,cd->fhwd', widened[:, row_tap:row_tap + out_rows, col_ta...  60.5 us
    all_to_all x3, blocking collectives, copy_for_each(): lax.all_to_all(jnp.broadcast_to(shard[None], (size, *shard.shape)), axis,...  31.5 us
    ppermute x4, starting transfers between devices, padded_2(): before = lax.ppermute(last, axis, up)  26.6 us
    ppermute x4, waiting for transfers between devices, padded_2(): after = lax.ppermute(initial, axis, down)  18.3 us
    all_to_all x3, starting transfers between devices, copy_for_each(): lax.all_to_all(jnp.broadcast_to(shard[None], (size, *shard.shape)), axis,...  14.5 us
    all_to_all x3, waiting for transfers between devices, copy_for_each(): lax.all_to_all(jnp.broadcast_to(shard[None], (size, *shard.shape)), axis,...  11.1 us
    ppermute x4, starting transfers between devices, padded_2(): after = lax.ppermute(initial, axis, down)  6.76 us
  transfers between devices with their start and end apart: 12, of which 10 were waited for; matrix products, arithmetic and copies ran while one was open for 4% of the time, Pallas kernels for 0%

commit v1 on v0

v1 whole, which is shorter than its diff:
```python
import functools
import math

import jax
import jax.numpy as jnp
import numpy as np
from jax import lax
from jax.experimental import pallas as pl
from jax.experimental.pallas import tpu as pltpu
from jax.sharding import PartitionSpec as P

GROUPS = 32
ITERS = 2
NSTEPS = 1000
STRIDE = 16

EPSILON = 1e-05
HIGHEST = lax.Precision.HIGHEST
BF16 = jnp.bfloat16
F32 = jnp.float32


def noise_plan():
    position = np.arange(NSTEPS, dtype=np.float64)
    root_beta = math.sqrt(0.00085) + position / (NSTEPS - 1) * (
        math.sqrt(0.012) - math.sqrt(0.00085)
    )
    return np.cumprod(1.0 - root_beta * root_beta).astype(np.float32)


def time_embed(step_ids, w_time):
    half_width = w_time.shape[0] // 2
    frequency = jnp.exp(-math.log(10000.0) * jnp.arange(half_width, dtype=F32) / half_width)
    angles = step_ids.astype(F32)[:, None] * frequency[None, :]
    harmonic = jnp.concatenate([jnp.cos(angles), jnp.sin(angles)], axis=1)
    return jax.nn.silu(jnp.dot(harmonic, w_time, precision=HIGHEST, preferred_element_type=F32))


def halves(v):
    hi = v.astype(BF16)
    return hi, (v - hi.astype(F32)).astype(BF16)


def thirds(v):
    one = v.astype(BF16).astype(F32)
    two = (v - one).astype(BF16).astype(F32)
    three = ((v - one) - two).astype(BF16).astype(F32)
    return one, two, three


def silu(v):
    return v / (1.0 + jnp.exp(-v))


def group_mean(rows):
    channels = rows.shape[1]
    per_group = channels // GROUPS
    one, two, three = thirds(rows)
    stacked = jnp.concatenate([one, two, three, one * 0.0], axis=0).astype(BF16)
    shape = (channels, channels)
    factor = (1 << 16) // per_group + 1
    here = (lax.broadcasted_iota(jnp.int32, shape, 0) * factor) >> 16
    there = (lax.broadcasted_iota(jnp.int32, shape, 1) * factor) >> 16
    member = jnp.where(here == there, 1.0, 0.0).astype(BF16)
    total = jnp.dot(stacked, member, preferred_element_type=F32)
    return (total[0:2] + total[2:4] + total[4:6]) * (1.0 / per_group)


def center_factor(means):
    grouped = group_mean(means)
    center = grouped[0:1]
    return center, lax.rsqrt(grouped[1:2] - center * center + EPSILON)


def lift(frame, w):
    f1, f2, f3 = thirds(frame)
    w1, w2, w3 = thirds(w)
    left = jnp.concatenate([f1, f1, f2, f1, f2, f3], axis=0).astype(BF16)
    right = jnp.concatenate([w1, w2, w1, w3, w2, w1], axis=0).astype(BF16)
    return lax.dot_general(left, right, (((0,), (0,)), ((), ())), preferred_element_type=F32)


def put_left(a_ref, rows, act):
    hi, lo = halves(act)
    a_ref[rows, 0:256] = hi[:, 0:256]
    a_ref[rows, 256:512] = lo[:, 0:256]
    a_ref[rows, 512:768] = hi[:, 0:256]
    a_ref[rows, 768:896] = jnp.concatenate([hi[:, 256:320], lo[:, 256:320]], axis=1)
    a_ref[rows, 896:960] = hi[:, 256:320]


def put_right(b_ref, w_ref):
    for k in range(5):
        hi, lo = zip(*[halves(w_ref[0, c, 64 * k : 64 * k + 64, :]) for c in range(3)])
        if k < 4:
            places = ((64 * k, hi), (256 + 64 * k, hi), (512 + 64 * k, lo))
        else:
            places = ((768, hi), (832, hi), (896, lo))
        for at, part in places:
            for c in range(3):
                b_ref[at : at + 64, 256 * c : 256 * c + 256] = part[c][:, 0:256]
            b_ref[at : at + 64, 768:896] = jnp.concatenate(
                [part[0][:, 256:320], part[1][:, 256:320]], axis=1
            )
            b_ref[at : at + 64, 896:960] = part[2][:, 256:320]


def accumulate(acc_ref, a_ref, b_ref, tap, count):
    left = a_ref[pl.ds(pl.multiple_of(tap * 64, 64), count), :]
    for n, (lo, hi) in enumerate(((0, 256), (256, 512), (512, 768), (768, 960))):
        part = jnp.dot(left, b_ref[:, lo:hi], preferred_element_type=F32)

        @pl.when(tap == 0)
        def _():
            acc_ref[8 : 8 + count, lo:hi] = part

        @pl.when(tap > 0)
        def _():
            acc_ref[8 : 8 + count, lo:hi] += part


def shifted_sum(acc_ref, row):
    base = 8 + 64 * row
    column = lax.broadcasted_iota(jnp.int32, (64, 1), 0)
    first = column > 0
    last = column < 63
    main = (
        jnp.where(first, acc_ref[base - 1 : base + 63, 0:256], 0.0)
        + acc_ref[base : base + 64, 256:512]
        + jnp.where(last, acc_ref[base + 1 : base + 65, 512:768], 0.0)
    )
    rest = (
        jnp.where(first, acc_ref[base - 1 : base + 63, 768:832], 0.0)
        + acc_ref[base : base + 64, 832:896]
        + jnp.where(last, acc_ref[base + 1 : base + 65, 896:960], 0.0)
    )
    return jnp.concatenate([main, rest], axis=1)


def conv1_kernel(
    members, band_ref, frame_ref, w_in_ref, emb_ref, w_ref, mid_ref, stat_ref, a_ref, b_ref,
    acc_ref, lift_ref,
):
    tap = pl.program_id(0)
    band = band_ref[0]
    bands = frame_ref.shape[0]

    @pl.when(tap == 0)
    def _():
        frame = frame_ref[...]
        w = w_in_ref[...]
        average = 1.0 / members
        mean = jnp.sum(jnp.sum(frame, axis=0), axis=1, keepdims=True) * average
        mean = jnp.sum(mean * w, axis=0, keepdims=True)
        square = jnp.zeros_like(mean)
        for j in range(4):
            moment = jnp.sum(frame * frame[:, j : j + 1, :], axis=0)
            moment = jnp.sum(moment, axis=1, keepdims=True) * average
            square += w[j : j + 1] * jnp.sum(moment * w, axis=0, keepdims=True)
        center, factor = center_factor(jnp.concatenate([mean, square], axis=0))
        before = frame_ref[jnp.maximum(band - 1, 0)]
        after = frame_ref[jnp.minimum(band + 1, bands - 1)]
        around = jnp.concatenate(
            [before[:, 192:320], frame_ref[band], after[:, 0:128]], axis=1
        )
        lift_ref[...] = lift(around, w)
        for i in range(9):
            rows = slice(64 * i, 64 * i + 64)
            act = silu((lift_ref[rows, :] - center) * factor)
            if i < 2:
                act = act * jnp.where(band > 0, 1.0, 0.0)
            elif i >= 7:
                act = act * jnp.where(band < bands - 1, 1.0, 0.0)
            put_left(a_ref, rows, act)

    put_right(b_ref, w_ref)
    accumulate(acc_ref, a_ref, b_ref, tap, 448)

    @pl.when(tap == 2)
    def _():
        total = jnp.zeros((8, 320), F32)
        square = jnp.zeros((8, 320), F32)
        for i in range(7):
            out = shifted_sum(acc_ref, i) + emb_ref[...]
            mid_ref[64 * i : 64 * i + 64, :] = out
            if 1 <= i <= 5:
                folded = out.reshape(8, 8, 320)
                total += jnp.sum(folded, axis=0)
                square += jnp.sum(folded * folded, axis=0)
        stat_ref[...] = jnp.broadcast_to(
            jnp.concatenate(
                [jnp.sum(total, axis=0, keepdims=True), jnp.sum(square, axis=0, keepdims=True)],
                axis=0,
            )[None],
            stat_ref.shape,
        )


def conv2_kernel(
    members, band_ref, mid_ref, sums_ref, own_ref, w_in_ref, w_ref, hid_ref, stat_ref, a_ref,
    b_ref, acc_ref,
):
    tap = pl.program_id(0)
    band = band_ref[0]
    bands = sums_ref.shape[0]

    @pl.when(tap == 0)
    def _():
        center, factor = center_factor(jnp.sum(sums_ref[...], axis=0) * (1.0 / members))
        for i in range(7):
            rows = slice(64 * i, 64 * i + 64)
            act = silu((mid_ref[rows, :] - center) * factor)
            if i == 0:
                act = act * jnp.where(band > 0, 1.0, 0.0)
            elif i == 6:
                act = act * jnp.where(band < bands - 1, 1.0, 0.0)
            put_left(a_ref, rows, act)

    put_right(b_ref, w_ref)
    accumulate(acc_ref, a_ref, b_ref, tap, 320)

    @pl.when(tap == 2)
    def _():
        total = jnp.zeros((8, 320), F32)
        square = jnp.zeros((8, 320), F32)
        hid_ref[...] = lift(own_ref[...], w_in_ref[...])
        for i in range(5):
            rows = slice(64 * i, 64 * i + 64)
            out = hid_ref[rows, :] + shifted_sum(acc_ref, i)
            hid_ref[rows, :] = out
            folded = out.reshape(8, 8, 320)
            total += jnp.sum(folded, axis=0)
            square += jnp.sum(folded * folded, axis=0)
        stat_ref[...] = jnp.broadcast_to(
            jnp.concatenate(
                [jnp.sum(total, axis=0, keepdims=True), jnp.sum(square, axis=0, keepdims=True)],
                axis=0,
            )[None],
            stat_ref.shape,
        )


def project_kernel(members, coef_ref, hid_ref, sums_ref, own_ref, w_out_ref, fold_ref, out_ref):
    center, factor = center_factor(jnp.sum(sums_ref[...], axis=0) * (1.0 / members))
    hidden = hid_ref[...]
    act = silu((hidden - center) * factor)
    dims = (((1,), (1,)), ((), ()))
    h_hi, h_lo = halves(hidden)
    a_hi, a_lo = halves(act)
    w_hi, w_lo = halves(w_out_ref[...])
    f_hi, f_lo = halves(fold_ref[...])

    def product(l_hi, l_lo, r_hi, r_lo):
        both = lax.dot_general(
            jnp.concatenate([l_hi, l_lo], axis=0), r_hi, dims, preferred_element_type=F32
        )
        n = l_hi.shape[0]
        return (
            both[0:n] + both[n:]
            + lax.dot_general(l_hi, r_lo, dims, preferred_element_type=F32)
        )

    from_hidden = product(w_hi, w_lo, h_hi, h_lo)
    from_act = product(f_hi, f_lo, a_hi, a_lo)
    local = from_hidden[0:4] + from_act[0:4]
    out_ref[0:4] = coef_ref[0] * own_ref[...] + coef_ref[1] * local
    out_ref[4:8] = from_act[4:8]
    out_ref[8:12] = from_act[8:12]
    out_ref[12:16] = jnp.full((4, out_ref.shape[1]), coef_ref[1], F32)


SMEM = functools.partial(pl.BlockSpec, memory_space=pltpu.SMEM)
LIMIT = 40 * 1024 * 1024


def whole(*shape):
    return pl.BlockSpec(shape, lambda *_: (0,) * len(shape))


def conv_call(kernel, operands, specs, rows_in, rows_out, extra, name):
    weights = pl.BlockSpec((1, 3, 320, 320), lambda r: (r, 0, 0, 0))
    flops = 2 * rows_out * 64 * 2880 * 320
    return pl.pallas_call(
        kernel,
        grid=(3,),
        in_specs=[*specs, weights],
        out_specs=[whole(rows_out * 64, 320), whole(8, 2, 320)],
        out_shape=[
            jax.ShapeDtypeStruct((rows_out * 64, 320), F32),
            jax.ShapeDtypeStruct((8, 2, 320), F32),
        ],
        scratch_shapes=[
            pltpu.VMEM((rows_in * 64, 960), BF16),
            pltpu.VMEM((960, 960), BF16),
            pltpu.VMEM((rows_out * 64 + 16, 960), F32),
            *extra,
        ],
        compiler_params=pltpu.CompilerParams(
            dimension_semantics=("arbitrary",), vmem_limit_bytes=LIMIT
        ),
        cost_estimate=pl.CostEstimate(
            flops=3 * flops, bytes_accessed=4_000_000, transcendentals=rows_in * 64 * 320
        ),
        name=name,
    )(*operands)


def gather_bands(piece):
    size = lax.axis_size("band")
    return lax.all_to_all(
        jnp.broadcast_to(piece[None], (size, *piece.shape)), "band", 0, 0, tiled=True
    )


def on_device(latents, timesteps, fresh, w_in, conv_first, conv_second, w_time, temporal, w_out):
    bands = lax.axis_size("band")
    levels = lax.axis_size("level")
    positions = latents.shape[2] * latents.shape[3]
    frame_positions = float(positions * bands)
    level = lax.axis_index("level")
    band = lax.axis_index("band").astype(jnp.int32).reshape(1)

    own = latents[0].reshape(4, positions)
    frame = gather_bands(own)

    plan = jnp.asarray(noise_plan())
    step = timesteps[0]
    now = lax.dynamic_index_in_dim(plan, step, keepdims=False)
    prev = lax.dynamic_index_in_dim(plan, step - STRIDE, keepdims=False)
    ratio = jnp.sqrt(prev) / jnp.sqrt(now)
    coef = jnp.stack([ratio, jnp.sqrt(1.0 - prev) - ratio * jnp.sqrt(1.0 - now)])
    embedded = time_embed(timesteps, w_time)
    folded = jnp.einsum("kcd,dj->kjc", temporal, w_out, precision=HIGHEST)
    folded = jnp.concatenate([folded[1], folded[0], folded[2], jnp.zeros_like(folded[0])], axis=0)
    out_rows = jnp.concatenate([w_out.T, jnp.zeros_like(w_out.T)], axis=0)

    for iteration in range(ITERS):
        middle, stats = conv_call(
            functools.partial(conv1_kernel, frame_positions),
            (band, frame, w_in, embedded, conv_first),
            [SMEM(), whole(8, 4, 320), whole(4, 320), whole(1, 320)],
            9, 7, [pltpu.VMEM((576, 320), F32)], "conv_one",
        )
        sums = lax.all_to_all(stats, "band", 0, 0, tiled=True)
        hidden, stats = conv_call(
            functools.partial(conv2_kernel, frame_positions),
            (band, middle, sums, own, w_in, conv_second),
            [SMEM(), whole(448, 320), whole(8, 2, 320), whole(4, 320), whole(4, 320)],
            7, 5, [], "conv_two",
        )
        sums = lax.all_to_all(stats, "band", 0, 0, tiled=True)
        parts = pl.pallas_call(
            functools.partial(project_kernel, frame_positions),
            in_specs=[SMEM()] + [pl.BlockSpec(memory_space=pltpu.VMEM)] * 5,
            out_specs=pl.BlockSpec(memory_space=pltpu.VMEM),
            out_shape=jax.ShapeDtypeStruct((16, positions), F32),
            compiler_params=pltpu.CompilerParams(vmem_limit_bytes=LIMIT),
            name="project",
        )(coef, hidden, sums, own, out_rows, folded)
        if iteration + 1 < ITERS:
            inside = [(i, i + 1) for i in range(0, levels, 2)]
            across = [(i, i + 2) for i in range(1, levels - 2, 2)]
            back = [(i + 1, i) for i in range(0, levels, 2)]
            from_zero = lax.ppermute(parts, "level", inside)
            over = jnp.concatenate([parts[0:8], parts[12:16], from_zero[4:8]], axis=0)
            from_chip = lax.ppermute(over, "level", across)
            handed = lax.ppermute(
                jnp.concatenate([from_chip[0:4], from_chip[8:16]], axis=0), "level", back
            )
            odd = level % 2 == 1
            update = jnp.where(odd, from_zero[0:4], handed[0:4])
            noise = jnp.where(odd, from_zero[12:16], handed[4:8])
            below = jnp.where(odd, from_chip[4:8], handed[8:12])
            moved = update + noise * (below + parts[8:12])
            own = jnp.where(level == 0, fresh[iteration].reshape(4, positions), moved)
            frame = gather_bands(own)
        else:
            up = [(i, i + 1) for i in range(levels - 1)]
            down = [(j, i) for i, j in up]
            below = lax.ppermute(parts[4:8], "level", up)
            above = lax.ppermute(parts[8:12], "level", down)
            own = parts[0:4] + parts[12:16] * (below + above)
    return own.reshape(latents.shape)


def solution(mesh):
    placed = (
        P("level", None, "band", None),
        P("level"),
        P(None, None, "band", None),
        P(),
        P(),
        P(),
        P(),
        P(),
        P(),
    )
    return jax.shard_map(
        on_device,
        mesh=mesh,
        in_specs=placed,
        out_specs=P("level", None, "band", None),
        check_vma=False,
    )
```

time: 206 us -> 140 us (0.68)
  the two profiles are of different devices: /device:TPU:97 before, /device:TPU:8 now
where the time goes in v1:
time: 140 us; the launch traced here: 139 us
  Pallas kernels  38.4 us (27%)
  blocking collectives  30.3 us (22%)
  waiting for transfers between devices  27.1 us (19%)
  starting transfers between devices  24.1 us (17%)
  local copies, waits for them, and re-layouts  12.9 us (9%)
  between operations  3.7 us (3%)
  matrix products  2.58 us (2%)
    pallas_call x4, Pallas kernels, conv_call(): pl.pallas_call(kernel, grid=(3,), in_specs=[*specs, weights], out_specs=[...  36.2 us
    all_to_all x2, blocking collectives, on_device(): sums = lax.all_to_all(stats, 'band', 0, 0, tiled=True)  20.2 us
    all_to_all x2, waiting for transfers between devices, on_device(): sums = lax.all_to_all(stats, 'band', 0, 0, tiled=True)  11 us
    all_to_all x1, blocking collectives, gather_bands(): lax.all_to_all(jnp.broadcast_to(piece[None], (size, *piece.shape)), 'band...  10.1 us
    unnamed x20, local copies, waits for them, and re-layouts  9.89 us
    ppermute x1, waiting for transfers between devices, on_device(): lax.ppermute(jnp.concatenate([from_chip[0:4], from_chip[8:16]], axis=0),...  9.68 us
    all_to_all x2, starting transfers between devices, on_device(): sums = lax.all_to_all(stats, 'band', 0, 0, tiled=True)  7.14 us
    all_to_all x1, starting transfers between devices, gather_bands(): lax.all_to_all(jnp.broadcast_to(piece[None], (size, *piece.shape)), 'band...  6.03 us
  transfers between devices with their start and end apart: 8, of which 6 were waited for; matrix products, arithmetic and copies ran while one was open for 3% of the time, Pallas kernels for 0%

profile of v1, /device:TPU:8, one launch (start us, length us, event | category | flops | bytes accessed | tf_op | source)
XLA Modules:
  0.0 139.3 jit_solution(7252988730302719395)
XLA Ops:
  0.0 0.8 copy.15
  0.9 0.6 broadcast_in_dim.7
  1.6 6.0 %all-to-all-start = ((f32[8,4,320]{2,1,0:T(4,128)}), f32[8,4,320]{2,1,0:T(4,128)S(1)}, u32[]{:S(2)}, u32[]{:S(2)}) async-start(f32[8,4,320]{2,1,0:T(4,128)} %broadcast_in_dim.7), calls=%async_computation | async-start | bytes 98304 | tf_op jit(solution)/shard_map/all_to_all | solution.py:310
  8.3 2.2 %convolution_bitcast_fusion = f32[3,4,320]{2,1,0:T(4,128)S(1)} fusion(f32[3,320,320]{2,1,0:T(8,128)S(1)} %copy-done, f32[320,4]{0,1:T(4,128)} %param.18), kind=kOutput, calls=%fused_computation | convolution fusion | flops 14745600 | bytes 1249280 | tf_op jit(solution)/shard_map/kcd,dj->kjc/dot_general | solution.py:333
  11.0 4.3 %all-to-all-done.frame_ref = f32[8,4,320]{2,1,0:T(4,128)S(1)} async-done(((f32[8,4,320]{2,1,0:T(4,128)}), f32[8,4,320]{2,1,0:T(4,128)S(1)}, u32[]{:S(2)}, u32[]{:S(2)}) %all-to-all-start) | async-done | bytes 40992 | tf_op jit(solution)/shard_map/all_to_all | solution.py:310
  15.3 2.3 %copy-done.1 = f32[3,3,320,320]{3,2,1,0:T(8,128)S(1)} copy-done((f32[3,3,320,320]{3,2,1,0:T(8,128)S(1)}, f32[3,3,320,320]{3,2,1,0:T(8,128)}, u32[]{:S(2)}) %copy-start.1) | copy-done | bytes 3686424
  17.6 10.3 %conv_one.2 = (f32[448,320]{1,0:T(8,128)S(1)}, f32[8,2,320]{2,1,0:T(2,128)}) custom-call(s32[1]{0:T(128)} %bitcast.1.band_ref, f32[8,4,320]{2,1,0:T(4,128)S(1)} %all-to-all-done.frame_ref, f32[4,320]{1,0:T(4,128)S(1)} %copy-done.5, f32[1,320]{1,0:T(1,128)S(1)} %mul.47.emb_ref, f32[3,3,320,320]{3,2,1,0:T(8,128)S(1)} %copy-done.1), custom_call_target="tpu_custom_call" | custom-call | flops 2477260800 | bytes 4000000 | tf_op jit(solution)/shard_map/conv_one/pallas_call | solution.py:283
  27.9 3.3 %all-to-all-start.1 = ((f32[8,2,320]{2,1,0:T(2,128)}), f32[8,2,320]{2,1,0:T(2,128)S(1)}, u32[]{:S(2)}, u32[]{:S(2)}) async-start(f32[8,2,320]{2,1,0:T(2,128)} %get-tuple-element.14), calls=%async_computation.1 | async-start | bytes 49152 | tf_op jit(solution)/shard_map/all_to_all | solution.py:344
  31.4 1.4 %fusion.11 = (f32[1]{0:T(128)}, f32[1]{0:T(128)}) fusion(f32[1000]{0:T(1024)} %constant.53.clone, s32[]{:T(128)S(6)} %select_n.37, s32[]{:T(128)S(6)} %select_n.36), kind=kLoop, calls=%fused_computation.28 | loop fusion | bytes 24 | tf_op jit(solution)/shard_map/jit(dynamic_index_in_dim)/dynamic_slice | solution.py:328
  35.6 3.3 %all-to-all-done.1.sums_ref = f32[8,2,320]{2,1,0:T(2,128)S(1)} async-done(((f32[8,2,320]{2,1,0:T(2,128)}), f32[8,2,320]{2,1,0:T(2,128)S(1)}, u32[]{:S(2)}, u32[]{:S(2)}) %all-to-all-start.1) | async-done | bytes 20512 | tf_op jit(solution)/shard_map/all_to_all | solution.py:344
  38.9 2.3 %copy-done.3 = f32[3,3,320,320]{3,2,1,0:T(8,128)S(1)} copy-done((f32[3,3,320,320]{3,2,1,0:T(8,128)S(1)}, f32[3,3,320,320]{3,2,1,0:T(8,128)}, u32[]{:S(2)}) %copy-start.3) | copy-done | bytes 3686424
  41.2 8.3 %conv_two.2 = (f32[320,320]{1,0:T(8,128)S(1)}, f32[8,2,320]{2,1,0:T(2,128)}) custom-call(s32[1]{0:T(128)} %bitcast.1.band_ref, f32[448,320]{1,0:T(8,128)S(1)} %get-tuple-element.13.mid_ref, f32[8,2,320]{2,1,0:T(2,128)S(1)} %all-to-all-done.1.sums_ref, f32[4,320]{1,0:T(4,128)S(1)} %broadcast_in_dim.6.own_ref, f32[4,320]{1,0:T(4,128)S(1)} %copy-done.5, ...), custom_call_target="tpu_custom_call" | custom-call | flops 1769472000 | bytes 4000000 | tf_op jit(solution)/shard_map/conv_two/pallas_call | solution.py:283
  49.5 3.8 %all-to-all-start.2 = ((f32[8,2,320]{2,1,0:T(2,128)}), f32[8,2,320]{2,1,0:T(2,128)S(1)}, u32[]{:S(2)}, u32[]{:S(2)}) async-start(f32[8,2,320]{2,1,0:T(2,128)} %get-tuple-element.16), calls=%async_computation.2 | async-start | bytes 49152 | tf_op jit(solution)/shard_map/all_to_all | solution.py:351
  53.4 7.6 %all-to-all-done.2.sums_ref = f32[8,2,320]{2,1,0:T(2,128)S(1)} async-done(((f32[8,2,320]{2,1,0:T(2,128)}), f32[8,2,320]{2,1,0:T(2,128)S(1)}, u32[]{:S(2)}, u32[]{:S(2)}) %all-to-all-start.2) | async-done | bytes 20512 | tf_op jit(solution)/shard_map/all_to_all | solution.py:351
  61.0 1.1 project.2
  62.1 1.3 collective-permute-start
  63.5 0.8 collective-permute-done
  64.3 0.7 collective-permute-start.1
  65.0 1.3 collective-permute-start.2
  66.4 9.7 %collective-permute-done.2 = f32[12,320]{1,0:T(8,128)S(1)} collective-permute-done((f32[12,320]{1,0:T(8,128)S(1)}, f32[12,320]{1,0:T(8,128)S(1)}, u32[]{:S(2)}, u32[]{:S(2)}) %collective-permute-start.2) | collective-permute-done | bytes 15392 | tf_op jit(solution)/shard_map/ppermute | solution.py:367
  76.1 10.1 %all_to_all.30.frame_ref = f32[8,4,320]{2,1,0:T(4,128)S(1)} all-to-all(f32[8,4,320]{2,1,0:T(4,128)S(1)} %broadcast_in_dim.8), channel_id=1, replica_groups=mesh['level'=32,'band'=8] {'band'}, dimensions={0} | all-to-all | bytes 81920 | tf_op jit(solution)/shard_map/all_to_all | solution.py:310
  86.2 2.3 %copy-done.2 = f32[3,3,320,320]{3,2,1,0:T(8,128)S(1)} copy-done((f32[3,3,320,320]{3,2,1,0:T(8,128)S(1)}, f32[3,3,320,320]{3,2,1,0:T(8,128)}, u32[]{:S(2)}) %copy-start.2) | copy-done | bytes 3686424
  88.5 9.8 %conv_one.3 = (f32[448,320]{1,0:T(8,128)S(1)}, f32[8,2,320]{2,1,0:T(2,128)S(1)}) custom-call(s32[1]{0:T(128)} %bitcast.1.band_ref, f32[8,4,320]{2,1,0:T(4,128)S(1)} %all_to_all.30.frame_ref, f32[4,320]{1,0:T(4,128)S(1)} %copy-done.5, f32[1,320]{1,0:T(1,128)S(1)} %mul.47.emb_ref, f32[3,3,320,320]{3,2,1,0:T(8,128)S(1)} %copy-done.2), custom_call_target="tpu_custom_call" | custom-call | flops 2477260800 | bytes 4000000 | tf_op jit(solution)/shard_map/conv_one/pallas_call | solution.py:283
  98.3 10.1 %all_to_all.31.sums_ref = f32[8,2,320]{2,1,0:T(2,128)S(1)} all-to-all(f32[8,2,320]{2,1,0:T(2,128)S(1)} %get-tuple-element.18), channel_id=1, replica_groups=mesh['level'=32,'band'=8] {'band'}, dimensions={0} | all-to-all | bytes 40960 | tf_op jit(solution)/shard_map/all_to_all | solution.py:344
  108.4 2.3 %copy-done.4 = f32[3,3,320,320]{3,2,1,0:T(8,128)S(1)} copy-done((f32[3,3,320,320]{3,2,1,0:T(8,128)S(1)}, f32[3,3,320,320]{3,2,1,0:T(8,128)}, u32[]{:S(2)}) %copy-start.4) | copy-done | bytes 3686424
  110.6 7.8 %conv_two.3 = (f32[320,320]{1,0:T(8,128)S(1)}, f32[8,2,320]{2,1,0:T(2,128)S(1)}) custom-call(s32[1]{0:T(128)} %bitcast.1.band_ref, f32[448,320]{1,0:T(8,128)S(1)} %get-tuple-element.17.mid_ref, f32[8,2,320]{2,1,0:T(2,128)S(1)} %all_to_all.31.sums_ref, f32[4,320]{1,0:T(4,128)S(1)} %fusion.3.own_ref, f32[4,320]{1,0:T(4,128)S(1)} %copy-done.5, ...), custom_call_target="tpu_custom_call" | custom-call | flops 1769472000 | bytes 4000000 | tf_op jit(solution)/shard_map/conv_two/pallas_call | solution.py:283
  118.4 10.1 %all_to_all.32.sums_ref = f32[8,2,320]{2,1,0:T(2,128)S(1)} all-to-all(f32[8,2,320]{2,1,0:T(2,128)S(1)} %get-tuple-element.20), channel_id=1, replica_groups=mesh['level'=32,'band'=8] {'band'}, dimensions={0} | all-to-all | bytes 40960 | tf_op jit(solution)/shard_map/all_to_all | solution.py:351
  128.5 1.1 project.3
  129.6 1.9 %collective-permute-start.3 = (f32[4,320]{1,0:T(4,128)S(1)}, f32[4,320]{1,0:T(4,128)S(1)}, u32[]{:S(2)}, u32[]{:S(2)}) collective-permute-start(f32[4,320]{1,0:T(4,128)S(1)} %get-tuple-element.22), channel_id=1, source_target_pairs={{0,8},{8,16},{16,24},{24,32},{32,40},{40,48},{48,56},{56,64},{64,7... | collective-permute-start | bytes 15368 | tf_op jit(solution)/shard_map/ppermute | solution.py:380
  131.5 5.8 %collective-permute-start.4 = (f32[4,320]{1,0:T(4,128)S(1)}, f32[4,320]{1,0:T(4,128)S(1)}, u32[]{:S(2)}, u32[]{:S(2)}) collective-permute-start(f32[4,320]{1,0:T(4,128)S(1)} %get-tuple-element.21), channel_id=1, source_target_pairs={{8,0},{16,8},{24,16},{32,24},{40,32},{48,40},{56,48},{64,56},{72,6... | collective-permute-start | bytes 15368 | tf_op jit(solution)/shard_map/ppermute | solution.py:381
  137.3 1.3 collective-permute-done.4
  138.7 0.6 copy.16
  (41 shorter events, 1.1 us)
Async XLA Ops:
  0.0 8.3 %copy-start = (f32[3,320,320]{2,1,0:T(8,128)S(1)}, f32[3,320,320]{2,1,0:T(8,128)}, u32[]{:S(2)}) copy-start(f32[3,320,320]{2,1,0:T(8,128)} %param.17) | copy-start | bytes 3686404
  0.0 10.5 %copy-start.6 = (f32[320,320]{1,0:T(8,128)S(1)}, f32[320,320]{1,0:T(8,128)}, u32[]{:S(2)}) copy-start(f32[320,320]{1,0:T(8,128)} %param.16) | copy-start | bytes 1228804
  0.0 15.3 %copy-start.5 = (f32[4,320]{1,0:T(4,128)S(1)}, f32[4,320]{1,0:T(4,128)}, u32[]{:S(2)}) copy-start(f32[4,320]{1,0:T(4,128)} %w_in_ref.7) | copy-start | bytes 15364
  1.6 13.8 %all-to-all-start = ((f32[8,4,320]{2,1,0:T(4,128)}), f32[8,4,320]{2,1,0:T(4,128)S(1)}, u32[]{:S(2)}, u32[]{:S(2)}) async-start(f32[8,4,320]{2,1,0:T(4,128)} %broadcast_in_dim.7), calls=%async_computation | async-start | bytes 98304 | tf_op jit(solution)/shard_map/all_to_all | solution.py:310
  15.3 2.3 %copy-start.1 = (f32[3,3,320,320]{3,2,1,0:T(8,128)S(1)}, f32[3,3,320,320]{3,2,1,0:T(8,128)}, u32[]{:S(2)}) copy-start(f32[3,3,320,320]{3,2,1,0:T(8,128)} %w_ref.6) | copy-start | bytes 11059204
  27.9 11.0 %all-to-all-start.1 = ((f32[8,2,320]{2,1,0:T(2,128)}), f32[8,2,320]{2,1,0:T(2,128)S(1)}, u32[]{:S(2)}, u32[]{:S(2)}) async-start(f32[8,2,320]{2,1,0:T(2,128)} %get-tuple-element.14), calls=%async_computation.1 | async-start | bytes 49152 | tf_op jit(solution)/shard_map/all_to_all | solution.py:344
  38.9 2.3 %copy-start.3 = (f32[3,3,320,320]{3,2,1,0:T(8,128)S(1)}, f32[3,3,320,320]{3,2,1,0:T(8,128)}, u32[]{:S(2)}) copy-start(f32[3,3,320,320]{3,2,1,0:T(8,128)} %w_ref.7) | copy-start | bytes 11059204
  41.2 12.2 %copy-start.7 = (f32[320,4]{0,1:T(4,128)S(1)}, f32[320,4]{0,1:T(4,128)}, u32[]{:S(2)}) copy-start(f32[320,4]{0,1:T(4,128)} %param.18) | copy-start | bytes 15364
  41.2 25.2 %copy-start.8 = (f32[1,4,5,64]{3,1,2,0:T(4,128)S(1)}, f32[1,4,5,64]{3,1,2,0:T(4,128)}, u32[]{:S(2)}) copy-start(f32[1,4,5,64]{3,1,2,0:T(4,128)} %param.12) | copy-start | bytes 15364
  49.5 11.5 %all-to-all-start.2 = ((f32[8,2,320]{2,1,0:T(2,128)}), f32[8,2,320]{2,1,0:T(2,128)S(1)}, u32[]{:S(2)}, u32[]{:S(2)}) async-start(f32[8,2,320]{2,1,0:T(2,128)} %get-tuple-element.16), calls=%async_computation.2 | async-start | bytes 49152 | tf_op jit(solution)/shard_map/all_to_all | solution.py:351
  62.1 2.1 %collective-permute-start = (f32[16,320]{1,0:T(8,128)S(1)}, f32[16,320]{1,0:T(8,128)S(1)}, u32[]{:S(2)}, u32[]{:S(2)}) collective-permute-start(f32[16,320]{1,0:T(8,128)S(1)} %project.2), channel_id=1, source_target_pairs={{0,8},{16,24},{32,40},{48,56},{64,72},{80,88},{96,104},{112,120},{... | collective-permute-start | bytes 61448 | tf_op jit(solution)/shard_map/ppermute | solution.py:364
  64.3 0.7 collective-permute-start.1
  65.0 11.1 %collective-permute-start.2 = (f32[12,320]{1,0:T(8,128)S(1)}, f32[12,320]{1,0:T(8,128)S(1)}, u32[]{:S(2)}, u32[]{:S(2)}) collective-permute-start(f32[12,320]{1,0:T(8,128)S(1)} %pad_maximum_fusion.1), channel_id=1, source_target_pairs={{8,0},{24,16},{40,32},{56,48},{72,64},{88,80},{104,96},{120,112},{... | collective-permute-start | bytes 46088 | tf_op jit(solution)/shard_map/ppermute | solution.py:367
  86.2 2.3 %copy-start.2 = (f32[3,3,320,320]{3,2,1,0:T(8,128)S(1)}, f32[3,3,320,320]{3,2,1,0:T(8,128)}, u32[]{:S(2)}) copy-start(f32[3,3,320,320]{3,2,1,0:T(8,128)} %w_ref.6) | copy-start | bytes 11059204
  108.4 2.3 %copy-start.4 = (f32[3,3,320,320]{3,2,1,0:T(8,128)S(1)}, f32[3,3,320,320]{3,2,1,0:T(8,128)}, u32[]{:S(2)}) copy-start(f32[3,3,320,320]{3,2,1,0:T(8,128)} %w_ref.7) | copy-start | bytes 11059204
  129.6 7.7 %collective-permute-start.3 = (f32[4,320]{1,0:T(4,128)S(1)}, f32[4,320]{1,0:T(4,128)S(1)}, u32[]{:S(2)}, u32[]{:S(2)}) collective-permute-start(f32[4,320]{1,0:T(4,128)S(1)} %get-tuple-element.22), channel_id=1, source_target_pairs={{0,8},{8,16},{16,24},{24,32},{32,40},{40,48},{48,56},{56,64},{64,7... | collective-permute-start | bytes 15368 | tf_op jit(solution)/shard_map/ppermute | solution.py:380
  131.5 7.1 %collective-permute-start.4 = (f32[4,320]{1,0:T(4,128)S(1)}, f32[4,320]{1,0:T(4,128)S(1)}, u32[]{:S(2)}, u32[]{:S(2)}) collective-permute-start(f32[4,320]{1,0:T(4,128)S(1)} %get-tuple-element.21), channel_id=1, source_target_pairs={{8,0},{16,8},{24,16},{32,24},{40,32},{48,40},{56,48},{64,56},{72,6... | collective-permute-start | bytes 15368 | tf_op jit(solution)/shard_map/ppermute | solution.py:381

commit v2 on v1

v2 whole, which is shorter than its diff:
```python
import functools
import math

import jax
import jax.numpy as jnp
import numpy as np
from jax import lax
from jax.experimental import pallas as pl
from jax.experimental.pallas import tpu as pltpu
from jax.sharding import PartitionSpec as P

GROUPS = 32
ITERS = 2
NSTEPS = 1000
STRIDE = 16

EPSILON = 1e-05
HIGHEST = lax.Precision.HIGHEST
BF16 = jnp.bfloat16
F32 = jnp.float32


def noise_plan():
    position = np.arange(NSTEPS, dtype=np.float64)
    root_beta = math.sqrt(0.00085) + position / (NSTEPS - 1) * (
        math.sqrt(0.012) - math.sqrt(0.00085)
    )
    return np.cumprod(1.0 - root_beta * root_beta).astype(np.float32)


def harmonics(step_ids, width):
    half_width = width // 2
    frequency = jnp.exp(-math.log(10000.0) * jnp.arange(half_width, dtype=F32) / half_width)
    angles = step_ids.astype(F32)[:, None] * frequency[None, :]
    return jnp.concatenate([jnp.cos(angles), jnp.sin(angles)], axis=1)


def halves(v):
    hi = v.astype(BF16)
    return hi, (v - hi.astype(F32)).astype(BF16)


def thirds(v):
    one = v.astype(BF16).astype(F32)
    two = (v - one).astype(BF16).astype(F32)
    three = ((v - one) - two).astype(BF16).astype(F32)
    return one, two, three


def silu(v):
    return v / (1.0 + jnp.exp(-v))


def group_mean(rows):
    channels = rows.shape[1]
    per_group = channels // GROUPS
    one, two, three = thirds(rows)
    stacked = jnp.concatenate([one, two, three, one * 0.0], axis=0).astype(BF16)
    shape = (channels, channels)
    factor = (1 << 16) // per_group + 1
    here = (lax.broadcasted_iota(jnp.int32, shape, 0) * factor) >> 16
    there = (lax.broadcasted_iota(jnp.int32, shape, 1) * factor) >> 16
    member = jnp.where(here == there, 1.0, 0.0).astype(BF16)
    total = jnp.dot(stacked, member, preferred_element_type=F32)
    return (total[0:2] + total[2:4] + total[4:6]) * (1.0 / per_group)


def center_factor(means):
    grouped = group_mean(means)
    center = grouped[0:1]
    return center, lax.rsqrt(grouped[1:2] - center * center + EPSILON)


def lift(frame, w):
    f1, f2, f3 = thirds(frame)
    w1, w2, w3 = thirds(w)
    left = jnp.concatenate([f1, f1, f2, f1, f2, f3], axis=0).astype(BF16)
    right = jnp.concatenate([w1, w2, w1, w3, w2, w1], axis=0).astype(BF16)
    return lax.dot_general(left, right, (((0,), (0,)), ((), ())), preferred_element_type=F32)


def put_left(a_ref, rows, act):
    hi, lo = halves(act)
    a_ref[rows, 0:256] = hi[:, 0:256]
    a_ref[rows, 256:512] = lo[:, 0:256]
    a_ref[rows, 512:768] = hi[:, 0:256]
    a_ref[rows, 768:896] = jnp.concatenate([hi[:, 256:320], lo[:, 256:320]], axis=1)
    a_ref[rows, 896:1024] = jnp.concatenate([hi[:, 256:320], hi[:, 256:320] * 0.0], axis=1)


def put_right(b_ref, tap, w_ref):
    for k in range(5):
        hi, lo = zip(*[halves(w_ref[c, 64 * k : 64 * k + 64, :]) for c in range(3)])
        if k < 4:
            places = ((64 * k, hi), (256 + 64 * k, hi), (512 + 64 * k, lo))
        else:
            places = ((768, hi), (832, hi), (896, lo))
        for at, part in places:
            for c in range(3):
                b_ref[tap, at : at + 64, 256 * c : 256 * c + 256] = part[c][:, 0:256]
            b_ref[tap, at : at + 64, 768:896] = jnp.concatenate(
                [part[0][:, 256:320], part[1][:, 256:320]], axis=1
            )
            b_ref[tap, at : at + 64, 896:960] = part[2][:, 256:320]
    b_ref[tap, 960:1024, :] = jnp.zeros((64, 960), BF16)


def product(left, right, dims):
    l_hi, l_lo = halves(left)
    r_hi, r_lo = halves(right)
    n = left.shape[0]
    both = lax.dot_general(
        jnp.concatenate([l_hi, l_lo], axis=0), r_hi, (dims, ((), ())), preferred_element_type=F32
    )
    rest = lax.dot_general(l_hi, r_lo, (dims, ((), ())), preferred_element_type=F32)
    return both[0:n] + both[n:] + rest


def spread_kernel(
    steps_ref, latents_ref, harmonic_ref, spread_ref, own_ref, step_ref
):
    own = jnp.concatenate([latents_ref[0, r] for r in range(5)], axis=1)
    own_ref[...] = own
    spread_ref[...] = jnp.broadcast_to(own[None], spread_ref.shape)
    step_ref[...] = jnp.full(step_ref.shape, steps_ref[0].astype(F32), F32)


def setup_kernel(
    after_ref, step_ref, plan_ref, fresh_ref, harmonic_ref, w_out_ref, time_ref, temporal_ref,
    one_ref, two_ref, new_ref, coef_ref, emb_ref, fold_ref, first_ref, second_ref,
):
    new_ref[...] = jnp.concatenate([fresh_ref[0, r] for r in range(5)], axis=1)
    step = step_ref[...].astype(jnp.int32)
    plan = plan_ref[...]
    place = lax.broadcasted_iota(jnp.int32, plan.shape, 0) * 128 + lax.broadcasted_iota(
        jnp.int32, plan.shape, 1
    )

    def at(i):
        return jnp.sum(
            jnp.sum(jnp.where(place == i, plan, 0.0), axis=0, keepdims=True), axis=1, keepdims=True
        )

    now = at(step)
    prev = at(step - STRIDE)
    ratio = jnp.sqrt(prev) / jnp.sqrt(now)
    noise = jnp.sqrt(1.0 - prev) - ratio * jnp.sqrt(1.0 - now)
    coef_ref[0:1] = jnp.broadcast_to(ratio, (1, 128))
    coef_ref[1:2] = jnp.broadcast_to(noise, (1, 128))
    for raw, ref in ((one_ref, first_ref), (two_ref, second_ref)):
        for r in range(3):
            put_right(ref, r, raw.at[r])
    harmonic = jnp.broadcast_to(harmonic_ref[...], (8, 320))
    emb_ref[...] = silu(product(harmonic, time_ref[...], ((1,), (0,)))[0:1])
    w_out = jnp.concatenate([w_out_ref[...], w_out_ref[...] * 0.0], axis=0)
    for row, tap in enumerate((1, 0, 2)):
        fold = product(w_out, temporal_ref[tap], ((1,), (1,)))
        fold_ref[4 * row : 4 * row + 4] = fold[0:4]
    fold_ref[12:16] = jnp.zeros((4, 320), F32)


def setup(*operands):
    shapes = (
        ((4, 320), F32), ((2, 128), F32), ((1, 320), F32), ((16, 320), F32),
        ((3, 1024, 960), BF16), ((3, 1024, 960), BF16),
    )
    return pl.pallas_call(
        setup_kernel,
        in_specs=[ANY] + [VMEM] * (len(operands) - 1),
        out_specs=[VMEM] * len(shapes),
        out_shape=[jax.ShapeDtypeStruct(*shape) for shape in shapes],
        compiler_params=pltpu.CompilerParams(vmem_limit_bytes=LIMIT),
        cost_estimate=pl.CostEstimate(flops=0, bytes_accessed=20_000_000, transcendentals=0),
        name="setup",
    )(*operands)


def multiply(acc_ref, a_ref, b_ref, count):
    left = jnp.concatenate([a_ref[64 * tap : 64 * tap + count, :] for tap in range(3)], axis=1)
    for lo, hi in ((0, 256), (256, 512), (512, 768), (768, 960)):
        right = jnp.concatenate([b_ref[tap, :, lo:hi] for tap in range(3)], axis=0)
        acc_ref[8 : 8 + count, lo:hi] = jnp.dot(left, right, preferred_element_type=F32)


def shifted_sum(acc_ref, row):
    base = 8 + 64 * row
    column = lax.broadcasted_iota(jnp.int32, (64, 1), 0)
    first = column > 0
    last = column < 63
    main = (
        jnp.where(first, acc_ref[base - 1 : base + 63, 0:256], 0.0)
        + acc_ref[base : base + 64, 256:512]
        + jnp.where(last, acc_ref[base + 1 : base + 65, 512:768], 0.0)
    )
    rest = (
        jnp.where(first, acc_ref[base - 1 : base + 63, 768:832], 0.0)
        + acc_ref[base : base + 64, 832:896]
        + jnp.where(last, acc_ref[base + 1 : base + 65, 896:960], 0.0)
    )
    return jnp.concatenate([main, rest], axis=1)


def conv1_kernel(
    members, frame_ref, w_in_ref, emb_ref, w_ref, mid_ref, stat_ref, a_ref, acc_ref,
    lift_ref,
):
    band = lax.axis_index("band")
    bands = frame_ref.shape[0]

    frame = frame_ref[...]
    w = w_in_ref[...]
    average = 1.0 / members
    mean = jnp.sum(jnp.sum(frame, axis=0), axis=1, keepdims=True) * average
    mean = jnp.sum(mean * w, axis=0, keepdims=True)
    square = jnp.zeros_like(mean)
    for j in range(4):
        moment = jnp.sum(frame * frame[:, j : j + 1, :], axis=0)
        moment = jnp.sum(moment, axis=1, keepdims=True) * average
        square += w[j : j + 1] * jnp.sum(moment * w, axis=0, keepdims=True)
    center, factor = center_factor(jnp.concatenate([mean, square], axis=0))
    before = frame_ref[jnp.maximum(band - 1, 0)]
    after = frame_ref[jnp.minimum(band + 1, bands - 1)]
    around = jnp.concatenate(
        [before[:, 192:320], frame_ref[band], after[:, 0:128]], axis=1
    )
    lift_ref[...] = lift(around, w)
    for i in range(9):
        rows = slice(64 * i, 64 * i + 64)
        act = silu((lift_ref[rows, :] - center) * factor)
        if i < 2:
            act = act * jnp.where(band > 0, 1.0, 0.0)
        elif i >= 7:
            act = act * jnp.where(band < bands - 1, 1.0, 0.0)
        put_left(a_ref, rows, act)

    multiply(acc_ref, a_ref, w_ref, 448)

    total = jnp.zeros((8, 320), F32)
    square = jnp.zeros((8, 320), F32)
    for i in range(7):
        out = shifted_sum(acc_ref, i) + emb_ref[...]
        mid_ref[64 * i : 64 * i + 64, :] = out
        if 1 <= i <= 5:
            folded = out.reshape(8, 8, 320)
            total += jnp.sum(folded, axis=0)
            square += jnp.sum(folded * folded, axis=0)
    stat_ref[...] = jnp.broadcast_to(
        jnp.concatenate(
            [jnp.sum(total, axis=0, keepdims=True), jnp.sum(square, axis=0, keepdims=True)],
            axis=0,
        )[None],
        stat_ref.shape,
    )


def conv2_kernel(
    members, mid_ref, sums_ref, own_ref, w_in_ref, w_ref, hid_ref, stat_ref, a_ref,
    acc_ref,
):
    band = lax.axis_index("band")
    bands = sums_ref.shape[0]

    center, factor = center_factor(jnp.sum(sums_ref[...], axis=0) * (1.0 / members))
    for i in range(7):
        rows = slice(64 * i, 64 * i + 64)
        act = silu((mid_ref[rows, :] - center) * factor)
        if i == 0:
            act = act * jnp.where(band > 0, 1.0, 0.0)
        elif i == 6:
            act = act * jnp.where(band < bands - 1, 1.0, 0.0)
        put_left(a_ref, rows, act)

    multiply(acc_ref, a_ref, w_ref, 320)

    total = jnp.zeros((8, 320), F32)
    square = jnp.zeros((8, 320), F32)
    hid_ref[...] = lift(own_ref[...], w_in_ref[...])
    for i in range(5):
        rows = slice(64 * i, 64 * i + 64)
        out = hid_ref[rows, :] + shifted_sum(acc_ref, i)
        hid_ref[rows, :] = out
        folded = out.reshape(8, 8, 320)
        total += jnp.sum(folded, axis=0)
        square += jnp.sum(folded * folded, axis=0)
    stat_ref[...] = jnp.broadcast_to(
        jnp.concatenate(
            [jnp.sum(total, axis=0, keepdims=True), jnp.sum(square, axis=0, keepdims=True)],
            axis=0,
        )[None],
        stat_ref.shape,
    )


def project_kernel(members, hid_ref, sums_ref, own_ref, w_out_ref, fold_ref, coef_ref, out_ref):
    center, factor = center_factor(jnp.sum(sums_ref[...], axis=0) * (1.0 / members))
    hidden = hid_ref[...]
    act = silu((hidden - center) * factor)
    w_out = jnp.concatenate([w_out_ref[...], w_out_ref[...] * 0.0], axis=0)
    from_hidden = product(w_out, hidden, ((1,), (1,)))
    from_act = product(fold_ref[...], act, ((1,), (1,)))
    local = from_hidden[0:4] + from_act[0:4]
    ratio = coef_ref[0:1, 0:1]
    noise = coef_ref[1:2, 0:1]
    out_ref[0:4] = ratio * own_ref[...] + noise * local
    out_ref[4:8] = from_act[4:8]
    out_ref[8:12] = from_act[8:12]
    out_ref[12:16] = jnp.broadcast_to(noise, (4, out_ref.shape[1]))


def merge_kernel(parts_ref, zero_ref, chip_ref, handed_ref, fresh_ref, own_ref, spread_ref):
    level = lax.axis_index("level")
    odd = jnp.where(level % 2 == 1, 1.0, 0.0)
    even = 1.0 - odd
    new = jnp.where(level == 0, 1.0, 0.0)
    update = odd * zero_ref[0:4] + even * handed_ref[0:4]
    noise = odd * zero_ref[12:16] + even * handed_ref[4:8]
    below = odd * chip_ref[4:8] + even * handed_ref[8:12]
    moved = update + noise * (below + parts_ref[8:12])
    own = new * fresh_ref[...] + (1.0 - new) * moved
    own_ref[...] = own
    spread_ref[...] = jnp.broadcast_to(own[None], spread_ref.shape)


def finish_kernel(parts_ref, below_ref, above_ref, out_ref):
    own = parts_ref[0:4] + parts_ref[12:16] * (below_ref[...] + above_ref[...])
    for r in range(5):
        out_ref[0, r] = own[:, 64 * r : 64 * r + 64]


SMEM = pl.BlockSpec(memory_space=pltpu.SMEM)
VMEM = pl.BlockSpec(memory_space=pltpu.VMEM)
ANY = pl.BlockSpec(memory_space=pl.ANY)
LIMIT = 20 * 1024 * 1024


def conv_call(kernel, operands, rows_in, rows_out, extra, name):
    return pl.pallas_call(
        kernel,
        in_specs=[VMEM] * len(operands),
        out_specs=[VMEM, VMEM],
        out_shape=[
            jax.ShapeDtypeStruct((rows_out * 64, 320), F32),
            jax.ShapeDtypeStruct((8, 2, 320), F32),
        ],
        scratch_shapes=[
            pltpu.VMEM((rows_in * 64, 1024), BF16),
            pltpu.VMEM((rows_out * 64 + 16, 960), F32),
            *extra,
        ],
        compiler_params=pltpu.CompilerParams(vmem_limit_bytes=LIMIT),
        cost_estimate=pl.CostEstimate(
            flops=6 * rows_out * 64 * 2880 * 320,
            bytes_accessed=4_000_000,
            transcendentals=rows_in * 64 * 320,
        ),
        name=name,
    )(*operands)


def call(kernel, in_specs, shapes, operands, name, cost=None):
    return pl.pallas_call(
        kernel,
        in_specs=in_specs,
        out_specs=[VMEM] * len(shapes),
        out_shape=[jax.ShapeDtypeStruct(shape, F32) for shape in shapes],
        compiler_params=pltpu.CompilerParams(vmem_limit_bytes=LIMIT),
        cost_estimate=cost,
        name=name,
    )(*operands)


def on_device(latents, timesteps, fresh, w_in, conv_first, conv_second, w_time, temporal, w_out):
    levels = lax.axis_size("level")
    positions = latents.shape[2] * latents.shape[3]
    members = float(positions * lax.axis_size("band"))
    out_rows = w_out.T
    harmonic = harmonics(timesteps, w_time.shape[0])
    plan = np.zeros((8, 128), np.float32)
    plan.reshape(-1)[:NSTEPS] = noise_plan()
    plan = jnp.asarray(plan)
    spread, own, step = call(
        spread_kernel, [SMEM, VMEM, ANY], [(8, 4, positions), (4, positions), (1, 128)],
        (timesteps, latents.transpose(0, 2, 1, 3), harmonic), "spread",
        pl.CostEstimate(flops=8_000_000_000, bytes_accessed=40_000, transcendentals=0),
    )
    for iteration in range(ITERS):
        frame = lax.all_to_all(spread, "band", 0, 0, tiled=True)
        if iteration == 0:
            new, coef, embedded, folded, first_ready, second_ready = setup(
                frame, step, plan, fresh.transpose(0, 2, 1, 3), harmonic, out_rows, w_time,
                temporal, conv_first, conv_second,
            )
        middle, stats = conv_call(
            functools.partial(conv1_kernel, members),
            (frame, w_in, embedded, first_ready),
            9, 7, [pltpu.VMEM((576, 320), F32)], "conv_one",
        )
        sums = lax.all_to_all(stats, "band", 0, 0, tiled=True)
        hidden, stats = conv_call(
            functools.partial(conv2_kernel, members),
            (middle, sums, own, w_in, second_ready),
            7, 5, [], "conv_two",
        )
        sums = lax.all_to_all(stats, "band", 0, 0, tiled=True)
        (parts,) = call(
            functools.partial(project_kernel, members), [VMEM] * 6, [(16, positions)],
            (hidden, sums, own, out_rows, folded, coef), "project",
        )
        if iteration + 1 < ITERS:
            inside = [(i, i + 1) for i in range(0, levels, 2)]
            across = [(i, i + 2) for i in range(1, levels - 2, 2)]
            back = [(i + 1, i) for i in range(0, levels, 2)]
            from_zero = lax.ppermute(parts, "level", inside)
            over = jnp.concatenate([parts[0:8], parts[12:16], from_zero[4:8]], axis=0)
            from_chip = lax.ppermute(over, "level", across)
            handed = lax.ppermute(
                jnp.concatenate([from_chip[0:4], from_chip[8:16]], axis=0), "level", back
            )
            own, spread = call(
                merge_kernel, [VMEM] * 5, [(4, positions), spread.shape],
                (parts, from_zero, from_chip, handed, new), "merge",
            )
        else:
            up = [(i, i + 1) for i in range(levels - 1)]
            down = [(j, i) for i, j in up]
            below = lax.ppermute(parts[4:8], "level", up)
            above = lax.ppermute(parts[8:12], "level", down)
            (out,) = call(
                finish_kernel, [VMEM] * 3, [(1, 5, 4, 64)], (parts, below, above), "finish"
            )
    return out.transpose(0, 2, 1, 3)


def solution(mesh):
    placed = (
        P("level", None, "band", None),
        P("level"),
        P(None, None, "band", None),
        P(),
        P(),
        P(),
        P(),
        P(),
        P(),
    )
    return jax.shard_map(
        on_device,
        mesh=mesh,
        in_specs=placed,
        out_specs=P("level", None, "band", None),
        check_vma=False,
    )
```

time: 140 us -> 107 us (0.76)
  blocking collectives: 30.3 us -> 64.4 us
  Pallas kernels: 38.4 us -> 17.4 us
  starting transfers between devices: 24.1 us -> 7.58 us
  local copies, waits for them, and re-layouts: 12.9 us -> 0.77 us
  waiting for transfers between devices: 27.1 us -> 15.2 us
  between operations: 3.7 us -> 0.88 us
  matrix products: 2.58 us -> 0 us
    pallas_call x6 -> x10, Pallas kernels: 38.4 us -> 17.4 us  [the longest x4 12.7 us: conv_call(): pl.pallas_call(kernel, in_specs=[VMEM] * len(operands), out_specs=[VMEM,...]
    all_to_all x2 -> x4, blocking collectives: 20.2 us -> 40.4 us  [on_device(): sums = lax.all_to_all(stats, 'band', 0, 0, tiled=True)]
    all_to_all x3 -> x0, waiting for transfers between devices: 15.3 us -> none  [the longest x2 11 us: on_device(): sums = lax.all_to_all(stats, 'band', 0, 0, tiled=True)]
    all_to_all x1 -> x2, blocking collectives: 10.1 us -> 23.9 us  [on_device(): frame = lax.all_to_all(spread, 'band', 0, 0, tiled=True)]
    all_to_all x3 -> x0, starting transfers between devices: 13.2 us -> none  [the longest x2 7.14 us: on_device(): sums = lax.all_to_all(stats, 'band', 0, 0, tiled=True)]
    unnamed x20 -> x18, local copies, waits for them, and re-layouts: 9.89 us -> 0.74 us
    ppermute x1, waiting for transfers between devices: 0.01 us -> 4.63 us  [on_device(): below = lax.ppermute(parts[4:8], 'level', up)]
    ppermute x1, starting transfers between devices: 5.75 us -> 1.92 us  [on_device(): above = lax.ppermute(parts[8:12], 'level', down)]
  transfers between devices with their start and end apart: 8 -> 5, of which waited for: 6 -> 3; matrix products, arithmetic and copies ran while one was open for 3% -> 0% of each run, Pallas kernels for 0% -> 0%
where the time goes in v2:
time: 107 us; the launch traced here: 106 us
  blocking collectives  64.4 us (60%)
  Pallas kernels  17.4 us (16%)
  waiting for transfers between devices  15.2 us (14%)
  starting transfers between devices  7.58 us (7%)
    all_to_all x4, blocking collectives, on_device(): sums = lax.all_to_all(stats, 'band', 0, 0, tiled=True)  40.4 us
    all_to_all x2, blocking collectives, on_device(): frame = lax.all_to_all(spread, 'band', 0, 0, tiled=True)  23.9 us
    pallas_call x4, Pallas kernels, conv_call(): pl.pallas_call(kernel, in_specs=[VMEM] * len(operands), out_specs=[VMEM,...  12.7 us
    ppermute x1, waiting for transfers between devices, on_device(): lax.ppermute(jnp.concatenate([from_chip[0:4], from_chip[8:16]], axis=0),...  9.78 us
    ppermute x1, waiting for transfers between devices, on_device(): below = lax.ppermute(parts[4:8], 'level', up)  4.63 us
    pallas_call x1, Pallas kernels, setup(): pl.pallas_call(setup_kernel, in_specs=[ANY] + [VMEM] * (len(operands) - 1...  2.78 us
    ppermute x1, starting transfers between devices, on_device(): below = lax.ppermute(parts[4:8], 'level', up)  2.41 us
  transfers between devices with their start and end apart: 5, of which 3 were waited for; matrix products, arithmetic and copies ran while one was open for 0% of the time, Pallas kernels for 0%

profile of v2, /device:TPU:8, one launch (start us, length us, event | category | flops | bytes accessed | tf_op | source)
XLA Modules:
  0.0 106.4 jit_solution(14004450721379403864)
XLA Ops:
  0.7 0.1 fusion
  0.7 0.1 pad_maximum_fusion.2.harmonic_ref
  0.8 0.7 copy-done.8
  1.5 0.0 copy-start.4
  1.5 0.0 copy-start.6
  1.5 0.0 copy-start.7
  1.5 0.1 spread.1
  1.6 13.8 %all_to_all.30.after_ref.frame_ref = f32[8,4,320]{2,1,0:T(4,128)S(1)} all-to-all(f32[8,4,320]{2,1,0:T(4,128)S(1)} %get-tuple-element.24), channel_id=1, replica_groups=mesh['level'=32,'band'=8] {'band'}, dimensions={0} | all-to-all | bytes 81920 | tf_op jit(solution)/shard_map/all_to_all | solution.py:387
  15.5 0.0 copy-start.5
  15.5 2.8 %setup.1 = (f32[4,320]{1,0:T(4,128)S(1)}, f32[2,128]{1,0:T(2,128)S(1)}, f32[1,320]{1,0:T(1,128)S(1)}, f32[16,320]{1,0:T(8,128)S(1)}, bf16[3,1024,960]{2,1,0:T(8,...) custom-call(f32[8,4,320]{2,1,0:T(4,128)S(1)} %all_to_all.30.after_ref.frame_ref, f32[1,128]{1,0:T(1,128)S(1)} %get-tuple-element.25.step_ref, ...), custom_call_target="tpu_custom_call" | custom-call | bytes 20000000 | tf_op jit(solution)/shard_map/setup/pallas_call | solution.py:167
  18.3 3.7 %conv_one.2 = (f32[448,320]{1,0:T(8,128)S(1)}, f32[8,2,320]{2,1,0:T(2,128)S(1)}) custom-call(f32[8,4,320]{2,1,0:T(4,128)S(1)} %all_to_all.30.after_ref.frame_ref, f32[4,320]{1,0:T(4,128)S(1)} %copy-done.5, f32[1,320]{1,0:T(1,128)S(1)} %get-tuple-element.26.emb_ref, bf16[3,1024,960]{2,1,0:T(8,128)(2,1)S(1)} %get-tuple-element.27.w_ref), custom_call_target="tpu_custom_call" | custom-call | flops 2477260800 | bytes 4000000 | tf_op jit(solution)/shard_map/conv_one/pallas_call | solution.py:337
  22.0 10.2 %all_to_all.31.sums_ref = f32[8,2,320]{2,1,0:T(2,128)S(1)} all-to-all(f32[8,2,320]{2,1,0:T(2,128)S(1)} %get-tuple-element.29), channel_id=1, replica_groups=mesh['level'=32,'band'=8] {'band'}, dimensions={0} | all-to-all | bytes 40960 | tf_op jit(solution)/shard_map/all_to_all | solution.py:398
  32.1 2.7 %conv_two.2 = (f32[320,320]{1,0:T(8,128)S(1)}, f32[8,2,320]{2,1,0:T(2,128)S(1)}) custom-call(f32[448,320]{1,0:T(8,128)S(1)} %get-tuple-element.28.mid_ref, f32[8,2,320]{2,1,0:T(2,128)S(1)} %all_to_all.31.sums_ref, f32[4,320]{1,0:T(4,128)S(1)} %get-tuple-element.30.own_ref, f32[4,320]{1,0:T(4,128)S(1)} %copy-done.5, ...), custom_call_target="tpu_custom_call" | custom-call | flops 1769472000 | bytes 4000000 | tf_op jit(solution)/shard_map/conv_two/pallas_call | solution.py:337
  34.8 10.1 %all_to_all.32.sums_ref = f32[8,2,320]{2,1,0:T(2,128)S(1)} all-to-all(f32[8,2,320]{2,1,0:T(2,128)S(1)} %get-tuple-element.33), channel_id=1, replica_groups=mesh['level'=32,'band'=8] {'band'}, dimensions={0} | all-to-all | bytes 40960 | tf_op jit(solution)/shard_map/all_to_all | solution.py:404
  44.9 0.6 project.2.parts_ref
  45.5 1.3 %collective-permute-start = (f32[16,320]{1,0:T(8,128)S(1)}, f32[16,320]{1,0:T(8,128)S(1)}, u32[]{:S(2)}, u32[]{:S(2)}) collective-permute-start(f32[16,320]{1,0:T(8,128)S(1)} %project.2.parts_ref), channel_id=1, source_target_pairs={{0,8},{16,24},{32,40},{48,56},{64,72},{80,88},{96,104},{112,120},{... | collective-permute-start | bytes 61448 | tf_op jit(solution)/shard_map/ppermute | solution.py:413
  46.8 0.8 collective-permute-done.zero_ref
  47.6 0.7 collective-permute-start.1
  48.3 0.0 collective-permute-done.1.chip_ref
  48.3 1.3 %collective-permute-start.2 = (f32[12,320]{1,0:T(8,128)S(1)}, f32[12,320]{1,0:T(8,128)S(1)}, u32[]{:S(2)}, u32[]{:S(2)}) collective-permute-start(f32[12,320]{1,0:T(8,128)S(1)} %pad_maximum_fusion.1), channel_id=1, source_target_pairs={{8,0},{24,16},{40,32},{56,48},{72,64},{88,80},{104,96},{120,112},{... | collective-permute-start | bytes 46088 | tf_op jit(solution)/shard_map/ppermute | solution.py:416
  49.6 9.8 %collective-permute-done.2.handed_ref = f32[12,320]{1,0:T(8,128)S(1)} collective-permute-done((f32[12,320]{1,0:T(8,128)S(1)}, f32[12,320]{1,0:T(8,128)S(1)}, u32[]{:S(2)}, u32[]{:S(2)}) %collective-permute-start.2) | collective-permute-done | bytes 15392 | tf_op jit(solution)/shard_map/ppermute | solution.py:416
  59.4 10.1 %all_to_all.33.frame_ref = f32[8,4,320]{2,1,0:T(4,128)S(1)} all-to-all(f32[8,4,320]{2,1,0:T(4,128)S(1)} %get-tuple-element.37), channel_id=1, replica_groups=mesh['level'=32,'band'=8] {'band'}, dimensions={0} | all-to-all | bytes 81920 | tf_op jit(solution)/shard_map/all_to_all | solution.py:387
  69.6 3.7 %conv_one.3 = (f32[448,320]{1,0:T(8,128)S(1)}, f32[8,2,320]{2,1,0:T(2,128)S(1)}) custom-call(f32[8,4,320]{2,1,0:T(4,128)S(1)} %all_to_all.33.frame_ref, f32[4,320]{1,0:T(4,128)S(1)} %copy-done.5, f32[1,320]{1,0:T(1,128)S(1)} %get-tuple-element.26.emb_ref, bf16[3,1024,960]{2,1,0:T(8,128)(2,1)S(1)} %get-tuple-element.27.w_ref), custom_call_target="tpu_custom_call" | custom-call | flops 2477260800 | bytes 4000000 | tf_op jit(solution)/shard_map/conv_one/pallas_call | solution.py:337
  73.2 10.1 %all_to_all.34.sums_ref = f32[8,2,320]{2,1,0:T(2,128)S(1)} all-to-all(f32[8,2,320]{2,1,0:T(2,128)S(1)} %get-tuple-element.39), channel_id=1, replica_groups=mesh['level'=32,'band'=8] {'band'}, dimensions={0} | all-to-all | bytes 40960 | tf_op jit(solution)/shard_map/all_to_all | solution.py:398
  83.4 2.7 %conv_two.3 = (f32[320,320]{1,0:T(8,128)S(1)}, f32[8,2,320]{2,1,0:T(2,128)S(1)}) custom-call(f32[448,320]{1,0:T(8,128)S(1)} %get-tuple-element.38.mid_ref, f32[8,2,320]{2,1,0:T(2,128)S(1)} %all_to_all.34.sums_ref, f32[4,320]{1,0:T(4,128)S(1)} %get-tuple-element.40.own_ref, f32[4,320]{1,0:T(4,128)S(1)} %copy-done.5, ...), custom_call_target="tpu_custom_call" | custom-call | flops 1769472000 | bytes 4000000 | tf_op jit(solution)/shard_map/conv_two/pallas_call | solution.py:337
  86.0 10.1 %all_to_all.35.sums_ref = f32[8,2,320]{2,1,0:T(2,128)S(1)} all-to-all(f32[8,2,320]{2,1,0:T(2,128)S(1)} %get-tuple-element.42), channel_id=1, replica_groups=mesh['level'=32,'band'=8] {'band'}, dimensions={0} | all-to-all | bytes 40960 | tf_op jit(solution)/shard_map/all_to_all | solution.py:404
  96.1 0.6 project.3.parts_ref
  96.7 1.9 %collective-permute-start.4 = (f32[4,320]{1,0:T(4,128)S(1)}, f32[4,320]{1,0:T(4,128)S(1)}, u32[]{:S(2)}, u32[]{:S(2)}) collective-permute-start(f32[4,320]{1,0:T(4,128)S(1)} %get-tuple-element.43), channel_id=1, source_target_pairs={{8,0},{16,8},{24,16},{32,24},{40,32},{48,40},{56,48},{64,56},{72,6... | collective-permute-start | bytes 15368 | tf_op jit(solution)/shard_map/ppermute | solution.py:427
  98.6 2.4 %collective-permute-start.3 = (f32[4,320]{1,0:T(4,128)S(1)}, f32[4,320]{1,0:T(4,128)S(1)}, u32[]{:S(2)}, u32[]{:S(2)}) collective-permute-start(f32[4,320]{1,0:T(4,128)S(1)} %get-tuple-element.44), channel_id=1, source_target_pairs={{0,8},{8,16},{16,24},{24,32},{32,40},{40,48},{48,56},{56,64},{64,7... | collective-permute-start | bytes 15368 | tf_op jit(solution)/shard_map/ppermute | solution.py:426
  101.0 0.0 collective-permute-done.4.above_ref
  101.0 4.6 %collective-permute-done.3.below_ref = f32[4,320]{1,0:T(4,128)S(1)} collective-permute-done((f32[4,320]{1,0:T(4,128)S(1)}, f32[4,320]{1,0:T(4,128)S(1)}, u32[]{:S(2)}, u32[]{:S(2)}) %collective-permute-start.3) | collective-permute-done | bytes 5152 | tf_op jit(solution)/shard_map/ppermute | solution.py:426
  105.7 0.7 finish.1
  (22 shorter events, 0.1 us)
Async XLA Ops:
  0.8 0.7 copy-start.8
  1.5 14.0 %copy-start = (f32[3,3,320,320]{3,2,1,0:T(8,128)S(1)}, f32[3,3,320,320]{3,2,1,0:T(8,128)}, u32[]{:S(2)}) copy-start(f32[3,3,320,320]{3,2,1,0:T(8,128)} %one_ref.1) | copy-start | bytes 11059204
  1.5 14.0 %copy-start.1 = (f32[3,3,320,320]{3,2,1,0:T(8,128)S(1)}, f32[3,3,320,320]{3,2,1,0:T(8,128)}, u32[]{:S(2)}) copy-start(f32[3,3,320,320]{3,2,1,0:T(8,128)} %two_ref.1) | copy-start | bytes 11059204
  1.5 14.0 %copy-start.2 = (f32[3,320,320]{2,1,0:T(8,128)S(1)}, f32[3,320,320]{2,1,0:T(8,128)}, u32[]{:S(2)}) copy-start(f32[3,320,320]{2,1,0:T(8,128)} %temporal_ref.1) | copy-start | bytes 3686404
  1.5 14.0 %copy-start.3 = (f32[320,320]{1,0:T(8,128)S(1)}, f32[320,320]{1,0:T(8,128)}, u32[]{:S(2)}) copy-start(f32[320,320]{1,0:T(8,128)} %time_ref.1) | copy-start | bytes 1228804
  1.5 14.0 %copy-start.4 = (f32[320,4]{0,1:T(4,128)S(1)}, f32[320,4]{0,1:T(4,128)}, u32[]{:S(2)}) copy-start(f32[320,4]{0,1:T(4,128)} %param.18) | copy-start | bytes 15364
  1.5 14.0 %copy-start.6 = (f32[1,4,5,64]{3,1,2,0:T(4,128)S(1)}, f32[1,4,5,64]{3,1,2,0:T(4,128)}, u32[]{:S(2)}) copy-start(f32[1,4,5,64]{3,1,2,0:T(4,128)} %param.12) | copy-start | bytes 15364
  1.5 14.0 %copy-start.7 = (f32[8,128]{1,0:T(8,128)S(1)}, f32[8,128]{1,0:T(8,128)}, u32[]{:S(2)}) copy-start(f32[8,128]{1,0:T(8,128)} %constant.8.clone.plan_ref) | copy-start | bytes 12292
  15.5 2.8 %copy-start.5 = (f32[4,320]{1,0:T(4,128)S(1)}, f32[4,320]{1,0:T(4,128)}, u32[]{:S(2)}) copy-start(f32[4,320]{1,0:T(4,128)} %w_in_ref.7) | copy-start | bytes 15364
  45.5 2.1 %collective-permute-start = (f32[16,320]{1,0:T(8,128)S(1)}, f32[16,320]{1,0:T(8,128)S(1)}, u32[]{:S(2)}, u32[]{:S(2)}) collective-permute-start(f32[16,320]{1,0:T(8,128)S(1)} %project.2.parts_ref), channel_id=1, source_target_pairs={{0,8},{16,24},{32,40},{48,56},{64,72},{80,88},{96,104},{112,120},{... | collective-permute-start | bytes 61448 | tf_op jit(solution)/shard_map/ppermute | solution.py:413
  47.6 0.7 collective-permute-start.1
  48.3 11.1 %collective-permute-start.2 = (f32[12,320]{1,0:T(8,128)S(1)}, f32[12,320]{1,0:T(8,128)S(1)}, u32[]{:S(2)}, u32[]{:S(2)}) collective-permute-start(f32[12,320]{1,0:T(8,128)S(1)} %pad_maximum_fusion.1), channel_id=1, source_target_pairs={{8,0},{24,16},{40,32},{56,48},{72,64},{88,80},{104,96},{120,112},{... | collective-permute-start | bytes 46088 | tf_op jit(solution)/shard_map/ppermute | solution.py:416
  96.7 4.3 %collective-permute-start.4 = (f32[4,320]{1,0:T(4,128)S(1)}, f32[4,320]{1,0:T(4,128)S(1)}, u32[]{:S(2)}, u32[]{:S(2)}) collective-permute-start(f32[4,320]{1,0:T(4,128)S(1)} %get-tuple-element.43), channel_id=1, source_target_pairs={{8,0},{16,8},{24,16},{32,24},{40,32},{48,40},{56,48},{64,56},{72,6... | collective-permute-start | bytes 15368 | tf_op jit(solution)/shard_map/ppermute | solution.py:427
  98.6 7.1 %collective-permute-start.3 = (f32[4,320]{1,0:T(4,128)S(1)}, f32[4,320]{1,0:T(4,128)S(1)}, u32[]{:S(2)}, u32[]{:S(2)}) collective-permute-start(f32[4,320]{1,0:T(4,128)S(1)} %get-tuple-element.44), channel_id=1, source_target_pairs={{0,8},{8,16},{16,24},{24,32},{32,40},{40,48},{48,56},{56,64},{64,7... | collective-permute-start | bytes 15368 | tf_op jit(solution)/shard_map/ppermute | solution.py:426

commit v3 on v2

--- a/solution.py
+++ b/solution.py
@@ -117,19 +117,32 @@
 
 
 def spread_kernel(
-    steps_ref, latents_ref, harmonic_ref, spread_ref, own_ref, step_ref
+    steps_ref, latents_ref, fresh_ref, harmonic_ref, spread_ref, step_ref
 ):
-    own = jnp.concatenate([latents_ref[0, r] for r in range(5)], axis=1)
-    own_ref[...] = own
-    spread_ref[...] = jnp.broadcast_to(own[None], spread_ref.shape)
+    rows = [
+        jnp.concatenate([ref[0, r] for r in range(5)], axis=1) for ref in (latents_ref, fresh_ref)
+    ]
+    both = jnp.concatenate(rows, axis=0)
+    spread_ref[...] = jnp.broadcast_to(both[None], spread_ref.shape)
     step_ref[...] = jnp.full(step_ref.shape, steps_ref[0].astype(F32), F32)
 
 
 def setup_kernel(
-    after_ref, step_ref, plan_ref, fresh_ref, harmonic_ref, w_out_ref, time_ref, temporal_ref,
-    one_ref, two_ref, new_ref, coef_ref, emb_ref, fold_ref, first_ref, second_ref,
+    frame_ref, step_ref, plan_ref, harmonic_ref, w_out_ref, time_ref, temporal_ref, one_ref,
+    two_ref, own_ref, before_ref, after_ref, across_ref, new_ref, coef_ref, emb_ref, fold_ref,
+    first_ref, second_ref,
 ):
-    new_ref[...] = jnp.concatenate([fresh_ref[0, r] for r in range(5)], axis=1)
+    strip = lax.axis_index("band") >> 1
+
+    def piece(ahead, row):
+        at = 2 * ((strip + ahead) & 3)
+        return jnp.concatenate(
+            [frame_ref[at, row : row + 4, :], frame_ref[at + 1, row : row + 4, :]], axis=1
+        )
+
+    for ref, ahead in ((own_ref, 0), (before_ref, 3), (after_ref, 1), (across_ref, 2)):
+        ref[...] = piece(ahead, 0)
+    new_ref[...] = piece(0, 4)
     step = step_ref[...].astype(jnp.int32)
     plan = plan_ref[...]
     place = lax.broadcasted_iota(jnp.int32, plan.shape, 0) * 128 + lax.broadcasted_iota(
@@ -161,12 +174,12 @@
 
 def setup(*operands):
     shapes = (
-        ((4, 320), F32), ((2, 128), F32), ((1, 320), F32), ((16, 320), F32),
+        *[((4, 640), F32)] * 5, ((2, 128), F32), ((1, 320), F32), ((16, 320), F32),
         ((3, 1024, 960), BF16), ((3, 1024, 960), BF16),
     )
     return pl.pallas_call(
         setup_kernel,
-        in_specs=[ANY] + [VMEM] * (len(operands) - 1),
+        in_specs=[VMEM] * len(operands),
         out_specs=[VMEM] * len(shapes),
         out_shape=[jax.ShapeDtypeStruct(*shape) for shape in shapes],
         compiler_params=pltpu.CompilerParams(vmem_limit_bytes=LIMIT),
@@ -200,100 +213,94 @@
     return jnp.concatenate([main, rest], axis=1)
 
 
+def write_sums(stat_ref, total, square):
+    stat_ref[...] = jnp.concatenate(
+        [jnp.sum(total, axis=0, keepdims=True), jnp.sum(square, axis=0, keepdims=True)], axis=0
+    )
+
+
 def conv1_kernel(
-    members, frame_ref, w_in_ref, emb_ref, w_ref, mid_ref, stat_ref, a_ref, acc_ref,
-    lift_ref,
+    members, own_ref, before_ref, after_ref, across_ref, w_in_ref, emb_ref, w_ref, mid_ref, stat_ref,
+    a_ref, acc_ref, lift_ref,
 ):
-    band = lax.axis_index("band")
-    bands = frame_ref.shape[0]
-
-    frame = frame_ref[...]
+    strip = lax.axis_index("band") >> 1
+    pieces = [ref[...] for ref in (own_ref, before_ref, after_ref, across_ref)]
     w = w_in_ref[...]
     average = 1.0 / members
-    mean = jnp.sum(jnp.sum(frame, axis=0), axis=1, keepdims=True) * average
+    mean = jnp.sum(sum(pieces), axis=1, keepdims=True) * average
     mean = jnp.sum(mean * w, axis=0, keepdims=True)
     square = jnp.zeros_like(mean)
     for j in range(4):
-        moment = jnp.sum(frame * frame[:, j : j + 1, :], axis=0)
+        moment = sum(piece * piece[j : j + 1] for piece in pieces)
         moment = jnp.sum(moment, axis=1, keepdims=True) * average
         square += w[j : j + 1] * jnp.sum(moment * w, axis=0, keepdims=True)
     center, factor = center_factor(jnp.concatenate([mean, square], axis=0))
-    before = frame_ref[jnp.maximum(band - 1, 0)]
-    after = frame_ref[jnp.minimum(band + 1, bands - 1)]
-    around = jnp.concatenate(
-        [before[:, 192:320], frame_ref[band], after[:, 0:128]], axis=1
-    )
+    around = jnp.concatenate([pieces[1][:, 512:640], pieces[0], pieces[2][:, 0:128]], axis=1)
     lift_ref[...] = lift(around, w)
-    for i in range(9):
+    for i in range(14):
         rows = slice(64 * i, 64 * i + 64)
         act = silu((lift_ref[rows, :] - center) * factor)
         if i < 2:
-            act = act * jnp.where(band > 0, 1.0, 0.0)
-        elif i >= 7:
-            act = act * jnp.where(band < bands - 1, 1.0, 0.0)
+            act = act * jnp.where(strip > 0, 1.0, 0.0)
+        elif i >= 12:
+            act = act * jnp.where(strip < 3, 1.0, 0.0)
         put_left(a_ref, rows, act)
-
-    multiply(acc_ref, a_ref, w_ref, 448)
-
+    multiply(acc_ref, a_ref, w_ref, 768)
     total = jnp.zeros((8, 320), F32)
     square = jnp.zeros((8, 320), F32)
-    for i in range(7):
+    for i in range(12):
         out = shifted_sum(acc_ref, i) + emb_ref[...]
         mid_ref[64 * i : 64 * i + 64, :] = out
-        if 1 <= i <= 5:
+        if 1 <= i <= 10:
             folded = out.reshape(8, 8, 320)
             total += jnp.sum(folded, axis=0)
             square += jnp.sum(folded * folded, axis=0)
-    stat_ref[...] = jnp.broadcast_to(
-        jnp.concatenate(
-            [jnp.sum(total, axis=0, keepdims=True), jnp.sum(square, axis=0, keepdims=True)],
-            axis=0,
-        )[None],
-        stat_ref.shape,
-    )
+    write_sums(stat_ref, total, square)
 
 
 def conv2_kernel(
-    members, mid_ref, sums_ref, own_ref, w_in_ref, w_ref, hid_ref, stat_ref, a_ref,
-    acc_ref,
+    members, mid_ref, sum0_ref, sum1_ref, sum2_ref, sum3_ref, own_ref, w_in_ref, w_ref, hid_ref,
+    stat_ref, a_ref, acc_ref,
 ):
-    band = lax.axis_index("band")
-    bands = sums_ref.shape[0]
-
-    center, factor = center_factor(jnp.sum(sums_ref[...], axis=0) * (1.0 / members))
-    for i in range(7):
+    strip = lax.axis_index("band") >> 1
+    sums = sum0_ref[...] + sum1_ref[...] + sum2_ref[...] + sum3_ref[...]
+    center, factor = center_factor(sums * (1.0 / members))
+    for i in range(12):
         rows = slice(64 * i, 64 * i + 64)
         act = silu((mid_ref[rows, :] - center) * factor)
         if i == 0:
-            act = act * jnp.where(band > 0, 1.0, 0.0)
-        elif i == 6:
-            act = act * jnp.where(band < bands - 1, 1.0, 0.0)
+            act = act * jnp.where(strip > 0, 1.0, 0.0)
+        elif i == 11:
+            act = act * jnp.where(strip < 3, 1.0, 0.0)
         put_left(a_ref, rows, act)
-
-    multiply(acc_ref, a_ref, w_ref, 320)
-
+    multiply(acc_ref, a_ref, w_ref, 640)
     total = jnp.zeros((8, 320), F32)
     square = jnp.zeros((8, 320), F32)
     hid_ref[...] = lift(own_ref[...], w_in_ref[...])
-    for i in range(5):
+    for i in range(10):
         rows = slice(64 * i, 64 * i + 64)
         out = hid_ref[rows, :] + shifted_sum(acc_ref, i)
         hid_ref[rows, :] = out
         folded = out.reshape(8, 8, 320)
         total += jnp.sum(folded, axis=0)
         square += jnp.sum(folded * folded, axis=0)
-    stat_ref[...] = jnp.broadcast_to(
-        jnp.concatenate(
-            [jnp.sum(total, axis=0, keepdims=True), jnp.sum(square, axis=0, keepdims=True)],
-            axis=0,
-        )[None],
-        stat_ref.shape,
-    )
-
-
-def project_kernel(members, hid_ref, sums_ref, own_ref, w_out_ref, fold_ref, coef_ref, out_ref):
-    center, factor = center_factor(jnp.sum(sums_ref[...], axis=0) * (1.0 / members))
-    hidden = hid_ref[...]
+    write_sums(stat_ref, total, square)
+
+
+def project_kernel(
+    members, last, hid_ref, sum0_ref, sum1_ref, sum2_ref, sum3_ref, own_ref, w_out_ref, fold_ref,
+    coef_ref, out_ref,
+):
+    sums = sum0_ref[...] + sum1_ref[...] + sum2_ref[...] + sum3_ref[...]
+    center, factor = center_factor(sums * (1.0 / members))
+    if last:
+        low = lax.axis_index("band") & 1
+        hidden = hid_ref[pl.ds(pl.multiple_of(low * 320, 64), 320), :]
+        both = own_ref[...]
+        own = jnp.where(low == 0, both[:, 0:320], both[:, 320:640])
+    else:
+        hidden = hid_ref[...]
+        own = own_ref[...]
     act = silu((hidden - center) * factor)
     w_out = jnp.concatenate([w_out_ref[...], w_out_ref[...] * 0.0], axis=0)
     from_hidden = product(w_out, hidden, ((1,), (1,)))
@@ -301,28 +308,19 @@
     local = from_hidden[0:4] + from_act[0:4]
     ratio = coef_ref[0:1, 0:1]
     noise = coef_ref[1:2, 0:1]
-    out_ref[0:4] = ratio * own_ref[...] + noise * local
-    out_ref[4:8] = from_act[4:8]
-    out_ref[8:12] = from_act[8:12]
-    out_ref[12:16] = jnp.broadcast_to(noise, (4, out_ref.shape[1]))
-
-
-def merge_kernel(parts_ref, zero_ref, chip_ref, handed_ref, fresh_ref, own_ref, spread_ref):
-    level = lax.axis_index("level")
-    odd = jnp.where(level % 2 == 1, 1.0, 0.0)
-    even = 1.0 - odd
-    new = jnp.where(level == 0, 1.0, 0.0)
-    update = odd * zero_ref[0:4] + even * handed_ref[0:4]
-    noise = odd * zero_ref[12:16] + even * handed_ref[4:8]
-    below = odd * chip_ref[4:8] + even * handed_ref[8:12]
-    moved = update + noise * (below + parts_ref[8:12])
-    own = new * fresh_ref[...] + (1.0 - new) * moved
-    own_ref[...] = own
-    spread_ref[...] = jnp.broadcast_to(own[None], spread_ref.shape)
+    out_ref[0:4] = ratio * own + noise * local
+    out_ref[4:8] = jnp.broadcast_to(noise, (4, out_ref.shape[1]))
+    out_ref[8:12] = from_act[4:8]
+    out_ref[12:16] = from_act[8:12]
+
+
+def merge_kernel(parts_ref, one_ref, two_ref, fresh_ref, own_ref):
+    moved = one_ref[0:4] + one_ref[4:8] * (two_ref[...] + parts_ref[12:16])
+    own_ref[...] = jnp.where(lax.axis_index("level") == 0, fresh_ref[...], moved)
 
 
 def finish_kernel(parts_ref, below_ref, above_ref, out_ref):
-    own = parts_ref[0:4] + parts_ref[12:16] * (below_ref[...] + above_ref[...])
+    own = parts_ref[0:4] + parts_ref[4:8] * (below_ref[...] + above_ref[...])
     for r in range(5):
         out_ref[0, r] = own[:, 64 * r : 64 * r + 64]
 
@@ -340,7 +338,7 @@
         out_specs=[VMEM, VMEM],
         out_shape=[
             jax.ShapeDtypeStruct((rows_out * 64, 320), F32),
-            jax.ShapeDtypeStruct((8, 2, 320), F32),
+            jax.ShapeDtypeStruct((2, 320), F32),
         ],
         scratch_shapes=[
             pltpu.VMEM((rows_in * 64, 1024), BF16),
@@ -369,6 +367,14 @@
     )(*operands)
 
 
+def around_strip(value):
+    bands = lax.axis_size("band")
+    return [value] + [
+        lax.ppermute(value, "band", [(i, (i + 2 * k) % bands) for i in range(bands)])
+        for k in (1, 3, 2)
+    ]
+
+
 def on_device(latents, timesteps, fresh, w_in, conv_first, conv_second, w_time, temporal, w_out):
     levels = lax.axis_size("level")
     positions = latents.shape[2] * latents.shape[3]
@@ -378,56 +384,47 @@
     plan = np.zeros((8, 128), np.float32)
     plan.reshape(-1)[:NSTEPS] = noise_plan()
     plan = jnp.asarray(plan)
-    spread, own, step = call(
-        spread_kernel, [SMEM, VMEM, ANY], [(8, 4, positions), (4, positions), (1, 128)],
-        (timesteps, latents.transpose(0, 2, 1, 3), harmonic), "spread",
-        pl.CostEstimate(flops=8_000_000_000, bytes_accessed=40_000, transcendentals=0),
+    spread, step = call(
+        spread_kernel, [SMEM, VMEM, VMEM, ANY], [(8, 8, positions), (1, 128)],
+        (timesteps, latents.transpose(0, 2, 1, 3), fresh.transpose(0, 2, 1, 3), harmonic),
+        "spread", pl.CostEstimate(flops=8_000_000_000, bytes_accessed=40_000, transcendentals=0),
+    )
+    frame = lax.all_to_all(spread, "band", 0, 0, tiled=True)
+    *pieces, new, coef, embedded, folded, first_ready, second_ready = setup(
+        frame, step, plan, harmonic, out_rows, w_time, temporal, conv_first, conv_second
     )
     for iteration in range(ITERS):
-        frame = lax.all_to_all(spread, "band", 0, 0, tiled=True)
-        if iteration == 0:
-            new, coef, embedded, folded, first_ready, second_ready = setup(
-                frame, step, plan, fresh.transpose(0, 2, 1, 3), harmonic, out_rows, w_time,
-                temporal, conv_first, conv_second,
-            )
+        last = iteration + 1 == ITERS
         middle, stats = conv_call(
             functools.partial(conv1_kernel, members),
-            (frame, w_in, embedded, first_ready),
-            9, 7, [pltpu.VMEM((576, 320), F32)], "conv_one",
+            (*pieces, w_in, embedded, first_ready),
+            14, 12, [pltpu.VMEM((896, 320), F32)], "conv_one",
         )
-        sums = lax.all_to_all(stats, "band", 0, 0, tiled=True)
         hidden, stats = conv_call(
             functools.partial(conv2_kernel, members),
-            (middle, sums, own, w_in, second_ready),
-            7, 5, [], "conv_two",
+            (middle, *around_strip(stats), pieces[0], w_in, second_ready),
+            12, 10, [], "conv_two",
         )
-        sums = lax.all_to_all(stats, "band", 0, 0, tiled=True)
+        width = positions if last else 2 * positions
         (parts,) = call(
-            functools.partial(project_kernel, members), [VMEM] * 6, [(16, positions)],
-            (hidden, sums, own, out_rows, folded, coef), "project",
+            functools.partial(project_kernel, members, last), [VMEM] * 9, [(16, width)],
+            (hidden, *around_strip(stats), pieces[0], out_rows, folded, coef), "project",
         )
-        if iteration + 1 < ITERS:
-            inside = [(i, i + 1) for i in range(0, levels, 2)]
-            across = [(i, i + 2) for i in range(1, levels - 2, 2)]
-            back = [(i + 1, i) for i in range(0, levels, 2)]
-            from_zero = lax.ppermute(parts, "level", inside)
-            over = jnp.concatenate([parts[0:8], parts[12:16], from_zero[4:8]], axis=0)
-            from_chip = lax.ppermute(over, "level", across)
-            handed = lax.ppermute(
-                jnp.concatenate([from_chip[0:4], from_chip[8:16]], axis=0), "level", back
-            )
-            own, spread = call(
-                merge_kernel, [VMEM] * 5, [(4, positions), spread.shape],
-                (parts, from_zero, from_chip, handed, new), "merge",
-            )
-        else:
+        if last:
             up = [(i, i + 1) for i in range(levels - 1)]
             down = [(j, i) for i, j in up]
-            below = lax.ppermute(parts[4:8], "level", up)
-            above = lax.ppermute(parts[8:12], "level", down)
+            below = lax.ppermute(parts[8:12], "level", up)
+            above = lax.ppermute(parts[12:16], "level", down)
             (out,) = call(
                 finish_kernel, [VMEM] * 3, [(1, 5, 4, 64)], (parts, below, above), "finish"
             )
+        else:
+            one = lax.ppermute(parts[0:8], "level", [(i, i + 1) for i in range(levels - 1)])
+            two = lax.ppermute(parts[8:12], "level", [(i, i + 2) for i in range(levels - 2)])
+            (own,) = call(
+                merge_kernel, [VMEM] * 4, [(4, width)], (parts, one, two, new), "merge"
+            )
+            pieces = around_strip(own)
     return out.transpose(0, 2, 1, 3)
 
 

time: 107 us -> 100 us (0.935)
  blocking collectives: 64.4 us -> 13.9 us
  waiting for transfers between devices: 15.2 us -> 32.6 us
  starting transfers between devices: 7.58 us -> 24.3 us
  Pallas kernels: 17.4 us -> 26.6 us
    all_to_all x4 -> x0, blocking collectives: 40.4 us -> none  [on_device(): sums = lax.all_to_all(stats, 'band', 0, 0, tiled=True)]
    ppermute x5 -> x19, waiting for transfers between devices: 15.2 us -> 32.6 us  [the longest x15 21.6 us: around_strip(): lax.ppermute(value, 'band', [(i, (i + 2 * k) % bands) for i in range(band...]
    ppermute x5 -> x19, starting transfers between devices: 7.58 us -> 24.3 us  [the longest x15 14.2 us: around_strip(): lax.ppermute(value, 'band', [(i, (i + 2 * k) % bands) for i in range(band...]
    all_to_all x2 -> x1, blocking collectives: 23.9 us -> 13.9 us  [on_device(): frame = lax.all_to_all(spread, 'band', 0, 0, tiled=True)]
    pallas_call x4, Pallas kernels: 12.7 us -> 21.4 us  [conv_call(): pl.pallas_call(kernel, in_specs=[VMEM] * len(operands), out_specs=[VMEM,...]
  transfers between devices with their start and end apart: 5 -> 19, of which waited for: 3 -> 12; matrix products, arithmetic and copies ran while one was open for 0% -> 0% of each run, Pallas kernels for 0% -> 0%
where the time goes in v3:
time: 100 us; the launch traced here: 99.9 us
  waiting for transfers between devices  32.6 us (33%)
  Pallas kernels  26.6 us (27%)
  starting transfers between devices  24.3 us (24%)
  blocking collectives  13.9 us (14%)
  local copies, waits for them, and re-layouts  1.45 us (1%)
    ppermute x15, waiting for transfers between devices, around_strip(): lax.ppermute(value, 'band', [(i, (i + 2 * k) % bands) for i in range(band...  21.6 us
    pallas_call x4, Pallas kernels, conv_call(): pl.pallas_call(kernel, in_specs=[VMEM] * len(operands), out_specs=[VMEM,...  21.4 us
    ppermute x15, starting transfers between devices, around_strip(): lax.ppermute(value, 'band', [(i, (i + 2 * k) % bands) for i in range(band...  14.2 us
    all_to_all x1, blocking collectives, on_device(): frame = lax.all_to_all(spread, 'band', 0, 0, tiled=True)  13.9 us
    ppermute x1, waiting for transfers between devices, on_device(): lax.ppermute(parts[8:12], 'level', [(i, i + 2) for i in range(levels - 2)])  6.36 us
    ppermute x1, waiting for transfers between devices, on_device(): below = lax.ppermute(parts[8:12], 'level', up)  4.63 us
    ppermute x1, starting transfers between devices, on_device(): lax.ppermute(parts[8:12], 'level', [(i, i + 2) for i in range(levels - 2)])  3.82 us
    pallas_call x1, Pallas kernels, setup(): pl.pallas_call(setup_kernel, in_specs=[VMEM] * len(operands), out_specs=[...  3 us
  transfers between devices with their start and end apart: 19, of which 12 were waited for; matrix products, arithmetic and copies ran while one was open for 0% of the time, Pallas kernels for 0%

profile of v3, /device:TPU:8, one launch (start us, length us, event | category | flops | bytes accessed | tf_op | source)
XLA Modules:
  0.0 99.9 jit_solution(3794531031118696244)
XLA Ops:
  2.3 13.9 %all_to_all.5.frame_ref = f32[8,8,320]{2,1,0:T(8,128)S(1)} all-to-all(f32[8,8,320]{2,1,0:T(8,128)S(1)} %get-tuple-element.25), channel_id=1, replica_groups=mesh['level'=32,'band'=8] {'band'}, dimensions={0} | all-to-all | bytes 163840 | tf_op jit(solution)/shard_map/all_to_all | solution.py:392
  16.3 3.0 %setup.1 = (f32[4,640]{1,0:T(4,128)S(1)}, f32[4,640]{1,0:T(4,128)S(1)}, f32[4,640]{1,0:T(4,128)S(1)}, f32[4,640]{1,0:T(4,128)S(1)}, f32[4,640]{1,0:T(4,128)S(1)}...) custom-call(f32[8,8,320]{2,1,0:T(8,128)S(1)} %all_to_all.5.frame_ref, ...), custom_call_target="tpu_custom_call" | custom-call | bytes 20000000 | tf_op jit(solution)/shard_map/setup/pallas_call | solution.py:180
  19.3 5.8 %conv_one.2 = (f32[768,320]{1,0:T(8,128)S(1)}, f32[2,320]{1,0:T(2,128)S(1)}) custom-call(f32[4,640]{1,0:T(4,128)S(1)} %get-tuple-element.27.own_ref, f32[4,640]{1,0:T(4,128)S(1)} %get-tuple-element.28.before_ref, f32[4,640]{1,0:T(4,128)S(1)} %get-tuple-element.29.after_ref, f32[4,640]{1,0:T(4,128)S(1)} %get-tuple-element.30.across_ref, ...), custom_call_target="tpu_custom_call" | custom-call | flops 4246732800 | bytes 4000000 | tf_op jit(solution)/shard_map/conv_one/pallas_call | solution.py:335
  25.1 1.5 %collective-permute-start.2 = (f32[2,320]{1,0:T(2,128)S(1)}, f32[2,320]{1,0:T(2,128)S(1)}, u32[]{:S(2)}, u32[]{:S(2)}) collective-permute-start(f32[2,320]{1,0:T(2,128)S(1)} %get-tuple-element.34.sum0_ref), channel_id=1, source_target_pairs={{0,4},{1,5},{2,6},{3,7},{4,0},{5,1},{6,2},{7,3},{8,12},{9,13},{10,... | collective-permute-start | bytes 7688 | tf_op jit(solution)/shard_map/ppermute | solution.py:373
  26.6 1.8 %collective-permute-start.1 = (f32[2,320]{1,0:T(2,128)S(1)}, f32[2,320]{1,0:T(2,128)S(1)}, u32[]{:S(2)}, u32[]{:S(2)}) collective-permute-start(f32[2,320]{1,0:T(2,128)S(1)} %get-tuple-element.34.sum0_ref), channel_id=1, source_target_pairs={{0,6},{1,7},{2,0},{3,1},{4,2},{5,3},{6,4},{7,5},{8,14},{9,15},{10,... | collective-permute-start | bytes 7688 | tf_op jit(solution)/shard_map/ppermute | solution.py:373
  28.6 1.6 %collective-permute-done.2.sum3_ref = f32[2,320]{1,0:T(2,128)S(1)} collective-permute-done((f32[2,320]{1,0:T(2,128)S(1)}, f32[2,320]{1,0:T(2,128)S(1)}, u32[]{:S(2)}, u32[]{:S(2)}) %collective-permute-start.2) | collective-permute-done | bytes 2592 | tf_op jit(solution)/shard_map/ppermute | solution.py:373
  30.3 2.9 %collective-permute-done.sum1_ref = f32[2,320]{1,0:T(2,128)S(1)} collective-permute-done((f32[2,320]{1,0:T(2,128)S(1)}, f32[2,320]{1,0:T(2,128)S(1)}, u32[]{:S(2)}, u32[]{:S(2)}) %collective-permute-start) | collective-permute-done | bytes 2592 | tf_op jit(solution)/shard_map/ppermute | solution.py:373
  33.2 4.9 %conv_two.2 = (f32[640,320]{1,0:T(8,128)S(1)}, f32[2,320]{1,0:T(2,128)S(1)}) custom-call(f32[768,320]{1,0:T(8,128)S(1)} %get-tuple-element.33.mid_ref, f32[2,320]{1,0:T(2,128)S(1)} %get-tuple-element.34.sum0_ref, f32[2,320]{1,0:T(2,128)S(1)} %collective-permute-done.sum1_ref, f32[2,320]{1,0:T(2,128)S(1)} %collective-permute-done.1.sum2_ref, ...), custom_call_target="tpu_custom_call" | custom-call | flops 3538944000 | bytes 4000000 | tf_op jit(solution)/shard_map/conv_two/pallas_call | solution.py:335
  38.2 1.7 %collective-permute-start.4 = (f32[2,320]{1,0:T(2,128)S(1)}, f32[2,320]{1,0:T(2,128)S(1)}, u32[]{:S(2)}, u32[]{:S(2)}) collective-permute-start(f32[2,320]{1,0:T(2,128)S(1)} %get-tuple-element.37.sum0_ref), channel_id=1, source_target_pairs={{0,6},{1,7},{2,0},{3,1},{4,2},{5,3},{6,4},{7,5},{8,14},{9,15},{10,... | collective-permute-start | bytes 7688 | tf_op jit(solution)/shard_map/ppermute | solution.py:373
  40.3 3.0 %collective-permute-done.5.sum3_ref = f32[2,320]{1,0:T(2,128)S(1)} collective-permute-done((f32[2,320]{1,0:T(2,128)S(1)}, f32[2,320]{1,0:T(2,128)S(1)}, u32[]{:S(2)}, u32[]{:S(2)}) %collective-permute-start.5) | collective-permute-done | bytes 2592 | tf_op jit(solution)/shard_map/ppermute | solution.py:373
  43.3 1.4 %collective-permute-done.3.sum1_ref = f32[2,320]{1,0:T(2,128)S(1)} collective-permute-done((f32[2,320]{1,0:T(2,128)S(1)}, f32[2,320]{1,0:T(2,128)S(1)}, u32[]{:S(2)}, u32[]{:S(2)}) %collective-permute-start.3) | collective-permute-done | bytes 2592 | tf_op jit(solution)/shard_map/ppermute | solution.py:373
  44.7 0.9 project.2.parts_ref
  45.6 1.9 %collective-permute-start.6 = (f32[8,640]{1,0:T(8,128)S(1)}, f32[8,640]{1,0:T(8,128)S(1)}, u32[]{:S(2)}, u32[]{:S(2)}) collective-permute-start(f32[8,640]{1,0:T(8,128)S(1)} %slice.16), channel_id=1, source_target_pairs={{0,8},{8,16},{16,24},{24,32},{32,40},{40,48},{48,56},{56,64},{64,7... | collective-permute-start | bytes 61448 | tf_op jit(solution)/shard_map/ppermute | solution.py:422
  47.5 3.8 %collective-permute-start.7 = (f32[4,640]{1,0:T(4,128)S(1)}, f32[4,640]{1,0:T(4,128)S(1)}, u32[]{:S(2)}, u32[]{:S(2)}) collective-permute-start(f32[4,640]{1,0:T(4,128)S(1)} %slice.17), channel_id=1, source_target_pairs={{0,16},{8,24},{16,32},{24,40},{32,48},{40,56},{48,64},{56,72},{64,... | collective-permute-start | bytes 30728 | tf_op jit(solution)/shard_map/ppermute | solution.py:423
  51.3 6.4 %collective-permute-done.7.two_ref = f32[4,640]{1,0:T(4,128)S(1)} collective-permute-done((f32[4,640]{1,0:T(4,128)S(1)}, f32[4,640]{1,0:T(4,128)S(1)}, u32[]{:S(2)}, u32[]{:S(2)}) %collective-permute-start.7) | collective-permute-done | bytes 10272 | tf_op jit(solution)/shard_map/ppermute | solution.py:423
  58.5 1.3 %collective-permute-start.9 = (f32[4,640]{1,0:T(4,128)S(1)}, f32[4,640]{1,0:T(4,128)S(1)}, u32[]{:S(2)}, u32[]{:S(2)}) collective-permute-start(f32[4,640]{1,0:T(4,128)S(1)} %merge.1.own_ref), channel_id=1, source_target_pairs={{0,6},{1,7},{2,0},{3,1},{4,2},{5,3},{6,4},{7,5},{8,14},{9,15},{10,... | collective-permute-start | bytes 30728 | tf_op jit(solution)/shard_map/ppermute | solution.py:373
  59.7 0.8 collective-permute-start.8
  60.5 2.5 %collective-permute-done.10.across_ref = f32[4,640]{1,0:T(4,128)S(1)} collective-permute-done((f32[4,640]{1,0:T(4,128)S(1)}, f32[4,640]{1,0:T(4,128)S(1)}, u32[]{:S(2)}, u32[]{:S(2)}) %collective-permute-start.10) | collective-permute-done | bytes 10272 | tf_op jit(solution)/shard_map/ppermute | solution.py:373
  63.0 1.6 %collective-permute-done.8.before_ref = f32[4,640]{1,0:T(4,128)S(1)} collective-permute-done((f32[4,640]{1,0:T(4,128)S(1)}, f32[4,640]{1,0:T(4,128)S(1)}, u32[]{:S(2)}, u32[]{:S(2)}) %collective-permute-start.8) | collective-permute-done | bytes 10272 | tf_op jit(solution)/shard_map/ppermute | solution.py:373
  64.6 5.8 %conv_one.3 = (f32[768,320]{1,0:T(8,128)S(1)}, f32[2,320]{1,0:T(2,128)S(1)}) custom-call(f32[4,640]{1,0:T(4,128)S(1)} %merge.1.own_ref, f32[4,640]{1,0:T(4,128)S(1)} %collective-permute-done.8.before_ref, f32[4,640]{1,0:T(4,128)S(1)} %collective-permute-done.9.after_ref, f32[4,640]{1,0:T(4,128)S(1)} %collective-permute-done.10.across_ref, ...), custom_call_target="tpu_custom_call" | custom-call | flops 4246732800 | bytes 4000000 | tf_op jit(solution)/shard_map/conv_one/pallas_call | solution.py:335
  70.4 1.1 %collective-permute-start.13 = (f32[2,320]{1,0:T(2,128)S(1)}, f32[2,320]{1,0:T(2,128)S(1)}, u32[]{:S(2)}, u32[]{:S(2)}) collective-permute-start(f32[2,320]{1,0:T(2,128)S(1)} %get-tuple-element.42.sum0_ref), channel_id=1, source_target_pairs={{0,4},{1,5},{2,6},{3,7},{4,0},{5,1},{6,2},{7,3},{8,12},{9,13},{10,... | collective-permute-start | bytes 7688 | tf_op jit(solution)/shard_map/ppermute | solution.py:373
  71.5 1.2 %collective-permute-start.12 = (f32[2,320]{1,0:T(2,128)S(1)}, f32[2,320]{1,0:T(2,128)S(1)}, u32[]{:S(2)}, u32[]{:S(2)}) collective-permute-start(f32[2,320]{1,0:T(2,128)S(1)} %get-tuple-element.42.sum0_ref), channel_id=1, source_target_pairs={{0,6},{1,7},{2,0},{3,1},{4,2},{5,3},{6,4},{7,5},{8,14},{9,15},{10,... | collective-permute-start | bytes 7688 | tf_op jit(solution)/shard_map/ppermute | solution.py:373
  72.7 0.8 collective-permute-start.11
  73.5 2.1 %collective-permute-done.13.sum3_ref = f32[2,320]{1,0:T(2,128)S(1)} collective-permute-done((f32[2,320]{1,0:T(2,128)S(1)}, f32[2,320]{1,0:T(2,128)S(1)}, u32[]{:S(2)}, u32[]{:S(2)}) %collective-permute-start.13) | collective-permute-done | bytes 2592 | tf_op jit(solution)/shard_map/ppermute | solution.py:373
  75.6 1.9 %collective-permute-done.11.sum1_ref = f32[2,320]{1,0:T(2,128)S(1)} collective-permute-done((f32[2,320]{1,0:T(2,128)S(1)}, f32[2,320]{1,0:T(2,128)S(1)}, u32[]{:S(2)}, u32[]{:S(2)}) %collective-permute-start.11) | collective-permute-done | bytes 2592 | tf_op jit(solution)/shard_map/ppermute | solution.py:373
  77.5 4.9 %conv_two.3 = (f32[640,320]{1,0:T(8,128)S(1)}, f32[2,320]{1,0:T(2,128)S(1)}) custom-call(f32[768,320]{1,0:T(8,128)S(1)} %get-tuple-element.41.mid_ref, f32[2,320]{1,0:T(2,128)S(1)} %get-tuple-element.42.sum0_ref, f32[2,320]{1,0:T(2,128)S(1)} %collective-permute-done.11.sum1_ref, f32[2,320]{1,0:T(2,128)S(1)} %collective-permute-done.12.sum2_ref, ...), custom_call_target="tpu_custom_call" | custom-call | flops 3538944000 | bytes 4000000 | tf_op jit(solution)/shard_map/conv_two/pallas_call | solution.py:335
  83.0 1.8 %collective-permute-start.15 = (f32[2,320]{1,0:T(2,128)S(1)}, f32[2,320]{1,0:T(2,128)S(1)}, u32[]{:S(2)}, u32[]{:S(2)}) collective-permute-start(f32[2,320]{1,0:T(2,128)S(1)} %get-tuple-element.44.sum0_ref), channel_id=1, source_target_pairs={{0,6},{1,7},{2,0},{3,1},{4,2},{5,3},{6,4},{7,5},{8,14},{9,15},{10,... | collective-permute-start | bytes 7688 | tf_op jit(solution)/shard_map/ppermute | solution.py:373
  85.0 2.6 %collective-permute-done.16.sum3_ref = f32[2,320]{1,0:T(2,128)S(1)} collective-permute-done((f32[2,320]{1,0:T(2,128)S(1)}, f32[2,320]{1,0:T(2,128)S(1)}, u32[]{:S(2)}, u32[]{:S(2)}) %collective-permute-start.16) | collective-permute-done | bytes 2592 | tf_op jit(solution)/shard_map/ppermute | solution.py:373
  87.6 2.0 %collective-permute-done.14.sum1_ref = f32[2,320]{1,0:T(2,128)S(1)} collective-permute-done((f32[2,320]{1,0:T(2,128)S(1)}, f32[2,320]{1,0:T(2,128)S(1)}, u32[]{:S(2)}, u32[]{:S(2)}) %collective-permute-start.14) | collective-permute-done | bytes 2592 | tf_op jit(solution)/shard_map/ppermute | solution.py:373
  90.2 1.9 %collective-permute-start.18 = (f32[4,320]{1,0:T(4,128)S(1)}, f32[4,320]{1,0:T(4,128)S(1)}, u32[]{:S(2)}, u32[]{:S(2)}) collective-permute-start(f32[4,320]{1,0:T(4,128)S(1)} %get-tuple-element.45), channel_id=1, source_target_pairs={{8,0},{16,8},{24,16},{32,24},{40,32},{48,40},{56,48},{64,56},{72,6... | collective-permute-start | bytes 15368 | tf_op jit(solution)/shard_map/ppermute | solution.py:417
  92.1 2.4 %collective-permute-start.17 = (f32[4,320]{1,0:T(4,128)S(1)}, f32[4,320]{1,0:T(4,128)S(1)}, u32[]{:S(2)}, u32[]{:S(2)}) collective-permute-start(f32[4,320]{1,0:T(4,128)S(1)} %get-tuple-element.46), channel_id=1, source_target_pairs={{0,8},{8,16},{16,24},{24,32},{32,40},{40,48},{48,56},{56,64},{64,7... | collective-permute-start | bytes 15368 | tf_op jit(solution)/shard_map/ppermute | solution.py:416
  94.6 4.6 %collective-permute-done.17.below_ref = f32[4,320]{1,0:T(4,128)S(1)} collective-permute-done((f32[4,320]{1,0:T(4,128)S(1)}, f32[4,320]{1,0:T(4,128)S(1)}, u32[]{:S(2)}, u32[]{:S(2)}) %collective-permute-start.17) | collective-permute-done | bytes 5152 | tf_op jit(solution)/shard_map/ppermute | solution.py:416
  (40 shorter events, 5.2 us)
Async XLA Ops:
  0.8 0.7 copy-start.6
  1.5 0.7 copy-start.7
  2.2 14.0 %copy-start = (f32[3,3,320,320]{3,2,1,0:T(8,128)S(1)}, f32[3,3,320,320]{3,2,1,0:T(8,128)}, u32[]{:S(2)}) copy-start(f32[3,3,320,320]{3,2,1,0:T(8,128)} %one_ref.1) | copy-start | bytes 11059204
  2.2 14.0 %copy-start.1 = (f32[3,3,320,320]{3,2,1,0:T(8,128)S(1)}, f32[3,3,320,320]{3,2,1,0:T(8,128)}, u32[]{:S(2)}) copy-start(f32[3,3,320,320]{3,2,1,0:T(8,128)} %two_ref.1) | copy-start | bytes 11059204
  2.2 14.0 %copy-start.2 = (f32[3,320,320]{2,1,0:T(8,128)S(1)}, f32[3,320,320]{2,1,0:T(8,128)}, u32[]{:S(2)}) copy-start(f32[3,320,320]{2,1,0:T(8,128)} %temporal_ref.1) | copy-start | bytes 3686404
  2.2 14.0 %copy-start.3 = (f32[320,320]{1,0:T(8,128)S(1)}, f32[320,320]{1,0:T(8,128)}, u32[]{:S(2)}) copy-start(f32[320,320]{1,0:T(8,128)} %time_ref.1) | copy-start | bytes 1228804
  2.2 14.0 %copy-start.4 = (f32[320,4]{0,1:T(4,128)S(1)}, f32[320,4]{0,1:T(4,128)}, u32[]{:S(2)}) copy-start(f32[320,4]{0,1:T(4,128)} %param.18) | copy-start | bytes 15364
  2.2 14.0 %copy-start.5 = (f32[8,128]{1,0:T(8,128)S(1)}, f32[8,128]{1,0:T(8,128)}, u32[]{:S(2)}) copy-start(f32[8,128]{1,0:T(8,128)} %constant.8.clone.plan_ref) | copy-start | bytes 12292
  16.2 3.0 %copy-start.8 = (f32[4,320]{1,0:T(4,128)S(1)}, f32[4,320]{1,0:T(4,128)}, u32[]{:S(2)}) copy-start(f32[4,320]{1,0:T(4,128)} %w_in_ref.7) | copy-start | bytes 15364
  25.1 5.2 %collective-permute-start.2 = (f32[2,320]{1,0:T(2,128)S(1)}, f32[2,320]{1,0:T(2,128)S(1)}, u32[]{:S(2)}, u32[]{:S(2)}) collective-permute-start(f32[2,320]{1,0:T(2,128)S(1)} %get-tuple-element.34.sum0_ref), channel_id=1, source_target_pairs={{0,4},{1,5},{2,6},{3,7},{4,0},{5,1},{6,2},{7,3},{8,12},{9,13},{10,... | collective-permute-start | bytes 7688 | tf_op jit(solution)/shard_map/ppermute | solution.py:373
  26.6 3.7 %collective-permute-start.1 = (f32[2,320]{1,0:T(2,128)S(1)}, f32[2,320]{1,0:T(2,128)S(1)}, u32[]{:S(2)}, u32[]{:S(2)}) collective-permute-start(f32[2,320]{1,0:T(2,128)S(1)} %get-tuple-element.34.sum0_ref), channel_id=1, source_target_pairs={{0,6},{1,7},{2,0},{3,1},{4,2},{5,3},{6,4},{7,5},{8,14},{9,15},{10,... | collective-permute-start | bytes 7688 | tf_op jit(solution)/shard_map/ppermute | solution.py:373
  28.4 4.8 %collective-permute-start = (f32[2,320]{1,0:T(2,128)S(1)}, f32[2,320]{1,0:T(2,128)S(1)}, u32[]{:S(2)}, u32[]{:S(2)}) collective-permute-start(f32[2,320]{1,0:T(2,128)S(1)} %get-tuple-element.34.sum0_ref), channel_id=1, source_target_pairs={{0,2},{1,3},{2,4},{3,5},{4,6},{5,7},{6,0},{7,1},{8,10},{9,11},{10,... | collective-permute-start | bytes 7688 | tf_op jit(solution)/shard_map/ppermute | solution.py:373
  38.1 5.2 %collective-permute-start.5 = (f32[2,320]{1,0:T(2,128)S(1)}, f32[2,320]{1,0:T(2,128)S(1)}, u32[]{:S(2)}, u32[]{:S(2)}) collective-permute-start(f32[2,320]{1,0:T(2,128)S(1)} %get-tuple-element.37.sum0_ref), channel_id=1, source_target_pairs={{0,4},{1,5},{2,6},{3,7},{4,0},{5,1},{6,2},{7,3},{8,12},{9,13},{10,... | collective-permute-start | bytes 7688 | tf_op jit(solution)/shard_map/ppermute | solution.py:373
  38.2 5.1 %collective-permute-start.4 = (f32[2,320]{1,0:T(2,128)S(1)}, f32[2,320]{1,0:T(2,128)S(1)}, u32[]{:S(2)}, u32[]{:S(2)}) collective-permute-start(f32[2,320]{1,0:T(2,128)S(1)} %get-tuple-element.37.sum0_ref), channel_id=1, source_target_pairs={{0,6},{1,7},{2,0},{3,1},{4,2},{5,3},{6,4},{7,5},{8,14},{9,15},{10,... | collective-permute-start | bytes 7688 | tf_op jit(solution)/shard_map/ppermute | solution.py:373
  39.9 4.8 %collective-permute-start.3 = (f32[2,320]{1,0:T(2,128)S(1)}, f32[2,320]{1,0:T(2,128)S(1)}, u32[]{:S(2)}, u32[]{:S(2)}) collective-permute-start(f32[2,320]{1,0:T(2,128)S(1)} %get-tuple-element.37.sum0_ref), channel_id=1, source_target_pairs={{0,2},{1,3},{2,4},{3,5},{4,6},{5,7},{6,0},{7,1},{8,10},{9,11},{10,... | collective-permute-start | bytes 7688 | tf_op jit(solution)/shard_map/ppermute | solution.py:373
  45.6 12.1 %collective-permute-start.6 = (f32[8,640]{1,0:T(8,128)S(1)}, f32[8,640]{1,0:T(8,128)S(1)}, u32[]{:S(2)}, u32[]{:S(2)}) collective-permute-start(f32[8,640]{1,0:T(8,128)S(1)} %slice.16), channel_id=1, source_target_pairs={{0,8},{8,16},{16,24},{24,32},{32,40},{40,48},{48,56},{56,64},{64,7... | collective-permute-start | bytes 61448 | tf_op jit(solution)/shard_map/ppermute | solution.py:422
  47.5 10.2 %collective-permute-start.7 = (f32[4,640]{1,0:T(4,128)S(1)}, f32[4,640]{1,0:T(4,128)S(1)}, u32[]{:S(2)}, u32[]{:S(2)}) collective-permute-start(f32[4,640]{1,0:T(4,128)S(1)} %slice.17), channel_id=1, source_target_pairs={{0,16},{8,24},{16,32},{24,40},{32,48},{40,56},{48,64},{56,72},{64,... | collective-permute-start | bytes 30728 | tf_op jit(solution)/shard_map/ppermute | solution.py:423
  57.7 5.3 %collective-permute-start.10 = (f32[4,640]{1,0:T(4,128)S(1)}, f32[4,640]{1,0:T(4,128)S(1)}, u32[]{:S(2)}, u32[]{:S(2)}) collective-permute-start(f32[4,640]{1,0:T(4,128)S(1)} %merge.1.own_ref), channel_id=1, source_target_pairs={{0,4},{1,5},{2,6},{3,7},{4,0},{5,1},{6,2},{7,3},{8,12},{9,13},{10,... | collective-permute-start | bytes 30728 | tf_op jit(solution)/shard_map/ppermute | solution.py:373
  58.5 4.5 %collective-permute-start.9 = (f32[4,640]{1,0:T(4,128)S(1)}, f32[4,640]{1,0:T(4,128)S(1)}, u32[]{:S(2)}, u32[]{:S(2)}) collective-permute-start(f32[4,640]{1,0:T(4,128)S(1)} %merge.1.own_ref), channel_id=1, source_target_pairs={{0,6},{1,7},{2,0},{3,1},{4,2},{5,3},{6,4},{7,5},{8,14},{9,15},{10,... | collective-permute-start | bytes 30728 | tf_op jit(solution)/shard_map/ppermute | solution.py:373
  59.7 4.9 %collective-permute-start.8 = (f32[4,640]{1,0:T(4,128)S(1)}, f32[4,640]{1,0:T(4,128)S(1)}, u32[]{:S(2)}, u32[]{:S(2)}) collective-permute-start(f32[4,640]{1,0:T(4,128)S(1)} %merge.1.own_ref), channel_id=1, source_target_pairs={{0,2},{1,3},{2,4},{3,5},{4,6},{5,7},{6,0},{7,1},{8,10},{9,11},{10,... | collective-permute-start | bytes 30728 | tf_op jit(solution)/shard_map/ppermute | solution.py:373
  70.4 5.2 %collective-permute-start.13 = (f32[2,320]{1,0:T(2,128)S(1)}, f32[2,320]{1,0:T(2,128)S(1)}, u32[]{:S(2)}, u32[]{:S(2)}) collective-permute-start(f32[2,320]{1,0:T(2,128)S(1)} %get-tuple-element.42.sum0_ref), channel_id=1, source_target_pairs={{0,4},{1,5},{2,6},{3,7},{4,0},{5,1},{6,2},{7,3},{8,12},{9,13},{10,... | collective-permute-start | bytes 7688 | tf_op jit(solution)/shard_map/ppermute | solution.py:373
  71.5 4.1 %collective-permute-start.12 = (f32[2,320]{1,0:T(2,128)S(1)}, f32[2,320]{1,0:T(2,128)S(1)}, u32[]{:S(2)}, u32[]{:S(2)}) collective-permute-start(f32[2,320]{1,0:T(2,128)S(1)} %get-tuple-element.42.sum0_ref), channel_id=1, source_target_pairs={{0,6},{1,7},{2,0},{3,1},{4,2},{5,3},{6,4},{7,5},{8,14},{9,15},{10,... | collective-permute-start | bytes 7688 | tf_op jit(solution)/shard_map/ppermute | solution.py:373
  72.7 4.8 %collective-permute-start.11 = (f32[2,320]{1,0:T(2,128)S(1)}, f32[2,320]{1,0:T(2,128)S(1)}, u32[]{:S(2)}, u32[]{:S(2)}) collective-permute-start(f32[2,320]{1,0:T(2,128)S(1)} %get-tuple-element.42.sum0_ref), channel_id=1, source_target_pairs={{0,2},{1,3},{2,4},{3,5},{4,6},{5,7},{6,0},{7,1},{8,10},{9,11},{10,... | collective-permute-start | bytes 7688 | tf_op jit(solution)/shard_map/ppermute | solution.py:373
  82.5 5.2 %collective-permute-start.16 = (f32[2,320]{1,0:T(2,128)S(1)}, f32[2,320]{1,0:T(2,128)S(1)}, u32[]{:S(2)}, u32[]{:S(2)}) collective-permute-start(f32[2,320]{1,0:T(2,128)S(1)} %get-tuple-element.44.sum0_ref), channel_id=1, source_target_pairs={{0,4},{1,5},{2,6},{3,7},{4,0},{5,1},{6,2},{7,3},{8,12},{9,13},{10,... | collective-permute-start | bytes 7688 | tf_op jit(solution)/shard_map/ppermute | solution.py:373
  83.0 4.6 %collective-permute-start.15 = (f32[2,320]{1,0:T(2,128)S(1)}, f32[2,320]{1,0:T(2,128)S(1)}, u32[]{:S(2)}, u32[]{:S(2)}) collective-permute-start(f32[2,320]{1,0:T(2,128)S(1)} %get-tuple-element.44.sum0_ref), channel_id=1, source_target_pairs={{0,6},{1,7},{2,0},{3,1},{4,2},{5,3},{6,4},{7,5},{8,14},{9,15},{10,... | collective-permute-start | bytes 7688 | tf_op jit(solution)/shard_map/ppermute | solution.py:373
  84.8 4.8 %collective-permute-start.14 = (f32[2,320]{1,0:T(2,128)S(1)}, f32[2,320]{1,0:T(2,128)S(1)}, u32[]{:S(2)}, u32[]{:S(2)}) collective-permute-start(f32[2,320]{1,0:T(2,128)S(1)} %get-tuple-element.44.sum0_ref), channel_id=1, source_target_pairs={{0,2},{1,3},{2,4},{3,5},{4,6},{5,7},{6,0},{7,1},{8,10},{9,11},{10,... | collective-permute-start | bytes 7688 | tf_op jit(solution)/shard_map/ppermute | solution.py:373
  90.2 4.3 %collective-permute-start.18 = (f32[4,320]{1,0:T(4,128)S(1)}, f32[4,320]{1,0:T(4,128)S(1)}, u32[]{:S(2)}, u32[]{:S(2)}) collective-permute-start(f32[4,320]{1,0:T(4,128)S(1)} %get-tuple-element.45), channel_id=1, source_target_pairs={{8,0},{16,8},{24,16},{32,24},{40,32},{48,40},{56,48},{64,56},{72,6... | collective-permute-start | bytes 15368 | tf_op jit(solution)/shard_map/ppermute | solution.py:417
  92.1 7.1 %collective-permute-start.17 = (f32[4,320]{1,0:T(4,128)S(1)}, f32[4,320]{1,0:T(4,128)S(1)}, u32[]{:S(2)}, u32[]{:S(2)}) collective-permute-start(f32[4,320]{1,0:T(4,128)S(1)} %get-tuple-element.46), channel_id=1, source_target_pairs={{0,8},{8,16},{16,24},{24,32},{32,40},{40,48},{48,56},{56,64},{64,7... | collective-permute-start | bytes 15368 | tf_op jit(solution)/shard_map/ppermute | solution.py:416

commit v4 on v3

--- a/solution.py
+++ b/solution.py
@@ -128,20 +128,19 @@
 
 
 def setup_kernel(
-    frame_ref, step_ref, plan_ref, harmonic_ref, w_out_ref, time_ref, temporal_ref, one_ref,
-    two_ref, own_ref, before_ref, after_ref, across_ref, new_ref, coef_ref, emb_ref, fold_ref,
-    first_ref, second_ref,
+    frame_ref, step_ref, plan_ref, harmonic_ref, time_ref, raw_ref, own_ref, flip1_ref, flip3_ref,
+    flip2_ref, new_ref, coef_ref, emb_ref, first_ref,
 ):
     strip = lax.axis_index("band") >> 1
 
-    def piece(ahead, row):
-        at = 2 * ((strip + ahead) & 3)
+    def piece(flip, row):
+        at = 2 * (strip ^ flip)
         return jnp.concatenate(
             [frame_ref[at, row : row + 4, :], frame_ref[at + 1, row : row + 4, :]], axis=1
         )
 
-    for ref, ahead in ((own_ref, 0), (before_ref, 3), (after_ref, 1), (across_ref, 2)):
-        ref[...] = piece(ahead, 0)
+    for ref, flip in ((own_ref, 0), (flip1_ref, 1), (flip3_ref, 3), (flip2_ref, 2)):
+        ref[...] = piece(flip, 0)
     new_ref[...] = piece(0, 4)
     step = step_ref[...].astype(jnp.int32)
     plan = plan_ref[...]
@@ -160,11 +159,15 @@
     noise = jnp.sqrt(1.0 - prev) - ratio * jnp.sqrt(1.0 - now)
     coef_ref[0:1] = jnp.broadcast_to(ratio, (1, 128))
     coef_ref[1:2] = jnp.broadcast_to(noise, (1, 128))
-    for raw, ref in ((one_ref, first_ref), (two_ref, second_ref)):
-        for r in range(3):
-            put_right(ref, r, raw.at[r])
+    for r in range(3):
+        put_right(first_ref, r, raw_ref.at[r])
     harmonic = jnp.broadcast_to(harmonic_ref[...], (8, 320))
     emb_ref[...] = silu(product(harmonic, time_ref[...], ((1,), (0,)))[0:1])
+
+
+def setup_second_kernel(after_ref, w_out_ref, temporal_ref, raw_ref, fold_ref, second_ref):
+    for r in range(3):
+        put_right(second_ref, r, raw_ref.at[r])
     w_out = jnp.concatenate([w_out_ref[...], w_out_ref[...] * 0.0], axis=0)
     for row, tap in enumerate((1, 0, 2)):
         fold = product(w_out, temporal_ref[tap], ((1,), (1,)))
@@ -172,19 +175,18 @@
     fold_ref[12:16] = jnp.zeros((4, 320), F32)
 
 
-def setup(*operands):
-    shapes = (
-        *[((4, 640), F32)] * 5, ((2, 128), F32), ((1, 320), F32), ((16, 320), F32),
-        ((3, 1024, 960), BF16), ((3, 1024, 960), BF16),
-    )
+def setup(kernel, specs, shapes, operands, name):
     return pl.pallas_call(
-        setup_kernel,
-        in_specs=[VMEM] * len(operands),
-        out_specs=[VMEM] * len(shapes),
-        out_shape=[jax.ShapeDtypeStruct(*shape) for shape in shapes],
+        kernel,
+        in_specs=specs,
+        out_specs=[VMEM] * (len(shapes) + 1),
+        out_shape=[
+            *[jax.ShapeDtypeStruct(shape, F32) for shape in shapes],
+            jax.ShapeDtypeStruct((3, 1024, 960), BF16),
+        ],
         compiler_params=pltpu.CompilerParams(vmem_limit_bytes=LIMIT),
-        cost_estimate=pl.CostEstimate(flops=0, bytes_accessed=20_000_000, transcendentals=0),
-        name="setup",
+        cost_estimate=pl.CostEstimate(flops=0, bytes_accessed=10_000_000, transcendentals=0),
+        name=name,
     )(*operands)
 
 
@@ -220,11 +222,11 @@
 
 
 def conv1_kernel(
-    members, own_ref, before_ref, after_ref, across_ref, w_in_ref, emb_ref, w_ref, mid_ref, stat_ref,
+    members, own_ref, flip1_ref, flip3_ref, flip2_ref, w_in_ref, emb_ref, w_ref, mid_ref, stat_ref,
     a_ref, acc_ref, lift_ref,
 ):
     strip = lax.axis_index("band") >> 1
-    pieces = [ref[...] for ref in (own_ref, before_ref, after_ref, across_ref)]
+    pieces = [ref[...] for ref in (own_ref, flip1_ref, flip3_ref, flip2_ref)]
     w = w_in_ref[...]
     average = 1.0 / members
     mean = jnp.sum(sum(pieces), axis=1, keepdims=True) * average
@@ -235,7 +237,10 @@
         moment = jnp.sum(moment, axis=1, keepdims=True) * average
         square += w[j : j + 1] * jnp.sum(moment * w, axis=0, keepdims=True)
     center, factor = center_factor(jnp.concatenate([mean, square], axis=0))
-    around = jnp.concatenate([pieces[1][:, 512:640], pieces[0], pieces[2][:, 0:128]], axis=1)
+    odd = (strip & 1) == 1
+    before = jnp.where(odd, pieces[1][:, 512:640], pieces[2][:, 512:640])
+    after = jnp.where(odd, pieces[2][:, 0:128], pieces[1][:, 0:128])
+    around = jnp.concatenate([before, pieces[0], after], axis=1)
     lift_ref[...] = lift(around, w)
     for i in range(14):
         rows = slice(64 * i, 64 * i + 64)
@@ -310,8 +315,9 @@
     noise = coef_ref[1:2, 0:1]
     out_ref[0:4] = ratio * own + noise * local
     out_ref[4:8] = jnp.broadcast_to(noise, (4, out_ref.shape[1]))
-    out_ref[8:12] = from_act[4:8]
-    out_ref[12:16] = from_act[8:12]
+    even = (lax.axis_index("level") & 1) == 0 if last else True
+    out_ref[8:12] = jnp.where(even, from_act[4:8], from_act[8:12])
+    out_ref[12:16] = jnp.where(even, from_act[8:12], from_act[4:8])
 
 
 def merge_kernel(parts_ref, one_ref, two_ref, fresh_ref, own_ref):
@@ -319,8 +325,8 @@
     own_ref[...] = jnp.where(lax.axis_index("level") == 0, fresh_ref[...], moved)
 
 
-def finish_kernel(parts_ref, below_ref, above_ref, out_ref):
-    own = parts_ref[0:4] + parts_ref[4:8] * (below_ref[...] + above_ref[...])
+def finish_kernel(parts_ref, core_ref, chip_ref, out_ref):
+    own = parts_ref[0:4] + parts_ref[4:8] * (core_ref[...] + chip_ref[...])
     for r in range(5):
         out_ref[0, r] = own[:, 64 * r : 64 * r + 64]
 
@@ -370,9 +376,18 @@
 def around_strip(value):
     bands = lax.axis_size("band")
     return [value] + [
-        lax.ppermute(value, "band", [(i, (i + 2 * k) % bands) for i in range(bands)])
-        for k in (1, 3, 2)
+        lax.ppermute(value, "band", [(i, i ^ (2 * flip)) for i in range(bands)])
+        for flip in (1, 3, 2)
     ]
+
+
+def swap_slots(to_core, to_chip):
+    levels = lax.axis_size("level")
+    across = [(i, i + 1) for i in range(1, levels - 1, 2)]
+    across = across + [(j, i) for i, j in across]
+    from_core = lax.ppermute(to_core, "level", [(i, i ^ 1) for i in range(levels)])
+    from_chip = lax.ppermute(to_chip, "level", across)
+    return from_core, from_chip
 
 
 def on_device(latents, timesteps, fresh, w_in, conv_first, conv_second, w_time, temporal, w_out):
@@ -390,8 +405,9 @@
         "spread", pl.CostEstimate(flops=8_000_000_000, bytes_accessed=40_000, transcendentals=0),
     )
     frame = lax.all_to_all(spread, "band", 0, 0, tiled=True)
-    *pieces, new, coef, embedded, folded, first_ready, second_ready = setup(
-        frame, step, plan, harmonic, out_rows, w_time, temporal, conv_first, conv_second
+    *pieces, new, coef, embedded, first_ready = setup(
+        setup_kernel, [VMEM] * 6, [*[(4, 2 * positions)] * 5, (2, 128), (1, 320)],
+        (frame, step, plan, harmonic, w_time, conv_first), "setup_first",
     )
     for iteration in range(ITERS):
         last = iteration + 1 == ITERS
@@ -400,6 +416,11 @@
             (*pieces, w_in, embedded, first_ready),
             14, 12, [pltpu.VMEM((896, 320), F32)], "conv_one",
         )
+        if iteration == 0:
+            folded, second_ready = setup(
+                setup_second_kernel, [ANY] + [VMEM] * 3, [(16, 320)],
+                (stats, out_rows, temporal, conv_second), "setup_second",
+            )
         hidden, stats = conv_call(
             functools.partial(conv2_kernel, members),
             (middle, *around_strip(stats), pieces[0], w_in, second_ready),
@@ -411,12 +432,9 @@
             (hidden, *around_strip(stats), pieces[0], out_rows, folded, coef), "project",
         )
         if last:
-            up = [(i, i + 1) for i in range(levels - 1)]
-            down = [(j, i) for i, j in up]
-            below = lax.ppermute(parts[8:12], "level", up)
-            above = lax.ppermute(parts[12:16], "level", down)
             (out,) = call(
-                finish_kernel, [VMEM] * 3, [(1, 5, 4, 64)], (parts, below, above), "finish"
+                finish_kernel, [VMEM] * 3, [(1, 5, 4, 64)],
+                (parts, *swap_slots(parts[8:12], parts[12:16])), "finish",
             )
         else:
             one = lax.ppermute(parts[0:8], "level", [(i, i + 1) for i in range(levels - 1)])

time: 100 us -> 95.1 us (0.951)
  waiting for transfers between devices: 32.6 us -> 26.1 us
  starting transfers between devices: 24.3 us -> 25.8 us
    ppermute x17, waiting for transfers between devices: 26.3 us -> 19.7 us  [the longest x15 14.7 us: around_strip(): lax.ppermute(value, 'band', [(i, i ^ 2 * flip) for i in range(bands)])]
    ppermute x17, starting transfers between devices: 18.5 us -> 20.1 us  [the longest x15 18.1 us: around_strip(): lax.ppermute(value, 'band', [(i, i ^ 2 * flip) for i in range(bands)])]
    pallas_call x1 -> x2, Pallas kernels: 3 us -> 2.88 us  [setup(): pl.pallas_call(kernel, in_specs=specs, out_specs=[VMEM] * (len(shapes) +...]
  transfers between devices with their start and end apart: 19 -> 19, of which waited for: 12 -> 17; matrix products, arithmetic and copies ran while one was open for 0% -> 0% of each run, Pallas kernels for 0% -> 2%
where the time goes in v4:
time: 95.1 us; the launch traced here: 94.8 us
  Pallas kernels  26.5 us (28%)
  waiting for transfers between devices  26.1 us (27%)
  starting transfers between devices  25.8 us (27%)
  blocking collectives  13.9 us (15%)
  local copies, waits for them, and re-layouts  1.47 us (2%)
    pallas_call x4, Pallas kernels, conv_call(): pl.pallas_call(kernel, in_specs=[VMEM] * len(operands), out_specs=[VMEM,...  21.4 us
    ppermute x15, starting transfers between devices, around_strip(): lax.ppermute(value, 'band', [(i, i ^ 2 * flip) for i in range(bands)])  18.1 us
    ppermute x15, waiting for transfers between devices, around_strip(): lax.ppermute(value, 'band', [(i, i ^ 2 * flip) for i in range(bands)])  14.7 us
    all_to_all x1, blocking collectives, on_device(): frame = lax.all_to_all(spread, 'band', 0, 0, tiled=True)  13.9 us
    ppermute x1, waiting for transfers between devices, on_device(): lax.ppermute(parts[8:12], 'level', [(i, i + 2) for i in range(levels - 2)])  6.36 us
    ppermute x1, waiting for transfers between devices, swap_slots(): from_chip = lax.ppermute(to_chip, 'level', across)  5.03 us
    ppermute x1, starting transfers between devices, on_device(): lax.ppermute(parts[8:12], 'level', [(i, i + 2) for i in range(levels - 2)])  3.82 us
    pallas_call x2, Pallas kernels, setup(): pl.pallas_call(kernel, in_specs=specs, out_specs=[VMEM] * (len(shapes) +...  2.88 us
  transfers between devices with their start and end apart: 19, of which 17 were waited for; matrix products, arithmetic and copies ran while one was open for 0% of the time, Pallas kernels for 2%

profile of v4, /device:TPU:8, one launch (start us, length us, event | category | flops | bytes accessed | tf_op | source)
XLA Modules:
  0.0 94.8 jit_solution(3714690793818983509)
XLA Ops:
  2.3 13.9 %all_to_all.5.frame_ref = f32[8,8,320]{2,1,0:T(8,128)S(1)} all-to-all(f32[8,8,320]{2,1,0:T(8,128)S(1)} %get-tuple-element.25), channel_id=1, replica_groups=mesh['level'=32,'band'=8] {'band'}, dimensions={0} | all-to-all | bytes 163840 | tf_op jit(solution)/shard_map/all_to_all | solution.py:407
  16.2 1.5 %setup_first.1 = (f32[4,640]{1,0:T(4,128)S(1)}, f32[4,640]{1,0:T(4,128)S(1)}, f32[4,640]{1,0:T(4,128)S(1)}, f32[4,640]{1,0:T(4,128)S(1)}, f32[4,640]{1,0:T(4,128...) custom-call(f32[8,8,320]{2,1,0:T(8,128)S(1)} %all_to_all.5.frame_ref, ...), custom_call_target="tpu_custom_call" | custom-call | bytes 10000000 | tf_op jit(solution)/shard_map/setup_first/pallas_call | solution.py:179
  17.7 5.8 %conv_one.2 = (f32[768,320]{1,0:T(8,128)S(1)}, f32[2,320]{1,0:T(2,128)S(1)}) custom-call(f32[4,640]{1,0:T(4,128)S(1)} %get-tuple-element.27.own_ref, f32[4,640]{1,0:T(4,128)S(1)} %get-tuple-element.28.flip1_ref, f32[4,640]{1,0:T(4,128)S(1)} %get-tuple-element.29.flip3_ref, f32[4,640]{1,0:T(4,128)S(1)} %get-tuple-element.30.flip2_ref, ...), custom_call_target="tpu_custom_call" | custom-call | flops 4246732800 | bytes 4000000 | tf_op jit(solution)/shard_map/conv_one/pallas_call | solution.py:341
  23.5 1.5 %collective-permute-start.2 = (f32[2,320]{1,0:T(2,128)S(1)}, f32[2,320]{1,0:T(2,128)S(1)}, u32[]{:S(2)}, u32[]{:S(2)}) collective-permute-start(f32[2,320]{1,0:T(2,128)S(1)} %get-tuple-element.34.after_ref.sum0_ref), channel_id=1, source_target_pairs={{0,4},{1,5},{2,6},{3,7},{4,0},{5,1},{6,2},{7,3},{8,12},{9,13},{10,... | collective-permute-start | bytes 7688 | tf_op jit(solution)/shard_map/ppermute | solution.py:379
  25.0 1.8 %collective-permute-start.1 = (f32[2,320]{1,0:T(2,128)S(1)}, f32[2,320]{1,0:T(2,128)S(1)}, u32[]{:S(2)}, u32[]{:S(2)}) collective-permute-start(f32[2,320]{1,0:T(2,128)S(1)} %get-tuple-element.34.after_ref.sum0_ref), channel_id=1, source_target_pairs={{0,6},{1,7},{2,4},{3,5},{4,2},{5,3},{6,0},{7,1},{8,14},{9,15},{10,... | collective-permute-start | bytes 7688 | tf_op jit(solution)/shard_map/ppermute | solution.py:379
  27.1 1.4 %setup_second.1 = (f32[16,320]{1,0:T(8,128)S(1)}, bf16[3,1024,960]{2,1,0:T(8,128)(2,1)S(1)}) custom-call(f32[2,320]{1,0:T(2,128)S(1)} %get-tuple-element.34.after_ref.sum0_ref, f32[4,320]{1,0:T(4,128)S(1)} %bitcast.7, f32[3,320,320]{2,1,0:T(8,128)S(1)} %copy-done.1, f32[3,3,320,320]{3,2,1,0:T(8,128)S(1)} %bitcast.6), custom_call_target="tpu_custom_call" | custom-call | bytes 10000000 | tf_op jit(solution)/shard_map/setup_second/pallas_call | solution.py:179
  28.7 1.1 %collective-permute-done.1.sum2_ref = f32[2,320]{1,0:T(2,128)S(1)} collective-permute-done((f32[2,320]{1,0:T(2,128)S(1)}, f32[2,320]{1,0:T(2,128)S(1)}, u32[]{:S(2)}, u32[]{:S(2)}) %collective-permute-start.1) | collective-permute-done | bytes 2592 | tf_op jit(solution)/shard_map/ppermute | solution.py:379
  30.4 4.9 %conv_two.2 = (f32[640,320]{1,0:T(8,128)S(1)}, f32[2,320]{1,0:T(2,128)S(1)}) custom-call(f32[768,320]{1,0:T(8,128)S(1)} %get-tuple-element.33.mid_ref, f32[2,320]{1,0:T(2,128)S(1)} %get-tuple-element.34.after_ref.sum0_ref, f32[2,320]{1,0:T(2,128)S(1)} %collective-permute-done.sum1_ref, f32[2,320]{1,0:T(2,128)S(1)} %collective-permute-done.1.sum2_ref, ...), custom_call_target="tpu_custom_call" | custom-call | flops 3538944000 | bytes 4000000 | tf_op jit(solution)/shard_map/conv_two/pallas_call | solution.py:341
  35.4 1.1 %collective-permute-start.5 = (f32[2,320]{1,0:T(2,128)S(1)}, f32[2,320]{1,0:T(2,128)S(1)}, u32[]{:S(2)}, u32[]{:S(2)}) collective-permute-start(f32[2,320]{1,0:T(2,128)S(1)} %get-tuple-element.37.sum0_ref), channel_id=1, source_target_pairs={{0,4},{1,5},{2,6},{3,7},{4,0},{5,1},{6,2},{7,3},{8,12},{9,13},{10,... | collective-permute-start | bytes 7688 | tf_op jit(solution)/shard_map/ppermute | solution.py:379
  36.5 2.1 %collective-permute-start.4 = (f32[2,320]{1,0:T(2,128)S(1)}, f32[2,320]{1,0:T(2,128)S(1)}, u32[]{:S(2)}, u32[]{:S(2)}) collective-permute-start(f32[2,320]{1,0:T(2,128)S(1)} %get-tuple-element.37.sum0_ref), channel_id=1, source_target_pairs={{0,6},{1,7},{2,4},{3,5},{4,2},{5,3},{6,0},{7,1},{8,14},{9,15},{10,... | collective-permute-start | bytes 7688 | tf_op jit(solution)/shard_map/ppermute | solution.py:379
  39.1 1.6 %collective-permute-done.5.sum3_ref = f32[2,320]{1,0:T(2,128)S(1)} collective-permute-done((f32[2,320]{1,0:T(2,128)S(1)}, f32[2,320]{1,0:T(2,128)S(1)}, u32[]{:S(2)}, u32[]{:S(2)}) %collective-permute-start.5) | collective-permute-done | bytes 2592 | tf_op jit(solution)/shard_map/ppermute | solution.py:379
  41.3 0.8 collective-permute-done.3.sum1_ref
  42.2 0.9 project.2.parts_ref
  43.0 1.9 %collective-permute-start.6 = (f32[8,640]{1,0:T(8,128)S(1)}, f32[8,640]{1,0:T(8,128)S(1)}, u32[]{:S(2)}, u32[]{:S(2)}) collective-permute-start(f32[8,640]{1,0:T(8,128)S(1)} %slice.16), channel_id=1, source_target_pairs={{0,8},{8,16},{16,24},{24,32},{32,40},{40,48},{48,56},{56,64},{64,7... | collective-permute-start | bytes 61448 | tf_op jit(solution)/shard_map/ppermute | solution.py:440
  45.0 3.8 %collective-permute-start.7 = (f32[4,640]{1,0:T(4,128)S(1)}, f32[4,640]{1,0:T(4,128)S(1)}, u32[]{:S(2)}, u32[]{:S(2)}) collective-permute-start(f32[4,640]{1,0:T(4,128)S(1)} %slice.17), channel_id=1, source_target_pairs={{0,16},{8,24},{16,32},{24,40},{32,48},{40,56},{48,64},{56,72},{64,... | collective-permute-start | bytes 30728 | tf_op jit(solution)/shard_map/ppermute | solution.py:441
  48.8 6.4 %collective-permute-done.7.two_ref = f32[4,640]{1,0:T(4,128)S(1)} collective-permute-done((f32[4,640]{1,0:T(4,128)S(1)}, f32[4,640]{1,0:T(4,128)S(1)}, u32[]{:S(2)}, u32[]{:S(2)}) %collective-permute-start.7) | collective-permute-done | bytes 10272 | tf_op jit(solution)/shard_map/ppermute | solution.py:441
  55.2 1.5 %collective-permute-start.10 = (f32[4,640]{1,0:T(4,128)S(1)}, f32[4,640]{1,0:T(4,128)S(1)}, u32[]{:S(2)}, u32[]{:S(2)}) collective-permute-start(f32[4,640]{1,0:T(4,128)S(1)} %merge.1.own_ref), channel_id=1, source_target_pairs={{0,4},{1,5},{2,6},{3,7},{4,0},{5,1},{6,2},{7,3},{8,12},{9,13},{10,... | collective-permute-start | bytes 30728 | tf_op jit(solution)/shard_map/ppermute | solution.py:379
  56.7 1.8 %collective-permute-start.9 = (f32[4,640]{1,0:T(4,128)S(1)}, f32[4,640]{1,0:T(4,128)S(1)}, u32[]{:S(2)}, u32[]{:S(2)}) collective-permute-start(f32[4,640]{1,0:T(4,128)S(1)} %merge.1.own_ref), channel_id=1, source_target_pairs={{0,6},{1,7},{2,4},{3,5},{4,2},{5,3},{6,0},{7,1},{8,14},{9,15},{10,... | collective-permute-start | bytes 30728 | tf_op jit(solution)/shard_map/ppermute | solution.py:379
  58.7 1.7 %collective-permute-done.10.flip2_ref = f32[4,640]{1,0:T(4,128)S(1)} collective-permute-done((f32[4,640]{1,0:T(4,128)S(1)}, f32[4,640]{1,0:T(4,128)S(1)}, u32[]{:S(2)}, u32[]{:S(2)}) %collective-permute-start.10) | collective-permute-done | bytes 10272 | tf_op jit(solution)/shard_map/ppermute | solution.py:379
  60.4 1.1 %collective-permute-done.9.flip3_ref = f32[4,640]{1,0:T(4,128)S(1)} collective-permute-done((f32[4,640]{1,0:T(4,128)S(1)}, f32[4,640]{1,0:T(4,128)S(1)}, u32[]{:S(2)}, u32[]{:S(2)}) %collective-permute-start.9) | collective-permute-done | bytes 10272 | tf_op jit(solution)/shard_map/ppermute | solution.py:379
  62.2 5.8 %conv_one.3 = (f32[768,320]{1,0:T(8,128)S(1)}, f32[2,320]{1,0:T(2,128)S(1)}) custom-call(f32[4,640]{1,0:T(4,128)S(1)} %merge.1.own_ref, f32[4,640]{1,0:T(4,128)S(1)} %collective-permute-done.8.flip1_ref, f32[4,640]{1,0:T(4,128)S(1)} %collective-permute-done.9.flip3_ref, f32[4,640]{1,0:T(4,128)S(1)} %collective-permute-done.10.flip2_ref, ...), custom_call_target="tpu_custom_call" | custom-call | flops 4246732800 | bytes 4000000 | tf_op jit(solution)/shard_map/conv_one/pallas_call | solution.py:341
  68.0 1.0 %collective-permute-start.13 = (f32[2,320]{1,0:T(2,128)S(1)}, f32[2,320]{1,0:T(2,128)S(1)}, u32[]{:S(2)}, u32[]{:S(2)}) collective-permute-start(f32[2,320]{1,0:T(2,128)S(1)} %get-tuple-element.42.sum0_ref), channel_id=1, source_target_pairs={{0,4},{1,5},{2,6},{3,7},{4,0},{5,1},{6,2},{7,3},{8,12},{9,13},{10,... | collective-permute-start | bytes 7688 | tf_op jit(solution)/shard_map/ppermute | solution.py:379
  69.0 2.0 %collective-permute-start.12 = (f32[2,320]{1,0:T(2,128)S(1)}, f32[2,320]{1,0:T(2,128)S(1)}, u32[]{:S(2)}, u32[]{:S(2)}) collective-permute-start(f32[2,320]{1,0:T(2,128)S(1)} %get-tuple-element.42.sum0_ref), channel_id=1, source_target_pairs={{0,6},{1,7},{2,4},{3,5},{4,2},{5,3},{6,0},{7,1},{8,14},{9,15},{10,... | collective-permute-start | bytes 7688 | tf_op jit(solution)/shard_map/ppermute | solution.py:379
  71.5 1.6 %collective-permute-done.13.sum3_ref = f32[2,320]{1,0:T(2,128)S(1)} collective-permute-done((f32[2,320]{1,0:T(2,128)S(1)}, f32[2,320]{1,0:T(2,128)S(1)}, u32[]{:S(2)}, u32[]{:S(2)}) %collective-permute-start.13) | collective-permute-done | bytes 2592 | tf_op jit(solution)/shard_map/ppermute | solution.py:379
  73.8 0.8 collective-permute-done.11.sum1_ref
  74.6 4.9 %conv_two.3 = (f32[640,320]{1,0:T(8,128)S(1)}, f32[2,320]{1,0:T(2,128)S(1)}) custom-call(f32[768,320]{1,0:T(8,128)S(1)} %get-tuple-element.41.mid_ref, f32[2,320]{1,0:T(2,128)S(1)} %get-tuple-element.42.sum0_ref, f32[2,320]{1,0:T(2,128)S(1)} %collective-permute-done.11.sum1_ref, f32[2,320]{1,0:T(2,128)S(1)} %collective-permute-done.12.sum2_ref, ...), custom_call_target="tpu_custom_call" | custom-call | flops 3538944000 | bytes 4000000 | tf_op jit(solution)/shard_map/conv_two/pallas_call | solution.py:341
  79.5 1.5 %collective-permute-start.16 = (f32[2,320]{1,0:T(2,128)S(1)}, f32[2,320]{1,0:T(2,128)S(1)}, u32[]{:S(2)}, u32[]{:S(2)}) collective-permute-start(f32[2,320]{1,0:T(2,128)S(1)} %get-tuple-element.44.sum0_ref), channel_id=1, source_target_pairs={{0,4},{1,5},{2,6},{3,7},{4,0},{5,1},{6,2},{7,3},{8,12},{9,13},{10,... | collective-permute-start | bytes 7688 | tf_op jit(solution)/shard_map/ppermute | solution.py:379
  81.0 1.8 %collective-permute-start.15 = (f32[2,320]{1,0:T(2,128)S(1)}, f32[2,320]{1,0:T(2,128)S(1)}, u32[]{:S(2)}, u32[]{:S(2)}) collective-permute-start(f32[2,320]{1,0:T(2,128)S(1)} %get-tuple-element.44.sum0_ref), channel_id=1, source_target_pairs={{0,6},{1,7},{2,4},{3,5},{4,2},{5,3},{6,0},{7,1},{8,14},{9,15},{10,... | collective-permute-start | bytes 7688 | tf_op jit(solution)/shard_map/ppermute | solution.py:379
  83.1 1.6 %collective-permute-done.16.sum3_ref = f32[2,320]{1,0:T(2,128)S(1)} collective-permute-done((f32[2,320]{1,0:T(2,128)S(1)}, f32[2,320]{1,0:T(2,128)S(1)}, u32[]{:S(2)}, u32[]{:S(2)}) %collective-permute-start.16) | collective-permute-done | bytes 2592 | tf_op jit(solution)/shard_map/ppermute | solution.py:379
  84.7 1.1 %collective-permute-done.15.sum2_ref = f32[2,320]{1,0:T(2,128)S(1)} collective-permute-done((f32[2,320]{1,0:T(2,128)S(1)}, f32[2,320]{1,0:T(2,128)S(1)}, u32[]{:S(2)}, u32[]{:S(2)}) %collective-permute-start.15) | collective-permute-done | bytes 2592 | tf_op jit(solution)/shard_map/ppermute | solution.py:379
  87.0 1.9 %collective-permute-start.18 = (f32[4,320]{1,0:T(4,128)S(1)}, f32[4,320]{1,0:T(4,128)S(1)}, u32[]{:S(2)}, u32[]{:S(2)}) collective-permute-start(f32[4,320]{1,0:T(4,128)S(1)} %get-tuple-element.45), channel_id=1, source_target_pairs={{8,16},{24,32},{40,48},{56,64},{72,80},{88,96},{104,112},{120,128}... | collective-permute-start | bytes 15368 | tf_op jit(solution)/shard_map/ppermute | solution.py:389
  89.0 5.0 %collective-permute-done.18.chip_ref = f32[4,320]{1,0:T(4,128)S(1)} collective-permute-done((f32[4,320]{1,0:T(4,128)S(1)}, f32[4,320]{1,0:T(4,128)S(1)}, u32[]{:S(2)}, u32[]{:S(2)}) %collective-permute-start.18) | collective-permute-done | bytes 5152 | tf_op jit(solution)/shard_map/ppermute | solution.py:389
  (44 shorter events, 8.0 us)
Async XLA Ops:
  0.8 0.7 copy-start.5
  1.5 0.7 copy-start.6
  2.2 14.0 %copy-start = (f32[3,3,320,320]{3,2,1,0:T(8,128)S(1)}, f32[3,3,320,320]{3,2,1,0:T(8,128)}, u32[]{:S(2)}) copy-start(f32[3,3,320,320]{3,2,1,0:T(8,128)} %raw_ref.2) | copy-start | bytes 11059204
  2.2 14.0 %copy-start.2 = (f32[320,320]{1,0:T(8,128)S(1)}, f32[320,320]{1,0:T(8,128)}, u32[]{:S(2)}) copy-start(f32[320,320]{1,0:T(8,128)} %time_ref.1) | copy-start | bytes 1228804
  2.2 14.0 %copy-start.4 = (f32[8,128]{1,0:T(8,128)S(1)}, f32[8,128]{1,0:T(8,128)}, u32[]{:S(2)}) copy-start(f32[8,128]{1,0:T(8,128)} %constant.8.clone.plan_ref) | copy-start | bytes 12292
  2.3 15.4 %copy-start.7 = (f32[4,320]{1,0:T(4,128)S(1)}, f32[4,320]{1,0:T(4,128)}, u32[]{:S(2)}) copy-start(f32[4,320]{1,0:T(4,128)} %w_in_ref.7) | copy-start | bytes 15364
  16.2 10.9 %slice-start = ((s8[4423680]{0:T(1024)(128)(4,1)}), s8[4194304]{0:T(1024)(128)(4,1)S(1)}, s32[]{:S(2)}) async-start(s8[4423680]{0:T(1024)(128)(4,1)} %bitcast.5), calls=%async_computation.1 | async-start | bytes 8388608
  17.7 9.4 %slice-start.1 = ((s8[4423680]{0:T(1024)(128)(4,1)}), s8[229376]{0:T(1024)(128)(4,1)S(1)}, s32[]{:S(2)}) async-start(s8[4423680]{0:T(1024)(128)(4,1)} %bitcast.5), calls=%async_computation.2 | async-start | bytes 458752
  17.7 9.4 %copy-start.1 = (f32[3,320,320]{2,1,0:T(8,128)S(1)}, f32[3,320,320]{2,1,0:T(8,128)}, u32[]{:S(2)}) copy-start(f32[3,320,320]{2,1,0:T(8,128)} %temporal_ref.1) | copy-start | bytes 3686404
  17.7 9.4 %copy-start.3 = (f32[320,4]{0,1:T(4,128)S(1)}, f32[320,4]{0,1:T(4,128)}, u32[]{:S(2)}) copy-start(f32[320,4]{0,1:T(4,128)} %param.18) | copy-start | bytes 15364
  23.5 5.2 %collective-permute-start.2 = (f32[2,320]{1,0:T(2,128)S(1)}, f32[2,320]{1,0:T(2,128)S(1)}, u32[]{:S(2)}, u32[]{:S(2)}) collective-permute-start(f32[2,320]{1,0:T(2,128)S(1)} %get-tuple-element.34.after_ref.sum0_ref), channel_id=1, source_target_pairs={{0,4},{1,5},{2,6},{3,7},{4,0},{5,1},{6,2},{7,3},{8,12},{9,13},{10,... | collective-permute-start | bytes 7688 | tf_op jit(solution)/shard_map/ppermute | solution.py:379
  25.0 4.8 %collective-permute-start.1 = (f32[2,320]{1,0:T(2,128)S(1)}, f32[2,320]{1,0:T(2,128)S(1)}, u32[]{:S(2)}, u32[]{:S(2)}) collective-permute-start(f32[2,320]{1,0:T(2,128)S(1)} %get-tuple-element.34.after_ref.sum0_ref), channel_id=1, source_target_pairs={{0,6},{1,7},{2,4},{3,5},{4,2},{5,3},{6,0},{7,1},{8,14},{9,15},{10,... | collective-permute-start | bytes 7688 | tf_op jit(solution)/shard_map/ppermute | solution.py:379
  26.8 3.6 %collective-permute-start = (f32[2,320]{1,0:T(2,128)S(1)}, f32[2,320]{1,0:T(2,128)S(1)}, u32[]{:S(2)}, u32[]{:S(2)}) collective-permute-start(f32[2,320]{1,0:T(2,128)S(1)} %get-tuple-element.34.after_ref.sum0_ref), channel_id=1, source_target_pairs={{0,2},{1,3},{2,0},{3,1},{4,6},{5,7},{6,4},{7,5},{8,10},{9,11},{10,... | collective-permute-start | bytes 7688 | tf_op jit(solution)/shard_map/ppermute | solution.py:379
  35.4 5.4 %collective-permute-start.5 = (f32[2,320]{1,0:T(2,128)S(1)}, f32[2,320]{1,0:T(2,128)S(1)}, u32[]{:S(2)}, u32[]{:S(2)}) collective-permute-start(f32[2,320]{1,0:T(2,128)S(1)} %get-tuple-element.37.sum0_ref), channel_id=1, source_target_pairs={{0,4},{1,5},{2,6},{3,7},{4,0},{5,1},{6,2},{7,3},{8,12},{9,13},{10,... | collective-permute-start | bytes 7688 | tf_op jit(solution)/shard_map/ppermute | solution.py:379
  36.5 4.8 %collective-permute-start.4 = (f32[2,320]{1,0:T(2,128)S(1)}, f32[2,320]{1,0:T(2,128)S(1)}, u32[]{:S(2)}, u32[]{:S(2)}) collective-permute-start(f32[2,320]{1,0:T(2,128)S(1)} %get-tuple-element.37.sum0_ref), channel_id=1, source_target_pairs={{0,6},{1,7},{2,4},{3,5},{4,2},{5,3},{6,0},{7,1},{8,14},{9,15},{10,... | collective-permute-start | bytes 7688 | tf_op jit(solution)/shard_map/ppermute | solution.py:379
  38.6 3.6 %collective-permute-start.3 = (f32[2,320]{1,0:T(2,128)S(1)}, f32[2,320]{1,0:T(2,128)S(1)}, u32[]{:S(2)}, u32[]{:S(2)}) collective-permute-start(f32[2,320]{1,0:T(2,128)S(1)} %get-tuple-element.37.sum0_ref), channel_id=1, source_target_pairs={{0,2},{1,3},{2,0},{3,1},{4,6},{5,7},{6,4},{7,5},{8,10},{9,11},{10,... | collective-permute-start | bytes 7688 | tf_op jit(solution)/shard_map/ppermute | solution.py:379
  43.0 12.1 %collective-permute-start.6 = (f32[8,640]{1,0:T(8,128)S(1)}, f32[8,640]{1,0:T(8,128)S(1)}, u32[]{:S(2)}, u32[]{:S(2)}) collective-permute-start(f32[8,640]{1,0:T(8,128)S(1)} %slice.16), channel_id=1, source_target_pairs={{0,8},{8,16},{16,24},{24,32},{32,40},{40,48},{48,56},{56,64},{64,7... | collective-permute-start | bytes 61448 | tf_op jit(solution)/shard_map/ppermute | solution.py:440
  45.0 10.2 %collective-permute-start.7 = (f32[4,640]{1,0:T(4,128)S(1)}, f32[4,640]{1,0:T(4,128)S(1)}, u32[]{:S(2)}, u32[]{:S(2)}) collective-permute-start(f32[4,640]{1,0:T(4,128)S(1)} %slice.17), channel_id=1, source_target_pairs={{0,16},{8,24},{16,32},{24,40},{32,48},{40,56},{48,64},{56,72},{64,... | collective-permute-start | bytes 30728 | tf_op jit(solution)/shard_map/ppermute | solution.py:441
  55.2 5.3 %collective-permute-start.10 = (f32[4,640]{1,0:T(4,128)S(1)}, f32[4,640]{1,0:T(4,128)S(1)}, u32[]{:S(2)}, u32[]{:S(2)}) collective-permute-start(f32[4,640]{1,0:T(4,128)S(1)} %merge.1.own_ref), channel_id=1, source_target_pairs={{0,4},{1,5},{2,6},{3,7},{4,0},{5,1},{6,2},{7,3},{8,12},{9,13},{10,... | collective-permute-start | bytes 30728 | tf_op jit(solution)/shard_map/ppermute | solution.py:379
  56.7 4.9 %collective-permute-start.9 = (f32[4,640]{1,0:T(4,128)S(1)}, f32[4,640]{1,0:T(4,128)S(1)}, u32[]{:S(2)}, u32[]{:S(2)}) collective-permute-start(f32[4,640]{1,0:T(4,128)S(1)} %merge.1.own_ref), channel_id=1, source_target_pairs={{0,6},{1,7},{2,4},{3,5},{4,2},{5,3},{6,0},{7,1},{8,14},{9,15},{10,... | collective-permute-start | bytes 30728 | tf_op jit(solution)/shard_map/ppermute | solution.py:379
  58.5 3.7 %collective-permute-start.8 = (f32[4,640]{1,0:T(4,128)S(1)}, f32[4,640]{1,0:T(4,128)S(1)}, u32[]{:S(2)}, u32[]{:S(2)}) collective-permute-start(f32[4,640]{1,0:T(4,128)S(1)} %merge.1.own_ref), channel_id=1, source_target_pairs={{0,2},{1,3},{2,0},{3,1},{4,6},{5,7},{6,4},{7,5},{8,10},{9,11},{10,... | collective-permute-start | bytes 30728 | tf_op jit(solution)/shard_map/ppermute | solution.py:379
  68.0 5.2 %collective-permute-start.13 = (f32[2,320]{1,0:T(2,128)S(1)}, f32[2,320]{1,0:T(2,128)S(1)}, u32[]{:S(2)}, u32[]{:S(2)}) collective-permute-start(f32[2,320]{1,0:T(2,128)S(1)} %get-tuple-element.42.sum0_ref), channel_id=1, source_target_pairs={{0,4},{1,5},{2,6},{3,7},{4,0},{5,1},{6,2},{7,3},{8,12},{9,13},{10,... | collective-permute-start | bytes 7688 | tf_op jit(solution)/shard_map/ppermute | solution.py:379
  69.0 4.8 %collective-permute-start.12 = (f32[2,320]{1,0:T(2,128)S(1)}, f32[2,320]{1,0:T(2,128)S(1)}, u32[]{:S(2)}, u32[]{:S(2)}) collective-permute-start(f32[2,320]{1,0:T(2,128)S(1)} %get-tuple-element.42.sum0_ref), channel_id=1, source_target_pairs={{0,6},{1,7},{2,4},{3,5},{4,2},{5,3},{6,0},{7,1},{8,14},{9,15},{10,... | collective-permute-start | bytes 7688 | tf_op jit(solution)/shard_map/ppermute | solution.py:379
  71.0 3.6 %collective-permute-start.11 = (f32[2,320]{1,0:T(2,128)S(1)}, f32[2,320]{1,0:T(2,128)S(1)}, u32[]{:S(2)}, u32[]{:S(2)}) collective-permute-start(f32[2,320]{1,0:T(2,128)S(1)} %get-tuple-element.42.sum0_ref), channel_id=1, source_target_pairs={{0,2},{1,3},{2,0},{3,1},{4,6},{5,7},{6,4},{7,5},{8,10},{9,11},{10,... | collective-permute-start | bytes 7688 | tf_op jit(solution)/shard_map/ppermute | solution.py:379
  79.5 5.2 %collective-permute-start.16 = (f32[2,320]{1,0:T(2,128)S(1)}, f32[2,320]{1,0:T(2,128)S(1)}, u32[]{:S(2)}, u32[]{:S(2)}) collective-permute-start(f32[2,320]{1,0:T(2,128)S(1)} %get-tuple-element.44.sum0_ref), channel_id=1, source_target_pairs={{0,4},{1,5},{2,6},{3,7},{4,0},{5,1},{6,2},{7,3},{8,12},{9,13},{10,... | collective-permute-start | bytes 7688 | tf_op jit(solution)/shard_map/ppermute | solution.py:379
  81.0 4.8 %collective-permute-start.15 = (f32[2,320]{1,0:T(2,128)S(1)}, f32[2,320]{1,0:T(2,128)S(1)}, u32[]{:S(2)}, u32[]{:S(2)}) collective-permute-start(f32[2,320]{1,0:T(2,128)S(1)} %get-tuple-element.44.sum0_ref), channel_id=1, source_target_pairs={{0,6},{1,7},{2,4},{3,5},{4,2},{5,3},{6,0},{7,1},{8,14},{9,15},{10,... | collective-permute-start | bytes 7688 | tf_op jit(solution)/shard_map/ppermute | solution.py:379
  82.8 3.6 %collective-permute-start.14 = (f32[2,320]{1,0:T(2,128)S(1)}, f32[2,320]{1,0:T(2,128)S(1)}, u32[]{:S(2)}, u32[]{:S(2)}) collective-permute-start(f32[2,320]{1,0:T(2,128)S(1)} %get-tuple-element.44.sum0_ref), channel_id=1, source_target_pairs={{0,2},{1,3},{2,0},{3,1},{4,6},{5,7},{6,4},{7,5},{8,10},{9,11},{10,... | collective-permute-start | bytes 7688 | tf_op jit(solution)/shard_map/ppermute | solution.py:379
  87.0 7.1 %collective-permute-start.18 = (f32[4,320]{1,0:T(4,128)S(1)}, f32[4,320]{1,0:T(4,128)S(1)}, u32[]{:S(2)}, u32[]{:S(2)}) collective-permute-start(f32[4,320]{1,0:T(4,128)S(1)} %get-tuple-element.45), channel_id=1, source_target_pairs={{8,16},{24,32},{40,48},{56,64},{72,80},{88,96},{104,112},{120,128}... | collective-permute-start | bytes 15368 | tf_op jit(solution)/shard_map/ppermute | solution.py:389
  88.9 5.1 %collective-permute-start.17 = (f32[4,320]{1,0:T(4,128)S(1)}, f32[4,320]{1,0:T(4,128)S(1)}, u32[]{:S(2)}, u32[]{:S(2)}) collective-permute-start(f32[4,320]{1,0:T(4,128)S(1)} %get-tuple-element.46), channel_id=1, source_target_pairs={{0,8},{8,0},{16,24},{24,16},{32,40},{40,32},{48,56},{56,48},{64,72... | collective-permute-start | bytes 15368 | tf_op jit(solution)/shard_map/ppermute | solution.py:388

commit v5 on v4

--- a/solution.py
+++ b/solution.py
@@ -79,30 +79,45 @@
     return lax.dot_general(left, right, (((0,), (0,)), ((), ())), preferred_element_type=F32)
 
 
-def put_left(a_ref, rows, act):
+def put_left(a_ref, j, rows, act):
     hi, lo = halves(act)
-    a_ref[rows, 0:256] = hi[:, 0:256]
-    a_ref[rows, 256:512] = lo[:, 0:256]
-    a_ref[rows, 512:768] = hi[:, 0:256]
-    a_ref[rows, 768:896] = jnp.concatenate([hi[:, 256:320], lo[:, 256:320]], axis=1)
-    a_ref[rows, 896:1024] = jnp.concatenate([hi[:, 256:320], hi[:, 256:320] * 0.0], axis=1)
-
-
-def put_right(b_ref, tap, w_ref):
+    a_ref[j, rows, 0:256] = hi[:, 0:256]
+    a_ref[j, rows, 256:512] = lo[:, 0:256]
+    a_ref[j, rows, 512:768] = hi[:, 0:256]
+    a_ref[j, rows, 768:896] = jnp.concatenate([hi[:, 256:320], lo[:, 256:320]], axis=1)
+    a_ref[j, rows, 896:1024] = jnp.concatenate([hi[:, 256:320], hi[:, 256:320] * 0.0], axis=1)
+
+
+def put_pairs(a_ref, act_ref, pairs):
+    for t in range(pairs):
+        d0, d1, d2, d3 = (act_ref[128 * t + 64 * i : 128 * t + 64 * i + 64, :] for i in range(4))
+        for j, mixed in enumerate((d0 - d2, d1 + d2, d2 - d1, d1 - d3)):
+            put_left(a_ref, j, slice(64 * t, 64 * t + 64), mixed)
+
+
+def put_right(b_ref, raw_ref):
     for k in range(5):
-        hi, lo = zip(*[halves(w_ref[c, 64 * k : 64 * k + 64, :]) for c in range(3)])
-        if k < 4:
-            places = ((64 * k, hi), (256 + 64 * k, hi), (512 + 64 * k, lo))
-        else:
-            places = ((768, hi), (832, hi), (896, lo))
-        for at, part in places:
-            for c in range(3):
-                b_ref[tap, at : at + 64, 256 * c : 256 * c + 256] = part[c][:, 0:256]
-            b_ref[tap, at : at + 64, 768:896] = jnp.concatenate(
-                [part[0][:, 256:320], part[1][:, 256:320]], axis=1
-            )
-            b_ref[tap, at : at + 64, 896:960] = part[2][:, 256:320]
-    b_ref[tap, 960:1024, :] = jnp.zeros((64, 960), BF16)
+        taps = []
+        for c in range(3):
+            g0, g1, g2 = (raw_ref[r, c, 64 * k : 64 * k + 64, :] for r in range(3))
+            ends = (g0 + g2) * 0.5
+            middle = g1 * 0.5
+            taps.append((g0, ends + middle, ends - middle, g2))
+        for j in range(4):
+            hi, lo = zip(*[halves(tap[j]) for tap in taps])
+            if k < 4:
+                places = ((64 * k, hi), (256 + 64 * k, hi), (512 + 64 * k, lo))
+            else:
+                places = ((768, hi), (832, hi), (896, lo))
+            for at, part in places:
+                for c in range(3):
+                    b_ref[j, at : at + 64, 256 * c : 256 * c + 256] = part[c][:, 0:256]
+                b_ref[j, at : at + 64, 768:896] = jnp.concatenate(
+                    [part[0][:, 256:320], part[1][:, 256:320]], axis=1
+                )
+                b_ref[j, at : at + 64, 896:960] = part[2][:, 256:320]
+    for j in range(4):
+        b_ref[j, 960:1024, :] = jnp.zeros((64, 960), BF16)
 
 
 def product(left, right, dims):
@@ -117,10 +132,10 @@
 
 
 def spread_kernel(
-    steps_ref, latents_ref, fresh_ref, harmonic_ref, spread_ref, step_ref
+    steps_ref, frames_ref, harmonic_ref, spread_ref, step_ref
 ):
     rows = [
-        jnp.concatenate([ref[0, r] for r in range(5)], axis=1) for ref in (latents_ref, fresh_ref)
+        jnp.concatenate([frames_ref[i, r] for r in range(5)], axis=1) for i in range(2)
     ]
     both = jnp.concatenate(rows, axis=0)
     spread_ref[...] = jnp.broadcast_to(both[None], spread_ref.shape)
@@ -159,15 +174,13 @@
     noise = jnp.sqrt(1.0 - prev) - ratio * jnp.sqrt(1.0 - now)
     coef_ref[0:1] = jnp.broadcast_to(ratio, (1, 128))
     coef_ref[1:2] = jnp.broadcast_to(noise, (1, 128))
-    for r in range(3):
-        put_right(first_ref, r, raw_ref.at[r])
+    put_right(first_ref, raw_ref)
     harmonic = jnp.broadcast_to(harmonic_ref[...], (8, 320))
     emb_ref[...] = silu(product(harmonic, time_ref[...], ((1,), (0,)))[0:1])
 
 
 def setup_second_kernel(after_ref, w_out_ref, temporal_ref, raw_ref, fold_ref, second_ref):
-    for r in range(3):
-        put_right(second_ref, r, raw_ref.at[r])
+    put_right(second_ref, raw_ref)
     w_out = jnp.concatenate([w_out_ref[...], w_out_ref[...] * 0.0], axis=0)
     for row, tap in enumerate((1, 0, 2)):
         fold = product(w_out, temporal_ref[tap], ((1,), (1,)))
@@ -182,7 +195,7 @@
         out_specs=[VMEM] * (len(shapes) + 1),
         out_shape=[
             *[jax.ShapeDtypeStruct(shape, F32) for shape in shapes],
-            jax.ShapeDtypeStruct((3, 1024, 960), BF16),
+            jax.ShapeDtypeStruct((4, 1024, 960), BF16),
         ],
         compiler_params=pltpu.CompilerParams(vmem_limit_bytes=LIMIT),
         cost_estimate=pl.CostEstimate(flops=0, bytes_accessed=10_000_000, transcendentals=0),
@@ -191,28 +204,35 @@
 
 
 def multiply(acc_ref, a_ref, b_ref, count):
-    left = jnp.concatenate([a_ref[64 * tap : 64 * tap + count, :] for tap in range(3)], axis=1)
-    for lo, hi in ((0, 256), (256, 512), (512, 768), (768, 960)):
-        right = jnp.concatenate([b_ref[tap, :, lo:hi] for tap in range(3)], axis=0)
-        acc_ref[8 : 8 + count, lo:hi] = jnp.dot(left, right, preferred_element_type=F32)
-
-
-def shifted_sum(acc_ref, row):
-    base = 8 + 64 * row
+    for j in range(4):
+        for lo, hi in ((0, 256), (256, 512), (512, 768), (768, 960)):
+            acc_ref[j, 8 : 8 + count, lo:hi] = jnp.dot(
+                a_ref[j], b_ref[j, :, lo:hi], preferred_element_type=F32
+            )
+
+
+def shifted_pair(acc_ref, t):
+    base = 8 + 64 * t
     column = lax.broadcasted_iota(jnp.int32, (64, 1), 0)
     first = column > 0
     last = column < 63
-    main = (
-        jnp.where(first, acc_ref[base - 1 : base + 63, 0:256], 0.0)
-        + acc_ref[base : base + 64, 256:512]
-        + jnp.where(last, acc_ref[base + 1 : base + 65, 512:768], 0.0)
-    )
-    rest = (
-        jnp.where(first, acc_ref[base - 1 : base + 63, 768:832], 0.0)
-        + acc_ref[base : base + 64, 832:896]
-        + jnp.where(last, acc_ref[base + 1 : base + 65, 896:960], 0.0)
-    )
-    return jnp.concatenate([main, rest], axis=1)
+
+    def tap(shift, lo, hi):
+        m1, m2, m3, m4 = (acc_ref[j, base + shift : base + shift + 64, lo:hi] for j in range(4))
+        return (m1 + (m2 + m3), (m2 - m3) - m4)
+
+    out = []
+    for at, width in ((0, 256), (768, 64)):
+        left = tap(-1, at, at + width)
+        here = tap(0, at + width, at + 2 * width)
+        right = tap(1, at + 2 * width, at + 3 * width)
+        out.append(
+            [
+                jnp.where(first, left[i], 0.0) + here[i] + jnp.where(last, right[i], 0.0)
+                for i in range(2)
+            ]
+        )
+    return [jnp.concatenate([out[0][i], out[1][i]], axis=1) for i in range(2)]
 
 
 def write_sums(stat_ref, total, square):
@@ -249,12 +269,15 @@
             act = act * jnp.where(strip > 0, 1.0, 0.0)
         elif i >= 12:
             act = act * jnp.where(strip < 3, 1.0, 0.0)
-        put_left(a_ref, rows, act)
-    multiply(acc_ref, a_ref, w_ref, 768)
+        lift_ref[rows, :] = act
+    put_pairs(a_ref, lift_ref, 6)
+    multiply(acc_ref, a_ref, w_ref, 384)
     total = jnp.zeros((8, 320), F32)
     square = jnp.zeros((8, 320), F32)
     for i in range(12):
-        out = shifted_sum(acc_ref, i) + emb_ref[...]
+        if i % 2 == 0:
+            pair = shifted_pair(acc_ref, i // 2)
+        out = pair[i % 2] + emb_ref[...]
         mid_ref[64 * i : 64 * i + 64, :] = out
         if 1 <= i <= 10:
             folded = out.reshape(8, 8, 320)
@@ -265,7 +288,7 @@
 
 def conv2_kernel(
     members, mid_ref, sum0_ref, sum1_ref, sum2_ref, sum3_ref, own_ref, w_in_ref, w_ref, hid_ref,
-    stat_ref, a_ref, acc_ref,
+    stat_ref, a_ref, acc_ref, act_ref,
 ):
     strip = lax.axis_index("band") >> 1
     sums = sum0_ref[...] + sum1_ref[...] + sum2_ref[...] + sum3_ref[...]
@@ -277,14 +300,17 @@
             act = act * jnp.where(strip > 0, 1.0, 0.0)
         elif i == 11:
             act = act * jnp.where(strip < 3, 1.0, 0.0)
-        put_left(a_ref, rows, act)
-    multiply(acc_ref, a_ref, w_ref, 640)
+        act_ref[rows, :] = act
+    put_pairs(a_ref, act_ref, 5)
+    multiply(acc_ref, a_ref, w_ref, 320)
     total = jnp.zeros((8, 320), F32)
     square = jnp.zeros((8, 320), F32)
     hid_ref[...] = lift(own_ref[...], w_in_ref[...])
     for i in range(10):
         rows = slice(64 * i, 64 * i + 64)
-        out = hid_ref[rows, :] + shifted_sum(acc_ref, i)
+        if i % 2 == 0:
+            pair = shifted_pair(acc_ref, i // 2)
+        out = hid_ref[rows, :] + pair[i % 2]
         hid_ref[rows, :] = out
         folded = out.reshape(8, 8, 320)
         total += jnp.sum(folded, axis=0)
@@ -337,7 +363,7 @@
 LIMIT = 20 * 1024 * 1024
 
 
-def conv_call(kernel, operands, rows_in, rows_out, extra, name):
+def conv_call(kernel, operands, rows_in, rows_out, name):
     return pl.pallas_call(
         kernel,
         in_specs=[VMEM] * len(operands),
@@ -347,13 +373,13 @@
             jax.ShapeDtypeStruct((2, 320), F32),
         ],
         scratch_shapes=[
-            pltpu.VMEM((rows_in * 64, 1024), BF16),
-            pltpu.VMEM((rows_out * 64 + 16, 960), F32),
-            *extra,
+            pltpu.VMEM((4, rows_out * 32, 1024), BF16),
+            pltpu.VMEM((4, rows_out * 32 + 16, 960), F32),
+            pltpu.VMEM((rows_in * 64, 320), F32),
         ],
         compiler_params=pltpu.CompilerParams(vmem_limit_bytes=LIMIT),
         cost_estimate=pl.CostEstimate(
-            flops=6 * rows_out * 64 * 2880 * 320,
+            flops=4 * rows_out * 64 * 2880 * 320,
             bytes_accessed=4_000_000,
             transcendentals=rows_in * 64 * 320,
         ),
@@ -400,8 +426,8 @@
     plan.reshape(-1)[:NSTEPS] = noise_plan()
     plan = jnp.asarray(plan)
     spread, step = call(
-        spread_kernel, [SMEM, VMEM, VMEM, ANY], [(8, 8, positions), (1, 128)],
-        (timesteps, latents.transpose(0, 2, 1, 3), fresh.transpose(0, 2, 1, 3), harmonic),
+        spread_kernel, [SMEM, VMEM, ANY], [(8, 8, positions), (1, 128)],
+        (timesteps, jnp.concatenate([latents, fresh]).transpose(0, 2, 1, 3), harmonic),
         "spread", pl.CostEstimate(flops=8_000_000_000, bytes_accessed=40_000, transcendentals=0),
     )
     frame = lax.all_to_all(spread, "band", 0, 0, tiled=True)
@@ -414,7 +440,7 @@
         middle, stats = conv_call(
             functools.partial(conv1_kernel, members),
             (*pieces, w_in, embedded, first_ready),
-            14, 12, [pltpu.VMEM((896, 320), F32)], "conv_one",
+            14, 12, "conv_one",
         )
         if iteration == 0:
             folded, second_ready = setup(
@@ -424,7 +450,7 @@
         hidden, stats = conv_call(
             functools.partial(conv2_kernel, members),
             (middle, *around_strip(stats), pieces[0], w_in, second_ready),
-            12, 10, [], "conv_two",
+            12, 10, "conv_two",
         )
         width = positions if last else 2 * positions
         (parts,) = call(

time: 95.1 us -> 90.7 us (0.954)
  Pallas kernels: 26.5 us -> 23.5 us
  local copies, waits for them, and re-layouts: 1.47 us -> 0.07 us
    pallas_call x4, Pallas kernels: 21.4 us -> 17.3 us  [conv_call(): pl.pallas_call(kernel, in_specs=[VMEM] * len(operands), out_specs=[VMEM,...]
    unnamed x20 -> x16, local copies, waits for them, and re-layouts: 1.45 us -> 0.05 us
    pallas_call x2, Pallas kernels: 2.88 us -> 4.04 us  [setup(): pl.pallas_call(kernel, in_specs=specs, out_specs=[VMEM] * (len(shapes) +...]
  transfers between devices with their start and end apart: 19 -> 19, of which waited for: 17 -> 16; matrix products, arithmetic and copies ran while one was open for 0% -> 0% of each run, Pallas kernels for 2% -> 2%
where the time goes in v5:
time: 90.7 us; the launch traced here: 90.3 us
  starting transfers between devices  25.6 us (28%)
  waiting for transfers between devices  25.5 us (28%)
  Pallas kernels  23.5 us (26%)
  blocking collectives  13.9 us (15%)
    ppermute x15, starting transfers between devices, around_strip(): lax.ppermute(value, 'band', [(i, i ^ 2 * flip) for i in range(bands)])  17.9 us
    pallas_call x4, Pallas kernels, conv_call(): pl.pallas_call(kernel, in_specs=[VMEM] * len(operands), out_specs=[VMEM,...  17.3 us
    ppermute x15, waiting for transfers between devices, around_strip(): lax.ppermute(value, 'band', [(i, i ^ 2 * flip) for i in range(bands)])  14.1 us
    all_to_all x1, blocking collectives, on_device(): frame = lax.all_to_all(spread, 'band', 0, 0, tiled=True)  13.9 us
    ppermute x1, waiting for transfers between devices, on_device(): lax.ppermute(parts[8:12], 'level', [(i, i + 2) for i in range(levels - 2)])  6.36 us
    ppermute x1, waiting for transfers between devices, swap_slots(): from_chip = lax.ppermute(to_chip, 'level', across)  5.03 us
    pallas_call x2, Pallas kernels, setup(): pl.pallas_call(kernel, in_specs=specs, out_specs=[VMEM] * (len(shapes) +...  4.04 us
    ppermute x1, starting transfers between devices, on_device(): lax.ppermute(parts[8:12], 'level', [(i, i + 2) for i in range(levels - 2)])  3.82 us
  transfers between devices with their start and end apart: 19, of which 16 were waited for; matrix products, arithmetic and copies ran while one was open for 0% of the time, Pallas kernels for 2%

profile of v5, /device:TPU:8, one launch (start us, length us, event | category | flops | bytes accessed | tf_op | source)
XLA Modules:
  0.0 90.3 jit_solution(16040272453159033567)
XLA Ops:
  0.8 0.7 maximum_bitcast_fusion.frames_ref
  1.6 13.9 %all_to_all.5.frame_ref = f32[8,8,320]{2,1,0:T(8,128)S(1)} all-to-all(f32[8,8,320]{2,1,0:T(8,128)S(1)} %get-tuple-element.25), channel_id=1, replica_groups=mesh['level'=32,'band'=8] {'band'}, dimensions={0} | all-to-all | bytes 163840 | tf_op jit(solution)/shard_map/all_to_all | solution.py:433
  15.5 2.0 %setup_first.1 = (f32[4,640]{1,0:T(4,128)S(1)}, f32[4,640]{1,0:T(4,128)S(1)}, f32[4,640]{1,0:T(4,128)S(1)}, f32[4,640]{1,0:T(4,128)S(1)}, f32[4,640]{1,0:T(4,128...) custom-call(f32[8,8,320]{2,1,0:T(8,128)S(1)} %all_to_all.5.frame_ref, ...), custom_call_target="tpu_custom_call" | custom-call | bytes 10000000 | tf_op jit(solution)/shard_map/setup_first/pallas_call | solution.py:192
  17.6 4.6 %conv_one.2 = (f32[768,320]{1,0:T(8,128)S(1)}, f32[2,320]{1,0:T(2,128)S(1)}) custom-call(f32[4,640]{1,0:T(4,128)S(1)} %get-tuple-element.27.own_ref, f32[4,640]{1,0:T(4,128)S(1)} %get-tuple-element.28.flip1_ref, f32[4,640]{1,0:T(4,128)S(1)} %get-tuple-element.29.flip3_ref, f32[4,640]{1,0:T(4,128)S(1)} %get-tuple-element.30.flip2_ref, ...), custom_call_target="tpu_custom_call" | custom-call | flops 2831155200 | bytes 4000000 | tf_op jit(solution)/shard_map/conv_one/pallas_call | solution.py:367
  22.2 1.5 %collective-permute-start.2 = (f32[2,320]{1,0:T(2,128)S(1)}, f32[2,320]{1,0:T(2,128)S(1)}, u32[]{:S(2)}, u32[]{:S(2)}) collective-permute-start(f32[2,320]{1,0:T(2,128)S(1)} %get-tuple-element.34.after_ref.sum0_ref), channel_id=1, source_target_pairs={{0,4},{1,5},{2,6},{3,7},{4,0},{5,1},{6,2},{7,3},{8,12},{9,13},{10,... | collective-permute-start | bytes 7688 | tf_op jit(solution)/shard_map/ppermute | solution.py:405
  23.7 1.8 %collective-permute-start.1 = (f32[2,320]{1,0:T(2,128)S(1)}, f32[2,320]{1,0:T(2,128)S(1)}, u32[]{:S(2)}, u32[]{:S(2)}) collective-permute-start(f32[2,320]{1,0:T(2,128)S(1)} %get-tuple-element.34.after_ref.sum0_ref), channel_id=1, source_target_pairs={{0,6},{1,7},{2,4},{3,5},{4,2},{5,3},{6,0},{7,1},{8,14},{9,15},{10,... | collective-permute-start | bytes 7688 | tf_op jit(solution)/shard_map/ppermute | solution.py:405
  25.8 2.0 %setup_second.1 = (f32[16,320]{1,0:T(8,128)S(1)}, bf16[4,1024,960]{2,1,0:T(8,128)(2,1)S(1)}) custom-call(f32[2,320]{1,0:T(2,128)S(1)} %get-tuple-element.34.after_ref.sum0_ref, f32[4,320]{1,0:T(4,128)S(1)} %bitcast.7, f32[3,320,320]{2,1,0:T(8,128)S(1)} %copy-done.1, f32[3,3,320,320]{3,2,1,0:T(8,128)S(1)} %bitcast.6), custom_call_target="tpu_custom_call" | custom-call | bytes 10000000 | tf_op jit(solution)/shard_map/setup_second/pallas_call | solution.py:192
  29.1 4.1 %conv_two.2 = (f32[640,320]{1,0:T(8,128)S(1)}, f32[2,320]{1,0:T(2,128)S(1)}) custom-call(f32[768,320]{1,0:T(8,128)S(1)} %get-tuple-element.33.mid_ref, f32[2,320]{1,0:T(2,128)S(1)} %get-tuple-element.34.after_ref.sum0_ref, f32[2,320]{1,0:T(2,128)S(1)} %collective-permute-done.sum1_ref, f32[2,320]{1,0:T(2,128)S(1)} %collective-permute-done.1.sum2_ref, ...), custom_call_target="tpu_custom_call" | custom-call | flops 2359296000 | bytes 4000000 | tf_op jit(solution)/shard_map/conv_two/pallas_call | solution.py:367
  33.2 1.5 %collective-permute-start.5 = (f32[2,320]{1,0:T(2,128)S(1)}, f32[2,320]{1,0:T(2,128)S(1)}, u32[]{:S(2)}, u32[]{:S(2)}) collective-permute-start(f32[2,320]{1,0:T(2,128)S(1)} %get-tuple-element.37.sum0_ref), channel_id=1, source_target_pairs={{0,4},{1,5},{2,6},{3,7},{4,0},{5,1},{6,2},{7,3},{8,12},{9,13},{10,... | collective-permute-start | bytes 7688 | tf_op jit(solution)/shard_map/ppermute | solution.py:405
  34.7 1.8 %collective-permute-start.4 = (f32[2,320]{1,0:T(2,128)S(1)}, f32[2,320]{1,0:T(2,128)S(1)}, u32[]{:S(2)}, u32[]{:S(2)}) collective-permute-start(f32[2,320]{1,0:T(2,128)S(1)} %get-tuple-element.37.sum0_ref), channel_id=1, source_target_pairs={{0,6},{1,7},{2,4},{3,5},{4,2},{5,3},{6,0},{7,1},{8,14},{9,15},{10,... | collective-permute-start | bytes 7688 | tf_op jit(solution)/shard_map/ppermute | solution.py:405
  36.8 1.6 %collective-permute-done.5.sum3_ref = f32[2,320]{1,0:T(2,128)S(1)} collective-permute-done((f32[2,320]{1,0:T(2,128)S(1)}, f32[2,320]{1,0:T(2,128)S(1)}, u32[]{:S(2)}, u32[]{:S(2)}) %collective-permute-start.5) | collective-permute-done | bytes 2592 | tf_op jit(solution)/shard_map/ppermute | solution.py:405
  38.4 1.1 %collective-permute-done.4.sum2_ref = f32[2,320]{1,0:T(2,128)S(1)} collective-permute-done((f32[2,320]{1,0:T(2,128)S(1)}, f32[2,320]{1,0:T(2,128)S(1)}, u32[]{:S(2)}, u32[]{:S(2)}) %collective-permute-start.4) | collective-permute-done | bytes 2592 | tf_op jit(solution)/shard_map/ppermute | solution.py:405
  40.1 0.8 project.2.parts_ref
  40.9 1.9 %collective-permute-start.6 = (f32[8,640]{1,0:T(8,128)S(1)}, f32[8,640]{1,0:T(8,128)S(1)}, u32[]{:S(2)}, u32[]{:S(2)}) collective-permute-start(f32[8,640]{1,0:T(8,128)S(1)} %slice.16), channel_id=1, source_target_pairs={{0,8},{8,16},{16,24},{24,32},{32,40},{40,48},{48,56},{56,64},{64,7... | collective-permute-start | bytes 61448 | tf_op jit(solution)/shard_map/ppermute | solution.py:466
  42.9 3.8 %collective-permute-start.7 = (f32[4,640]{1,0:T(4,128)S(1)}, f32[4,640]{1,0:T(4,128)S(1)}, u32[]{:S(2)}, u32[]{:S(2)}) collective-permute-start(f32[4,640]{1,0:T(4,128)S(1)} %slice.17), channel_id=1, source_target_pairs={{0,16},{8,24},{16,32},{24,40},{32,48},{40,56},{48,64},{56,72},{64,... | collective-permute-start | bytes 30728 | tf_op jit(solution)/shard_map/ppermute | solution.py:467
  46.7 6.4 %collective-permute-done.7.two_ref = f32[4,640]{1,0:T(4,128)S(1)} collective-permute-done((f32[4,640]{1,0:T(4,128)S(1)}, f32[4,640]{1,0:T(4,128)S(1)}, u32[]{:S(2)}, u32[]{:S(2)}) %collective-permute-start.7) | collective-permute-done | bytes 10272 | tf_op jit(solution)/shard_map/ppermute | solution.py:467
  53.1 1.3 %collective-permute-start.10 = (f32[4,640]{1,0:T(4,128)S(1)}, f32[4,640]{1,0:T(4,128)S(1)}, u32[]{:S(2)}, u32[]{:S(2)}) collective-permute-start(f32[4,640]{1,0:T(4,128)S(1)} %merge.1.own_ref), channel_id=1, source_target_pairs={{0,4},{1,5},{2,6},{3,7},{4,0},{5,1},{6,2},{7,3},{8,12},{9,13},{10,... | collective-permute-start | bytes 30728 | tf_op jit(solution)/shard_map/ppermute | solution.py:405
  54.3 1.8 %collective-permute-start.9 = (f32[4,640]{1,0:T(4,128)S(1)}, f32[4,640]{1,0:T(4,128)S(1)}, u32[]{:S(2)}, u32[]{:S(2)}) collective-permute-start(f32[4,640]{1,0:T(4,128)S(1)} %merge.1.own_ref), channel_id=1, source_target_pairs={{0,6},{1,7},{2,4},{3,5},{4,2},{5,3},{6,0},{7,1},{8,14},{9,15},{10,... | collective-permute-start | bytes 30728 | tf_op jit(solution)/shard_map/ppermute | solution.py:405
  56.6 1.7 %collective-permute-done.10.flip2_ref = f32[4,640]{1,0:T(4,128)S(1)} collective-permute-done((f32[4,640]{1,0:T(4,128)S(1)}, f32[4,640]{1,0:T(4,128)S(1)}, u32[]{:S(2)}, u32[]{:S(2)}) %collective-permute-start.10) | collective-permute-done | bytes 10272 | tf_op jit(solution)/shard_map/ppermute | solution.py:405
  58.3 0.9 collective-permute-done.9.flip3_ref
  59.8 4.6 %conv_one.3 = (f32[768,320]{1,0:T(8,128)S(1)}, f32[2,320]{1,0:T(2,128)S(1)}) custom-call(f32[4,640]{1,0:T(4,128)S(1)} %merge.1.own_ref, f32[4,640]{1,0:T(4,128)S(1)} %collective-permute-done.8.flip1_ref, f32[4,640]{1,0:T(4,128)S(1)} %collective-permute-done.9.flip3_ref, f32[4,640]{1,0:T(4,128)S(1)} %collective-permute-done.10.flip2_ref, ...), custom_call_target="tpu_custom_call" | custom-call | flops 2831155200 | bytes 4000000 | tf_op jit(solution)/shard_map/conv_one/pallas_call | solution.py:367
  64.4 1.5 %collective-permute-start.13 = (f32[2,320]{1,0:T(2,128)S(1)}, f32[2,320]{1,0:T(2,128)S(1)}, u32[]{:S(2)}, u32[]{:S(2)}) collective-permute-start(f32[2,320]{1,0:T(2,128)S(1)} %get-tuple-element.42.sum0_ref), channel_id=1, source_target_pairs={{0,4},{1,5},{2,6},{3,7},{4,0},{5,1},{6,2},{7,3},{8,12},{9,13},{10,... | collective-permute-start | bytes 7688 | tf_op jit(solution)/shard_map/ppermute | solution.py:405
  65.9 1.8 %collective-permute-start.12 = (f32[2,320]{1,0:T(2,128)S(1)}, f32[2,320]{1,0:T(2,128)S(1)}, u32[]{:S(2)}, u32[]{:S(2)}) collective-permute-start(f32[2,320]{1,0:T(2,128)S(1)} %get-tuple-element.42.sum0_ref), channel_id=1, source_target_pairs={{0,6},{1,7},{2,4},{3,5},{4,2},{5,3},{6,0},{7,1},{8,14},{9,15},{10,... | collective-permute-start | bytes 7688 | tf_op jit(solution)/shard_map/ppermute | solution.py:405
  68.0 1.6 %collective-permute-done.13.sum3_ref = f32[2,320]{1,0:T(2,128)S(1)} collective-permute-done((f32[2,320]{1,0:T(2,128)S(1)}, f32[2,320]{1,0:T(2,128)S(1)}, u32[]{:S(2)}, u32[]{:S(2)}) %collective-permute-start.13) | collective-permute-done | bytes 2592 | tf_op jit(solution)/shard_map/ppermute | solution.py:405
  69.6 1.1 %collective-permute-done.12.sum2_ref = f32[2,320]{1,0:T(2,128)S(1)} collective-permute-done((f32[2,320]{1,0:T(2,128)S(1)}, f32[2,320]{1,0:T(2,128)S(1)}, u32[]{:S(2)}, u32[]{:S(2)}) %collective-permute-start.12) | collective-permute-done | bytes 2592 | tf_op jit(solution)/shard_map/ppermute | solution.py:405
  71.3 4.1 %conv_two.3 = (f32[640,320]{1,0:T(8,128)S(1)}, f32[2,320]{1,0:T(2,128)S(1)}) custom-call(f32[768,320]{1,0:T(8,128)S(1)} %get-tuple-element.41.mid_ref, f32[2,320]{1,0:T(2,128)S(1)} %get-tuple-element.42.sum0_ref, f32[2,320]{1,0:T(2,128)S(1)} %collective-permute-done.11.sum1_ref, f32[2,320]{1,0:T(2,128)S(1)} %collective-permute-done.12.sum2_ref, ...), custom_call_target="tpu_custom_call" | custom-call | flops 2359296000 | bytes 4000000 | tf_op jit(solution)/shard_map/conv_two/pallas_call | solution.py:367
  75.3 1.3 %collective-permute-start.16 = (f32[2,320]{1,0:T(2,128)S(1)}, f32[2,320]{1,0:T(2,128)S(1)}, u32[]{:S(2)}, u32[]{:S(2)}) collective-permute-start(f32[2,320]{1,0:T(2,128)S(1)} %get-tuple-element.44.sum0_ref), channel_id=1, source_target_pairs={{0,4},{1,5},{2,6},{3,7},{4,0},{5,1},{6,2},{7,3},{8,12},{9,13},{10,... | collective-permute-start | bytes 7688 | tf_op jit(solution)/shard_map/ppermute | solution.py:405
  76.6 1.8 %collective-permute-start.15 = (f32[2,320]{1,0:T(2,128)S(1)}, f32[2,320]{1,0:T(2,128)S(1)}, u32[]{:S(2)}, u32[]{:S(2)}) collective-permute-start(f32[2,320]{1,0:T(2,128)S(1)} %get-tuple-element.44.sum0_ref), channel_id=1, source_target_pairs={{0,6},{1,7},{2,4},{3,5},{4,2},{5,3},{6,0},{7,1},{8,14},{9,15},{10,... | collective-permute-start | bytes 7688 | tf_op jit(solution)/shard_map/ppermute | solution.py:405
  78.9 1.6 %collective-permute-done.16.sum3_ref = f32[2,320]{1,0:T(2,128)S(1)} collective-permute-done((f32[2,320]{1,0:T(2,128)S(1)}, f32[2,320]{1,0:T(2,128)S(1)}, u32[]{:S(2)}, u32[]{:S(2)}) %collective-permute-start.16) | collective-permute-done | bytes 2592 | tf_op jit(solution)/shard_map/ppermute | solution.py:405
  80.5 0.9 collective-permute-done.15.sum2_ref
  82.6 1.9 %collective-permute-start.18 = (f32[4,320]{1,0:T(4,128)S(1)}, f32[4,320]{1,0:T(4,128)S(1)}, u32[]{:S(2)}, u32[]{:S(2)}) collective-permute-start(f32[4,320]{1,0:T(4,128)S(1)} %get-tuple-element.45), channel_id=1, source_target_pairs={{8,16},{24,32},{40,48},{56,64},{72,80},{88,96},{104,112},{120,128}... | collective-permute-start | bytes 15368 | tf_op jit(solution)/shard_map/ppermute | solution.py:415
  84.6 5.0 %collective-permute-done.18.chip_ref = f32[4,320]{1,0:T(4,128)S(1)} collective-permute-done((f32[4,320]{1,0:T(4,128)S(1)}, f32[4,320]{1,0:T(4,128)S(1)}, u32[]{:S(2)}, u32[]{:S(2)}) %collective-permute-start.18) | collective-permute-done | bytes 5152 | tf_op jit(solution)/shard_map/ppermute | solution.py:415
  (41 shorter events, 7.2 us)
Async XLA Ops:
  1.5 14.0 %copy-start = (f32[3,3,320,320]{3,2,1,0:T(8,128)S(1)}, f32[3,3,320,320]{3,2,1,0:T(8,128)}, u32[]{:S(2)}) copy-start(f32[3,3,320,320]{3,2,1,0:T(8,128)} %raw_ref.2) | copy-start | bytes 11059204
  1.5 14.0 %copy-start.2 = (f32[320,320]{1,0:T(8,128)S(1)}, f32[320,320]{1,0:T(8,128)}, u32[]{:S(2)}) copy-start(f32[320,320]{1,0:T(8,128)} %time_ref.1) | copy-start | bytes 1228804
  1.5 14.0 %copy-start.5 = (f32[8,128]{1,0:T(8,128)S(1)}, f32[8,128]{1,0:T(8,128)}, u32[]{:S(2)}) copy-start(f32[8,128]{1,0:T(8,128)} %constant.8.clone.plan_ref) | copy-start | bytes 12292
  1.6 15.9 %copy-start.4 = (f32[4,320]{1,0:T(4,128)S(1)}, f32[4,320]{1,0:T(4,128)}, u32[]{:S(2)}) copy-start(f32[4,320]{1,0:T(4,128)} %w_in_ref.7) | copy-start | bytes 15364
  15.5 10.3 %slice-start = ((s8[4423680]{0:T(1024)(128)(4,1)}), s8[4194304]{0:T(1024)(128)(4,1)S(1)}, s32[]{:S(2)}) async-start(s8[4423680]{0:T(1024)(128)(4,1)} %bitcast.5), calls=%async_computation.1 | async-start | bytes 8388608
  17.6 8.2 %slice-start.1 = ((s8[4423680]{0:T(1024)(128)(4,1)}), s8[229376]{0:T(1024)(128)(4,1)S(1)}, s32[]{:S(2)}) async-start(s8[4423680]{0:T(1024)(128)(4,1)} %bitcast.5), calls=%async_computation.2 | async-start | bytes 458752
  17.6 8.2 %copy-start.1 = (f32[3,320,320]{2,1,0:T(8,128)S(1)}, f32[3,320,320]{2,1,0:T(8,128)}, u32[]{:S(2)}) copy-start(f32[3,320,320]{2,1,0:T(8,128)} %temporal_ref.1) | copy-start | bytes 3686404
  17.6 8.2 %copy-start.3 = (f32[320,4]{0,1:T(4,128)S(1)}, f32[320,4]{0,1:T(4,128)}, u32[]{:S(2)}) copy-start(f32[320,4]{0,1:T(4,128)} %param.18) | copy-start | bytes 15364
  22.2 5.6 %collective-permute-start.2 = (f32[2,320]{1,0:T(2,128)S(1)}, f32[2,320]{1,0:T(2,128)S(1)}, u32[]{:S(2)}, u32[]{:S(2)}) collective-permute-start(f32[2,320]{1,0:T(2,128)S(1)} %get-tuple-element.34.after_ref.sum0_ref), channel_id=1, source_target_pairs={{0,4},{1,5},{2,6},{3,7},{4,0},{5,1},{6,2},{7,3},{8,12},{9,13},{10,... | collective-permute-start | bytes 7688 | tf_op jit(solution)/shard_map/ppermute | solution.py:405
  23.7 4.8 %collective-permute-start.1 = (f32[2,320]{1,0:T(2,128)S(1)}, f32[2,320]{1,0:T(2,128)S(1)}, u32[]{:S(2)}, u32[]{:S(2)}) collective-permute-start(f32[2,320]{1,0:T(2,128)S(1)} %get-tuple-element.34.after_ref.sum0_ref), channel_id=1, source_target_pairs={{0,6},{1,7},{2,4},{3,5},{4,2},{5,3},{6,0},{7,1},{8,14},{9,15},{10,... | collective-permute-start | bytes 7688 | tf_op jit(solution)/shard_map/ppermute | solution.py:405
  25.5 3.6 %collective-permute-start = (f32[2,320]{1,0:T(2,128)S(1)}, f32[2,320]{1,0:T(2,128)S(1)}, u32[]{:S(2)}, u32[]{:S(2)}) collective-permute-start(f32[2,320]{1,0:T(2,128)S(1)} %get-tuple-element.34.after_ref.sum0_ref), channel_id=1, source_target_pairs={{0,2},{1,3},{2,0},{3,1},{4,6},{5,7},{6,4},{7,5},{8,10},{9,11},{10,... | collective-permute-start | bytes 7688 | tf_op jit(solution)/shard_map/ppermute | solution.py:405
  33.2 5.2 %collective-permute-start.5 = (f32[2,320]{1,0:T(2,128)S(1)}, f32[2,320]{1,0:T(2,128)S(1)}, u32[]{:S(2)}, u32[]{:S(2)}) collective-permute-start(f32[2,320]{1,0:T(2,128)S(1)} %get-tuple-element.37.sum0_ref), channel_id=1, source_target_pairs={{0,4},{1,5},{2,6},{3,7},{4,0},{5,1},{6,2},{7,3},{8,12},{9,13},{10,... | collective-permute-start | bytes 7688 | tf_op jit(solution)/shard_map/ppermute | solution.py:405
  34.7 4.8 %collective-permute-start.4 = (f32[2,320]{1,0:T(2,128)S(1)}, f32[2,320]{1,0:T(2,128)S(1)}, u32[]{:S(2)}, u32[]{:S(2)}) collective-permute-start(f32[2,320]{1,0:T(2,128)S(1)} %get-tuple-element.37.sum0_ref), channel_id=1, source_target_pairs={{0,6},{1,7},{2,4},{3,5},{4,2},{5,3},{6,0},{7,1},{8,14},{9,15},{10,... | collective-permute-start | bytes 7688 | tf_op jit(solution)/shard_map/ppermute | solution.py:405
  36.5 3.6 %collective-permute-start.3 = (f32[2,320]{1,0:T(2,128)S(1)}, f32[2,320]{1,0:T(2,128)S(1)}, u32[]{:S(2)}, u32[]{:S(2)}) collective-permute-start(f32[2,320]{1,0:T(2,128)S(1)} %get-tuple-element.37.sum0_ref), channel_id=1, source_target_pairs={{0,2},{1,3},{2,0},{3,1},{4,6},{5,7},{6,4},{7,5},{8,10},{9,11},{10,... | collective-permute-start | bytes 7688 | tf_op jit(solution)/shard_map/ppermute | solution.py:405
  40.9 12.1 %collective-permute-start.6 = (f32[8,640]{1,0:T(8,128)S(1)}, f32[8,640]{1,0:T(8,128)S(1)}, u32[]{:S(2)}, u32[]{:S(2)}) collective-permute-start(f32[8,640]{1,0:T(8,128)S(1)} %slice.16), channel_id=1, source_target_pairs={{0,8},{8,16},{16,24},{24,32},{32,40},{40,48},{48,56},{56,64},{64,7... | collective-permute-start | bytes 61448 | tf_op jit(solution)/shard_map/ppermute | solution.py:466
  42.9 10.2 %collective-permute-start.7 = (f32[4,640]{1,0:T(4,128)S(1)}, f32[4,640]{1,0:T(4,128)S(1)}, u32[]{:S(2)}, u32[]{:S(2)}) collective-permute-start(f32[4,640]{1,0:T(4,128)S(1)} %slice.17), channel_id=1, source_target_pairs={{0,16},{8,24},{16,32},{24,40},{32,48},{40,56},{48,64},{56,72},{64,... | collective-permute-start | bytes 30728 | tf_op jit(solution)/shard_map/ppermute | solution.py:467
  53.1 5.3 %collective-permute-start.10 = (f32[4,640]{1,0:T(4,128)S(1)}, f32[4,640]{1,0:T(4,128)S(1)}, u32[]{:S(2)}, u32[]{:S(2)}) collective-permute-start(f32[4,640]{1,0:T(4,128)S(1)} %merge.1.own_ref), channel_id=1, source_target_pairs={{0,4},{1,5},{2,6},{3,7},{4,0},{5,1},{6,2},{7,3},{8,12},{9,13},{10,... | collective-permute-start | bytes 30728 | tf_op jit(solution)/shard_map/ppermute | solution.py:405
  54.3 4.9 %collective-permute-start.9 = (f32[4,640]{1,0:T(4,128)S(1)}, f32[4,640]{1,0:T(4,128)S(1)}, u32[]{:S(2)}, u32[]{:S(2)}) collective-permute-start(f32[4,640]{1,0:T(4,128)S(1)} %merge.1.own_ref), channel_id=1, source_target_pairs={{0,6},{1,7},{2,4},{3,5},{4,2},{5,3},{6,0},{7,1},{8,14},{9,15},{10,... | collective-permute-start | bytes 30728 | tf_op jit(solution)/shard_map/ppermute | solution.py:405
  56.1 3.7 %collective-permute-start.8 = (f32[4,640]{1,0:T(4,128)S(1)}, f32[4,640]{1,0:T(4,128)S(1)}, u32[]{:S(2)}, u32[]{:S(2)}) collective-permute-start(f32[4,640]{1,0:T(4,128)S(1)} %merge.1.own_ref), channel_id=1, source_target_pairs={{0,2},{1,3},{2,0},{3,1},{4,6},{5,7},{6,4},{7,5},{8,10},{9,11},{10,... | collective-permute-start | bytes 30728 | tf_op jit(solution)/shard_map/ppermute | solution.py:405
  64.4 5.2 %collective-permute-start.13 = (f32[2,320]{1,0:T(2,128)S(1)}, f32[2,320]{1,0:T(2,128)S(1)}, u32[]{:S(2)}, u32[]{:S(2)}) collective-permute-start(f32[2,320]{1,0:T(2,128)S(1)} %get-tuple-element.42.sum0_ref), channel_id=1, source_target_pairs={{0,4},{1,5},{2,6},{3,7},{4,0},{5,1},{6,2},{7,3},{8,12},{9,13},{10,... | collective-permute-start | bytes 7688 | tf_op jit(solution)/shard_map/ppermute | solution.py:405
  65.9 4.8 %collective-permute-start.12 = (f32[2,320]{1,0:T(2,128)S(1)}, f32[2,320]{1,0:T(2,128)S(1)}, u32[]{:S(2)}, u32[]{:S(2)}) collective-permute-start(f32[2,320]{1,0:T(2,128)S(1)} %get-tuple-element.42.sum0_ref), channel_id=1, source_target_pairs={{0,6},{1,7},{2,4},{3,5},{4,2},{5,3},{6,0},{7,1},{8,14},{9,15},{10,... | collective-permute-start | bytes 7688 | tf_op jit(solution)/shard_map/ppermute | solution.py:405
  67.7 3.6 %collective-permute-start.11 = (f32[2,320]{1,0:T(2,128)S(1)}, f32[2,320]{1,0:T(2,128)S(1)}, u32[]{:S(2)}, u32[]{:S(2)}) collective-permute-start(f32[2,320]{1,0:T(2,128)S(1)} %get-tuple-element.42.sum0_ref), channel_id=1, source_target_pairs={{0,2},{1,3},{2,0},{3,1},{4,6},{5,7},{6,4},{7,5},{8,10},{9,11},{10,... | collective-permute-start | bytes 7688 | tf_op jit(solution)/shard_map/ppermute | solution.py:405
  75.3 5.2 %collective-permute-start.16 = (f32[2,320]{1,0:T(2,128)S(1)}, f32[2,320]{1,0:T(2,128)S(1)}, u32[]{:S(2)}, u32[]{:S(2)}) collective-permute-start(f32[2,320]{1,0:T(2,128)S(1)} %get-tuple-element.44.sum0_ref), channel_id=1, source_target_pairs={{0,4},{1,5},{2,6},{3,7},{4,0},{5,1},{6,2},{7,3},{8,12},{9,13},{10,... | collective-permute-start | bytes 7688 | tf_op jit(solution)/shard_map/ppermute | solution.py:405
  76.6 4.8 %collective-permute-start.15 = (f32[2,320]{1,0:T(2,128)S(1)}, f32[2,320]{1,0:T(2,128)S(1)}, u32[]{:S(2)}, u32[]{:S(2)}) collective-permute-start(f32[2,320]{1,0:T(2,128)S(1)} %get-tuple-element.44.sum0_ref), channel_id=1, source_target_pairs={{0,6},{1,7},{2,4},{3,5},{4,2},{5,3},{6,0},{7,1},{8,14},{9,15},{10,... | collective-permute-start | bytes 7688 | tf_op jit(solution)/shard_map/ppermute | solution.py:405
  78.4 3.6 %collective-permute-start.14 = (f32[2,320]{1,0:T(2,128)S(1)}, f32[2,320]{1,0:T(2,128)S(1)}, u32[]{:S(2)}, u32[]{:S(2)}) collective-permute-start(f32[2,320]{1,0:T(2,128)S(1)} %get-tuple-element.44.sum0_ref), channel_id=1, source_target_pairs={{0,2},{1,3},{2,0},{3,1},{4,6},{5,7},{6,4},{7,5},{8,10},{9,11},{10,... | collective-permute-start | bytes 7688 | tf_op jit(solution)/shard_map/ppermute | solution.py:405
  82.6 7.1 %collective-permute-start.18 = (f32[4,320]{1,0:T(4,128)S(1)}, f32[4,320]{1,0:T(4,128)S(1)}, u32[]{:S(2)}, u32[]{:S(2)}) collective-permute-start(f32[4,320]{1,0:T(4,128)S(1)} %get-tuple-element.45), channel_id=1, source_target_pairs={{8,16},{24,32},{40,48},{56,64},{72,80},{88,96},{104,112},{120,128}... | collective-permute-start | bytes 15368 | tf_op jit(solution)/shard_map/ppermute | solution.py:415
  84.5 5.1 %collective-permute-start.17 = (f32[4,320]{1,0:T(4,128)S(1)}, f32[4,320]{1,0:T(4,128)S(1)}, u32[]{:S(2)}, u32[]{:S(2)}) collective-permute-start(f32[4,320]{1,0:T(4,128)S(1)} %get-tuple-element.46), channel_id=1, source_target_pairs={{0,8},{8,0},{16,24},{24,16},{32,40},{40,32},{48,56},{56,48},{64,72... | collective-permute-start | bytes 15368 | tf_op jit(solution)/shard_map/ppermute | solution.py:414

commit v6 on v5

--- a/solution.py
+++ b/solution.py
@@ -318,8 +318,18 @@
     write_sums(stat_ref, total, square)
 
 
+def base_kernel(last, hid_ref, w_out_ref, base_ref):
+    if last:
+        low = lax.axis_index("band") & 1
+        hidden = hid_ref[pl.ds(pl.multiple_of(low * 320, 64), 320), :]
+    else:
+        hidden = hid_ref[...]
+    w_out = jnp.concatenate([w_out_ref[...], w_out_ref[...] * 0.0], axis=0)
+    base_ref[...] = product(w_out, hidden, ((1,), (1,)))
+
+
 def project_kernel(
-    members, last, hid_ref, sum0_ref, sum1_ref, sum2_ref, sum3_ref, own_ref, w_out_ref, fold_ref,
+    members, last, hid_ref, sum0_ref, sum1_ref, sum2_ref, sum3_ref, own_ref, base_ref, fold_ref,
     coef_ref, out_ref,
 ):
     sums = sum0_ref[...] + sum1_ref[...] + sum2_ref[...] + sum3_ref[...]
@@ -333,10 +343,8 @@
         hidden = hid_ref[...]
         own = own_ref[...]
     act = silu((hidden - center) * factor)
-    w_out = jnp.concatenate([w_out_ref[...], w_out_ref[...] * 0.0], axis=0)
-    from_hidden = product(w_out, hidden, ((1,), (1,)))
     from_act = product(fold_ref[...], act, ((1,), (1,)))
-    local = from_hidden[0:4] + from_act[0:4]
+    local = base_ref[0:4] + from_act[0:4]
     ratio = coef_ref[0:1, 0:1]
     noise = coef_ref[1:2, 0:1]
     out_ref[0:4] = ratio * own + noise * local
@@ -453,9 +461,13 @@
             12, 10, "conv_two",
         )
         width = positions if last else 2 * positions
+        (base,) = call(
+            functools.partial(base_kernel, last), [VMEM] * 2, [(8, width)], (hidden, out_rows),
+            "base", pl.CostEstimate(flops=20_000_000, bytes_accessed=1_000_000, transcendentals=0),
+        )
         (parts,) = call(
             functools.partial(project_kernel, members, last), [VMEM] * 9, [(16, width)],
-            (hidden, *around_strip(stats), pieces[0], out_rows, folded, coef), "project",
+            (hidden, *around_strip(stats), pieces[0], base, folded, coef), "project",
         )
         if last:
             (out,) = call(

time: 90.7 us -> 90.6 us (level)
    pallas_call x5 -> x7, Pallas kernels: 2.17 us -> 2.64 us  [call(): pl.pallas_call(kernel, in_specs=in_specs, out_specs=[VMEM] * len(shapes),...]
  transfers between devices with their start and end apart: 19 -> 19, of which waited for: 16 -> 16; matrix products, arithmetic and copies ran while one was open for 0% -> 0% of each run, Pallas kernels for 2% -> 3%
where the time goes in v6:
time: 90.6 us; the launch traced here: 90.2 us
  starting transfers between devices  25.6 us (28%)
  waiting for transfers between devices  24.9 us (27%)
  Pallas kernels  24 us (26%)
  blocking collectives  13.9 us (15%)
    ppermute x15, starting transfers between devices, around_strip(): lax.ppermute(value, 'band', [(i, i ^ 2 * flip) for i in range(bands)])  17.9 us
    pallas_call x4, Pallas kernels, conv_call(): pl.pallas_call(kernel, in_specs=[VMEM] * len(operands), out_specs=[VMEM,...  17.3 us
    all_to_all x1, blocking collectives, on_device(): frame = lax.all_to_all(spread, 'band', 0, 0, tiled=True)  13.9 us
    ppermute x15, waiting for transfers between devices, around_strip(): lax.ppermute(value, 'band', [(i, i ^ 2 * flip) for i in range(bands)])  13.5 us
    ppermute x1, waiting for transfers between devices, on_device(): lax.ppermute(parts[8:12], 'level', [(i, i + 2) for i in range(levels - 2)])  6.36 us
    ppermute x1, waiting for transfers between devices, swap_slots(): from_chip = lax.ppermute(to_chip, 'level', across)  5.03 us
    pallas_call x2, Pallas kernels, setup(): pl.pallas_call(kernel, in_specs=specs, out_specs=[VMEM] * (len(shapes) +...  4.04 us
    ppermute x1, starting transfers between devices, on_device(): lax.ppermute(parts[8:12], 'level', [(i, i + 2) for i in range(levels - 2)])  3.82 us
  transfers between devices with their start and end apart: 19, of which 16 were waited for; matrix products, arithmetic and copies ran while one was open for 0% of the time, Pallas kernels for 3%

profile of v6, /device:TPU:8, one launch (start us, length us, event | category | flops | bytes accessed | tf_op | source)
XLA Modules:
  0.0 90.2 jit_solution(12365428498880203572)
XLA Ops:
  0.8 0.7 maximum_bitcast_fusion.frames_ref
  1.6 13.9 %all_to_all.5.frame_ref = f32[8,8,320]{2,1,0:T(8,128)S(1)} all-to-all(f32[8,8,320]{2,1,0:T(8,128)S(1)} %get-tuple-element.25), channel_id=1, replica_groups=mesh['level'=32,'band'=8] {'band'}, dimensions={0} | all-to-all | bytes 163840 | tf_op jit(solution)/shard_map/all_to_all | solution.py:441
  15.5 2.0 %setup_first.1 = (f32[4,640]{1,0:T(4,128)S(1)}, f32[4,640]{1,0:T(4,128)S(1)}, f32[4,640]{1,0:T(4,128)S(1)}, f32[4,640]{1,0:T(4,128)S(1)}, f32[4,640]{1,0:T(4,128...) custom-call(f32[8,8,320]{2,1,0:T(8,128)S(1)} %all_to_all.5.frame_ref, ...), custom_call_target="tpu_custom_call" | custom-call | bytes 10000000 | tf_op jit(solution)/shard_map/setup_first/pallas_call | solution.py:192
  17.6 4.6 %conv_one.2 = (f32[768,320]{1,0:T(8,128)S(1)}, f32[2,320]{1,0:T(2,128)S(1)}) custom-call(f32[4,640]{1,0:T(4,128)S(1)} %get-tuple-element.27.own_ref, f32[4,640]{1,0:T(4,128)S(1)} %get-tuple-element.28.flip1_ref, f32[4,640]{1,0:T(4,128)S(1)} %get-tuple-element.29.flip3_ref, f32[4,640]{1,0:T(4,128)S(1)} %get-tuple-element.30.flip2_ref, ...), custom_call_target="tpu_custom_call" | custom-call | flops 2831155200 | bytes 4000000 | tf_op jit(solution)/shard_map/conv_one/pallas_call | solution.py:375
  22.2 1.5 %collective-permute-start.2 = (f32[2,320]{1,0:T(2,128)S(1)}, f32[2,320]{1,0:T(2,128)S(1)}, u32[]{:S(2)}, u32[]{:S(2)}) collective-permute-start(f32[2,320]{1,0:T(2,128)S(1)} %get-tuple-element.34.after_ref.sum0_ref), channel_id=1, source_target_pairs={{0,4},{1,5},{2,6},{3,7},{4,0},{5,1},{6,2},{7,3},{8,12},{9,13},{10,... | collective-permute-start | bytes 7688 | tf_op jit(solution)/shard_map/ppermute | solution.py:413
  23.7 1.8 %collective-permute-start.1 = (f32[2,320]{1,0:T(2,128)S(1)}, f32[2,320]{1,0:T(2,128)S(1)}, u32[]{:S(2)}, u32[]{:S(2)}) collective-permute-start(f32[2,320]{1,0:T(2,128)S(1)} %get-tuple-element.34.after_ref.sum0_ref), channel_id=1, source_target_pairs={{0,6},{1,7},{2,4},{3,5},{4,2},{5,3},{6,0},{7,1},{8,14},{9,15},{10,... | collective-permute-start | bytes 7688 | tf_op jit(solution)/shard_map/ppermute | solution.py:413
  25.8 2.0 %setup_second.1 = (f32[16,320]{1,0:T(8,128)S(1)}, bf16[4,1024,960]{2,1,0:T(8,128)(2,1)S(1)}) custom-call(f32[2,320]{1,0:T(2,128)S(1)} %get-tuple-element.34.after_ref.sum0_ref, f32[4,320]{1,0:T(4,128)S(1)} %bitcast.7, f32[3,320,320]{2,1,0:T(8,128)S(1)} %copy-done.1, f32[3,3,320,320]{3,2,1,0:T(8,128)S(1)} %bitcast.6), custom_call_target="tpu_custom_call" | custom-call | bytes 10000000 | tf_op jit(solution)/shard_map/setup_second/pallas_call | solution.py:192
  29.1 4.1 %conv_two.2 = (f32[640,320]{1,0:T(8,128)S(1)}, f32[2,320]{1,0:T(2,128)S(1)}) custom-call(f32[768,320]{1,0:T(8,128)S(1)} %get-tuple-element.33.mid_ref, f32[2,320]{1,0:T(2,128)S(1)} %get-tuple-element.34.after_ref.sum0_ref, f32[2,320]{1,0:T(2,128)S(1)} %collective-permute-done.sum1_ref, f32[2,320]{1,0:T(2,128)S(1)} %collective-permute-done.1.sum2_ref, ...), custom_call_target="tpu_custom_call" | custom-call | flops 2359296000 | bytes 4000000 | tf_op jit(solution)/shard_map/conv_two/pallas_call | solution.py:375
  33.2 1.5 %collective-permute-start.5 = (f32[2,320]{1,0:T(2,128)S(1)}, f32[2,320]{1,0:T(2,128)S(1)}, u32[]{:S(2)}, u32[]{:S(2)}) collective-permute-start(f32[2,320]{1,0:T(2,128)S(1)} %get-tuple-element.37.sum0_ref), channel_id=1, source_target_pairs={{0,4},{1,5},{2,6},{3,7},{4,0},{5,1},{6,2},{7,3},{8,12},{9,13},{10,... | collective-permute-start | bytes 7688 | tf_op jit(solution)/shard_map/ppermute | solution.py:413
  34.7 1.8 %collective-permute-start.4 = (f32[2,320]{1,0:T(2,128)S(1)}, f32[2,320]{1,0:T(2,128)S(1)}, u32[]{:S(2)}, u32[]{:S(2)}) collective-permute-start(f32[2,320]{1,0:T(2,128)S(1)} %get-tuple-element.37.sum0_ref), channel_id=1, source_target_pairs={{0,6},{1,7},{2,4},{3,5},{4,2},{5,3},{6,0},{7,1},{8,14},{9,15},{10,... | collective-permute-start | bytes 7688 | tf_op jit(solution)/shard_map/ppermute | solution.py:413
  37.2 1.2 %collective-permute-done.5.sum3_ref = f32[2,320]{1,0:T(2,128)S(1)} collective-permute-done((f32[2,320]{1,0:T(2,128)S(1)}, f32[2,320]{1,0:T(2,128)S(1)}, u32[]{:S(2)}, u32[]{:S(2)}) %collective-permute-start.5) | collective-permute-done | bytes 2592 | tf_op jit(solution)/shard_map/ppermute | solution.py:413
  38.4 1.1 %collective-permute-done.4.sum2_ref = f32[2,320]{1,0:T(2,128)S(1)} collective-permute-done((f32[2,320]{1,0:T(2,128)S(1)}, f32[2,320]{1,0:T(2,128)S(1)}, u32[]{:S(2)}, u32[]{:S(2)}) %collective-permute-start.4) | collective-permute-done | bytes 2592 | tf_op jit(solution)/shard_map/ppermute | solution.py:413
  40.1 0.8 project.2.parts_ref
  40.8 1.9 %collective-permute-start.6 = (f32[8,640]{1,0:T(8,128)S(1)}, f32[8,640]{1,0:T(8,128)S(1)}, u32[]{:S(2)}, u32[]{:S(2)}) collective-permute-start(f32[8,640]{1,0:T(8,128)S(1)} %slice.16), channel_id=1, source_target_pairs={{0,8},{8,16},{16,24},{24,32},{32,40},{40,48},{48,56},{56,64},{64,7... | collective-permute-start | bytes 61448 | tf_op jit(solution)/shard_map/ppermute | solution.py:478
  42.8 3.8 %collective-permute-start.7 = (f32[4,640]{1,0:T(4,128)S(1)}, f32[4,640]{1,0:T(4,128)S(1)}, u32[]{:S(2)}, u32[]{:S(2)}) collective-permute-start(f32[4,640]{1,0:T(4,128)S(1)} %slice.17), channel_id=1, source_target_pairs={{0,16},{8,24},{16,32},{24,40},{32,48},{40,56},{48,64},{56,72},{64,... | collective-permute-start | bytes 30728 | tf_op jit(solution)/shard_map/ppermute | solution.py:479
  46.6 6.4 %collective-permute-done.7.two_ref = f32[4,640]{1,0:T(4,128)S(1)} collective-permute-done((f32[4,640]{1,0:T(4,128)S(1)}, f32[4,640]{1,0:T(4,128)S(1)}, u32[]{:S(2)}, u32[]{:S(2)}) %collective-permute-start.7) | collective-permute-done | bytes 10272 | tf_op jit(solution)/shard_map/ppermute | solution.py:479
  53.0 1.3 %collective-permute-start.10 = (f32[4,640]{1,0:T(4,128)S(1)}, f32[4,640]{1,0:T(4,128)S(1)}, u32[]{:S(2)}, u32[]{:S(2)}) collective-permute-start(f32[4,640]{1,0:T(4,128)S(1)} %merge.1.own_ref), channel_id=1, source_target_pairs={{0,4},{1,5},{2,6},{3,7},{4,0},{5,1},{6,2},{7,3},{8,12},{9,13},{10,... | collective-permute-start | bytes 30728 | tf_op jit(solution)/shard_map/ppermute | solution.py:413
  54.3 1.8 %collective-permute-start.9 = (f32[4,640]{1,0:T(4,128)S(1)}, f32[4,640]{1,0:T(4,128)S(1)}, u32[]{:S(2)}, u32[]{:S(2)}) collective-permute-start(f32[4,640]{1,0:T(4,128)S(1)} %merge.1.own_ref), channel_id=1, source_target_pairs={{0,6},{1,7},{2,4},{3,5},{4,2},{5,3},{6,0},{7,1},{8,14},{9,15},{10,... | collective-permute-start | bytes 30728 | tf_op jit(solution)/shard_map/ppermute | solution.py:413
  56.6 1.7 %collective-permute-done.10.flip2_ref = f32[4,640]{1,0:T(4,128)S(1)} collective-permute-done((f32[4,640]{1,0:T(4,128)S(1)}, f32[4,640]{1,0:T(4,128)S(1)}, u32[]{:S(2)}, u32[]{:S(2)}) %collective-permute-start.10) | collective-permute-done | bytes 10272 | tf_op jit(solution)/shard_map/ppermute | solution.py:413
  58.3 0.9 collective-permute-done.9.flip3_ref
  59.8 4.6 %conv_one.3 = (f32[768,320]{1,0:T(8,128)S(1)}, f32[2,320]{1,0:T(2,128)S(1)}) custom-call(f32[4,640]{1,0:T(4,128)S(1)} %merge.1.own_ref, f32[4,640]{1,0:T(4,128)S(1)} %collective-permute-done.8.flip1_ref, f32[4,640]{1,0:T(4,128)S(1)} %collective-permute-done.9.flip3_ref, f32[4,640]{1,0:T(4,128)S(1)} %collective-permute-done.10.flip2_ref, ...), custom_call_target="tpu_custom_call" | custom-call | flops 2831155200 | bytes 4000000 | tf_op jit(solution)/shard_map/conv_one/pallas_call | solution.py:375
  64.4 1.5 %collective-permute-start.13 = (f32[2,320]{1,0:T(2,128)S(1)}, f32[2,320]{1,0:T(2,128)S(1)}, u32[]{:S(2)}, u32[]{:S(2)}) collective-permute-start(f32[2,320]{1,0:T(2,128)S(1)} %get-tuple-element.42.sum0_ref), channel_id=1, source_target_pairs={{0,4},{1,5},{2,6},{3,7},{4,0},{5,1},{6,2},{7,3},{8,12},{9,13},{10,... | collective-permute-start | bytes 7688 | tf_op jit(solution)/shard_map/ppermute | solution.py:413
  65.8 1.8 %collective-permute-start.12 = (f32[2,320]{1,0:T(2,128)S(1)}, f32[2,320]{1,0:T(2,128)S(1)}, u32[]{:S(2)}, u32[]{:S(2)}) collective-permute-start(f32[2,320]{1,0:T(2,128)S(1)} %get-tuple-element.42.sum0_ref), channel_id=1, source_target_pairs={{0,6},{1,7},{2,4},{3,5},{4,2},{5,3},{6,0},{7,1},{8,14},{9,15},{10,... | collective-permute-start | bytes 7688 | tf_op jit(solution)/shard_map/ppermute | solution.py:413
  67.9 1.6 %collective-permute-done.13.sum3_ref = f32[2,320]{1,0:T(2,128)S(1)} collective-permute-done((f32[2,320]{1,0:T(2,128)S(1)}, f32[2,320]{1,0:T(2,128)S(1)}, u32[]{:S(2)}, u32[]{:S(2)}) %collective-permute-start.13) | collective-permute-done | bytes 2592 | tf_op jit(solution)/shard_map/ppermute | solution.py:413
  69.5 1.1 %collective-permute-done.12.sum2_ref = f32[2,320]{1,0:T(2,128)S(1)} collective-permute-done((f32[2,320]{1,0:T(2,128)S(1)}, f32[2,320]{1,0:T(2,128)S(1)}, u32[]{:S(2)}, u32[]{:S(2)}) %collective-permute-start.12) | collective-permute-done | bytes 2592 | tf_op jit(solution)/shard_map/ppermute | solution.py:413
  71.2 4.1 %conv_two.3 = (f32[640,320]{1,0:T(8,128)S(1)}, f32[2,320]{1,0:T(2,128)S(1)}) custom-call(f32[768,320]{1,0:T(8,128)S(1)} %get-tuple-element.41.mid_ref, f32[2,320]{1,0:T(2,128)S(1)} %get-tuple-element.42.sum0_ref, f32[2,320]{1,0:T(2,128)S(1)} %collective-permute-done.11.sum1_ref, f32[2,320]{1,0:T(2,128)S(1)} %collective-permute-done.12.sum2_ref, ...), custom_call_target="tpu_custom_call" | custom-call | flops 2359296000 | bytes 4000000 | tf_op jit(solution)/shard_map/conv_two/pallas_call | solution.py:375
  75.3 1.3 %collective-permute-start.16 = (f32[2,320]{1,0:T(2,128)S(1)}, f32[2,320]{1,0:T(2,128)S(1)}, u32[]{:S(2)}, u32[]{:S(2)}) collective-permute-start(f32[2,320]{1,0:T(2,128)S(1)} %get-tuple-element.44.sum0_ref), channel_id=1, source_target_pairs={{0,4},{1,5},{2,6},{3,7},{4,0},{5,1},{6,2},{7,3},{8,12},{9,13},{10,... | collective-permute-start | bytes 7688 | tf_op jit(solution)/shard_map/ppermute | solution.py:413
  76.6 1.8 %collective-permute-start.15 = (f32[2,320]{1,0:T(2,128)S(1)}, f32[2,320]{1,0:T(2,128)S(1)}, u32[]{:S(2)}, u32[]{:S(2)}) collective-permute-start(f32[2,320]{1,0:T(2,128)S(1)} %get-tuple-element.44.sum0_ref), channel_id=1, source_target_pairs={{0,6},{1,7},{2,4},{3,5},{4,2},{5,3},{6,0},{7,1},{8,14},{9,15},{10,... | collective-permute-start | bytes 7688 | tf_op jit(solution)/shard_map/ppermute | solution.py:413
  79.1 1.4 %collective-permute-done.16.sum3_ref = f32[2,320]{1,0:T(2,128)S(1)} collective-permute-done((f32[2,320]{1,0:T(2,128)S(1)}, f32[2,320]{1,0:T(2,128)S(1)}, u32[]{:S(2)}, u32[]{:S(2)}) %collective-permute-start.16) | collective-permute-done | bytes 2592 | tf_op jit(solution)/shard_map/ppermute | solution.py:413
  80.5 0.9 collective-permute-done.15.sum2_ref
  82.5 1.9 %collective-permute-start.18 = (f32[4,320]{1,0:T(4,128)S(1)}, f32[4,320]{1,0:T(4,128)S(1)}, u32[]{:S(2)}, u32[]{:S(2)}) collective-permute-start(f32[4,320]{1,0:T(4,128)S(1)} %get-tuple-element.45), channel_id=1, source_target_pairs={{8,16},{24,32},{40,48},{56,64},{72,80},{88,96},{104,112},{120,128}... | collective-permute-start | bytes 15368 | tf_op jit(solution)/shard_map/ppermute | solution.py:423
  84.5 5.0 %collective-permute-done.18.chip_ref = f32[4,320]{1,0:T(4,128)S(1)} collective-permute-done((f32[4,320]{1,0:T(4,128)S(1)}, f32[4,320]{1,0:T(4,128)S(1)}, u32[]{:S(2)}, u32[]{:S(2)}) %collective-permute-start.18) | collective-permute-done | bytes 5152 | tf_op jit(solution)/shard_map/ppermute | solution.py:423
  (43 shorter events, 7.7 us)
Async XLA Ops:
  1.5 14.0 %copy-start = (f32[3,3,320,320]{3,2,1,0:T(8,128)S(1)}, f32[3,3,320,320]{3,2,1,0:T(8,128)}, u32[]{:S(2)}) copy-start(f32[3,3,320,320]{3,2,1,0:T(8,128)} %raw_ref.2) | copy-start | bytes 11059204
  1.5 14.0 %copy-start.2 = (f32[320,320]{1,0:T(8,128)S(1)}, f32[320,320]{1,0:T(8,128)}, u32[]{:S(2)}) copy-start(f32[320,320]{1,0:T(8,128)} %time_ref.1) | copy-start | bytes 1228804
  1.5 14.0 %copy-start.5 = (f32[8,128]{1,0:T(8,128)S(1)}, f32[8,128]{1,0:T(8,128)}, u32[]{:S(2)}) copy-start(f32[8,128]{1,0:T(8,128)} %constant.8.clone.plan_ref) | copy-start | bytes 12292
  1.6 15.9 %copy-start.4 = (f32[4,320]{1,0:T(4,128)S(1)}, f32[4,320]{1,0:T(4,128)}, u32[]{:S(2)}) copy-start(f32[4,320]{1,0:T(4,128)} %w_in_ref.7) | copy-start | bytes 15364
  15.5 10.3 %slice-start = ((s8[4423680]{0:T(1024)(128)(4,1)}), s8[4194304]{0:T(1024)(128)(4,1)S(1)}, s32[]{:S(2)}) async-start(s8[4423680]{0:T(1024)(128)(4,1)} %bitcast.5), calls=%async_computation.1 | async-start | bytes 8388608
  17.6 8.2 %slice-start.1 = ((s8[4423680]{0:T(1024)(128)(4,1)}), s8[229376]{0:T(1024)(128)(4,1)S(1)}, s32[]{:S(2)}) async-start(s8[4423680]{0:T(1024)(128)(4,1)} %bitcast.5), calls=%async_computation.2 | async-start | bytes 458752
  17.6 8.2 %copy-start.1 = (f32[3,320,320]{2,1,0:T(8,128)S(1)}, f32[3,320,320]{2,1,0:T(8,128)}, u32[]{:S(2)}) copy-start(f32[3,320,320]{2,1,0:T(8,128)} %temporal_ref.1) | copy-start | bytes 3686404
  17.6 8.2 %copy-start.3 = (f32[320,4]{0,1:T(4,128)S(1)}, f32[320,4]{0,1:T(4,128)}, u32[]{:S(2)}) copy-start(f32[320,4]{0,1:T(4,128)} %param.18) | copy-start | bytes 15364
  22.2 5.6 %collective-permute-start.2 = (f32[2,320]{1,0:T(2,128)S(1)}, f32[2,320]{1,0:T(2,128)S(1)}, u32[]{:S(2)}, u32[]{:S(2)}) collective-permute-start(f32[2,320]{1,0:T(2,128)S(1)} %get-tuple-element.34.after_ref.sum0_ref), channel_id=1, source_target_pairs={{0,4},{1,5},{2,6},{3,7},{4,0},{5,1},{6,2},{7,3},{8,12},{9,13},{10,... | collective-permute-start | bytes 7688 | tf_op jit(solution)/shard_map/ppermute | solution.py:413
  23.7 4.8 %collective-permute-start.1 = (f32[2,320]{1,0:T(2,128)S(1)}, f32[2,320]{1,0:T(2,128)S(1)}, u32[]{:S(2)}, u32[]{:S(2)}) collective-permute-start(f32[2,320]{1,0:T(2,128)S(1)} %get-tuple-element.34.after_ref.sum0_ref), channel_id=1, source_target_pairs={{0,6},{1,7},{2,4},{3,5},{4,2},{5,3},{6,0},{7,1},{8,14},{9,15},{10,... | collective-permute-start | bytes 7688 | tf_op jit(solution)/shard_map/ppermute | solution.py:413
  25.5 3.6 %collective-permute-start = (f32[2,320]{1,0:T(2,128)S(1)}, f32[2,320]{1,0:T(2,128)S(1)}, u32[]{:S(2)}, u32[]{:S(2)}) collective-permute-start(f32[2,320]{1,0:T(2,128)S(1)} %get-tuple-element.34.after_ref.sum0_ref), channel_id=1, source_target_pairs={{0,2},{1,3},{2,0},{3,1},{4,6},{5,7},{6,4},{7,5},{8,10},{9,11},{10,... | collective-permute-start | bytes 7688 | tf_op jit(solution)/shard_map/ppermute | solution.py:413
  33.2 5.2 %collective-permute-start.5 = (f32[2,320]{1,0:T(2,128)S(1)}, f32[2,320]{1,0:T(2,128)S(1)}, u32[]{:S(2)}, u32[]{:S(2)}) collective-permute-start(f32[2,320]{1,0:T(2,128)S(1)} %get-tuple-element.37.sum0_ref), channel_id=1, source_target_pairs={{0,4},{1,5},{2,6},{3,7},{4,0},{5,1},{6,2},{7,3},{8,12},{9,13},{10,... | collective-permute-start | bytes 7688 | tf_op jit(solution)/shard_map/ppermute | solution.py:413
  34.7 4.8 %collective-permute-start.4 = (f32[2,320]{1,0:T(2,128)S(1)}, f32[2,320]{1,0:T(2,128)S(1)}, u32[]{:S(2)}, u32[]{:S(2)}) collective-permute-start(f32[2,320]{1,0:T(2,128)S(1)} %get-tuple-element.37.sum0_ref), channel_id=1, source_target_pairs={{0,6},{1,7},{2,4},{3,5},{4,2},{5,3},{6,0},{7,1},{8,14},{9,15},{10,... | collective-permute-start | bytes 7688 | tf_op jit(solution)/shard_map/ppermute | solution.py:413
  36.5 3.6 %collective-permute-start.3 = (f32[2,320]{1,0:T(2,128)S(1)}, f32[2,320]{1,0:T(2,128)S(1)}, u32[]{:S(2)}, u32[]{:S(2)}) collective-permute-start(f32[2,320]{1,0:T(2,128)S(1)} %get-tuple-element.37.sum0_ref), channel_id=1, source_target_pairs={{0,2},{1,3},{2,0},{3,1},{4,6},{5,7},{6,4},{7,5},{8,10},{9,11},{10,... | collective-permute-start | bytes 7688 | tf_op jit(solution)/shard_map/ppermute | solution.py:413
  40.8 12.1 %collective-permute-start.6 = (f32[8,640]{1,0:T(8,128)S(1)}, f32[8,640]{1,0:T(8,128)S(1)}, u32[]{:S(2)}, u32[]{:S(2)}) collective-permute-start(f32[8,640]{1,0:T(8,128)S(1)} %slice.16), channel_id=1, source_target_pairs={{0,8},{8,16},{16,24},{24,32},{32,40},{40,48},{48,56},{56,64},{64,7... | collective-permute-start | bytes 61448 | tf_op jit(solution)/shard_map/ppermute | solution.py:478
  42.8 10.2 %collective-permute-start.7 = (f32[4,640]{1,0:T(4,128)S(1)}, f32[4,640]{1,0:T(4,128)S(1)}, u32[]{:S(2)}, u32[]{:S(2)}) collective-permute-start(f32[4,640]{1,0:T(4,128)S(1)} %slice.17), channel_id=1, source_target_pairs={{0,16},{8,24},{16,32},{24,40},{32,48},{40,56},{48,64},{56,72},{64,... | collective-permute-start | bytes 30728 | tf_op jit(solution)/shard_map/ppermute | solution.py:479
  53.0 5.3 %collective-permute-start.10 = (f32[4,640]{1,0:T(4,128)S(1)}, f32[4,640]{1,0:T(4,128)S(1)}, u32[]{:S(2)}, u32[]{:S(2)}) collective-permute-start(f32[4,640]{1,0:T(4,128)S(1)} %merge.1.own_ref), channel_id=1, source_target_pairs={{0,4},{1,5},{2,6},{3,7},{4,0},{5,1},{6,2},{7,3},{8,12},{9,13},{10,... | collective-permute-start | bytes 30728 | tf_op jit(solution)/shard_map/ppermute | solution.py:413
  54.3 4.9 %collective-permute-start.9 = (f32[4,640]{1,0:T(4,128)S(1)}, f32[4,640]{1,0:T(4,128)S(1)}, u32[]{:S(2)}, u32[]{:S(2)}) collective-permute-start(f32[4,640]{1,0:T(4,128)S(1)} %merge.1.own_ref), channel_id=1, source_target_pairs={{0,6},{1,7},{2,4},{3,5},{4,2},{5,3},{6,0},{7,1},{8,14},{9,15},{10,... | collective-permute-start | bytes 30728 | tf_op jit(solution)/shard_map/ppermute | solution.py:413
  56.1 3.7 %collective-permute-start.8 = (f32[4,640]{1,0:T(4,128)S(1)}, f32[4,640]{1,0:T(4,128)S(1)}, u32[]{:S(2)}, u32[]{:S(2)}) collective-permute-start(f32[4,640]{1,0:T(4,128)S(1)} %merge.1.own_ref), channel_id=1, source_target_pairs={{0,2},{1,3},{2,0},{3,1},{4,6},{5,7},{6,4},{7,5},{8,10},{9,11},{10,... | collective-permute-start | bytes 30728 | tf_op jit(solution)/shard_map/ppermute | solution.py:413
  64.4 5.2 %collective-permute-start.13 = (f32[2,320]{1,0:T(2,128)S(1)}, f32[2,320]{1,0:T(2,128)S(1)}, u32[]{:S(2)}, u32[]{:S(2)}) collective-permute-start(f32[2,320]{1,0:T(2,128)S(1)} %get-tuple-element.42.sum0_ref), channel_id=1, source_target_pairs={{0,4},{1,5},{2,6},{3,7},{4,0},{5,1},{6,2},{7,3},{8,12},{9,13},{10,... | collective-permute-start | bytes 7688 | tf_op jit(solution)/shard_map/ppermute | solution.py:413
  65.8 4.8 %collective-permute-start.12 = (f32[2,320]{1,0:T(2,128)S(1)}, f32[2,320]{1,0:T(2,128)S(1)}, u32[]{:S(2)}, u32[]{:S(2)}) collective-permute-start(f32[2,320]{1,0:T(2,128)S(1)} %get-tuple-element.42.sum0_ref), channel_id=1, source_target_pairs={{0,6},{1,7},{2,4},{3,5},{4,2},{5,3},{6,0},{7,1},{8,14},{9,15},{10,... | collective-permute-start | bytes 7688 | tf_op jit(solution)/shard_map/ppermute | solution.py:413
  67.6 3.6 %collective-permute-start.11 = (f32[2,320]{1,0:T(2,128)S(1)}, f32[2,320]{1,0:T(2,128)S(1)}, u32[]{:S(2)}, u32[]{:S(2)}) collective-permute-start(f32[2,320]{1,0:T(2,128)S(1)} %get-tuple-element.42.sum0_ref), channel_id=1, source_target_pairs={{0,2},{1,3},{2,0},{3,1},{4,6},{5,7},{6,4},{7,5},{8,10},{9,11},{10,... | collective-permute-start | bytes 7688 | tf_op jit(solution)/shard_map/ppermute | solution.py:413
  75.3 5.2 %collective-permute-start.16 = (f32[2,320]{1,0:T(2,128)S(1)}, f32[2,320]{1,0:T(2,128)S(1)}, u32[]{:S(2)}, u32[]{:S(2)}) collective-permute-start(f32[2,320]{1,0:T(2,128)S(1)} %get-tuple-element.44.sum0_ref), channel_id=1, source_target_pairs={{0,4},{1,5},{2,6},{3,7},{4,0},{5,1},{6,2},{7,3},{8,12},{9,13},{10,... | collective-permute-start | bytes 7688 | tf_op jit(solution)/shard_map/ppermute | solution.py:413
  76.6 4.8 %collective-permute-start.15 = (f32[2,320]{1,0:T(2,128)S(1)}, f32[2,320]{1,0:T(2,128)S(1)}, u32[]{:S(2)}, u32[]{:S(2)}) collective-permute-start(f32[2,320]{1,0:T(2,128)S(1)} %get-tuple-element.44.sum0_ref), channel_id=1, source_target_pairs={{0,6},{1,7},{2,4},{3,5},{4,2},{5,3},{6,0},{7,1},{8,14},{9,15},{10,... | collective-permute-start | bytes 7688 | tf_op jit(solution)/shard_map/ppermute | solution.py:413
  78.4 3.6 %collective-permute-start.14 = (f32[2,320]{1,0:T(2,128)S(1)}, f32[2,320]{1,0:T(2,128)S(1)}, u32[]{:S(2)}, u32[]{:S(2)}) collective-permute-start(f32[2,320]{1,0:T(2,128)S(1)} %get-tuple-element.44.sum0_ref), channel_id=1, source_target_pairs={{0,2},{1,3},{2,0},{3,1},{4,6},{5,7},{6,4},{7,5},{8,10},{9,11},{10,... | collective-permute-start | bytes 7688 | tf_op jit(solution)/shard_map/ppermute | solution.py:413
  82.5 7.1 %collective-permute-start.18 = (f32[4,320]{1,0:T(4,128)S(1)}, f32[4,320]{1,0:T(4,128)S(1)}, u32[]{:S(2)}, u32[]{:S(2)}) collective-permute-start(f32[4,320]{1,0:T(4,128)S(1)} %get-tuple-element.45), channel_id=1, source_target_pairs={{8,16},{24,32},{40,48},{56,64},{72,80},{88,96},{104,112},{120,128}... | collective-permute-start | bytes 15368 | tf_op jit(solution)/shard_map/ppermute | solution.py:423
  84.4 5.1 %collective-permute-start.17 = (f32[4,320]{1,0:T(4,128)S(1)}, f32[4,320]{1,0:T(4,128)S(1)}, u32[]{:S(2)}, u32[]{:S(2)}) collective-permute-start(f32[4,320]{1,0:T(4,128)S(1)} %get-tuple-element.46), channel_id=1, source_target_pairs={{0,8},{8,0},{16,24},{24,16},{32,40},{40,32},{48,56},{56,48},{64,72... | collective-permute-start | bytes 15368 | tf_op jit(solution)/shard_map/ppermute | solution.py:422
